TPU v7x, 512 devices: a whole 4x8x8 slice. The times are simulated.
512 devices in a mesh: gx: 32 (over y, x_lo, core), gy: 16 (over z, x_hi).
Axes of the slice: x: 4 (x_hi: 2, x_lo: 2; x = x_hi * 2 + x_lo), y: 8, z: 8, core: 2. Of those that a mesh axis runs over, the one named last changes fastest.
Arguments:
- mass_per_volume: float32 [256, 128, 128], P('gx', 'gy'), may hold values from 0.4 to 2.5
- velocity: float32 [3, 256, 128, 128], P(None, 'gx', 'gy'), may hold values from -3 to 3
- thermal_stress: float32 [256, 128, 128], P('gx', 'gy'), may hold values from 0.06 to 1.5
- magnetic: float32 [3, 256, 128, 128], P(None, 'gx', 'gy'), may hold values from -4.8 to 4.8, as said below
Outputs:
- density_out: float32 [256, 128, 128], P('gx', 'gy')
- velocity_out: float32 [3, 256, 128, 128], P(None, 'gx', 'gy')
- pressure_out: float32 [256, 128, 128], P('gx', 'gy')
- magnetic_out: float32 [3, 256, 128, 128], P(None, 'gx', 'gy')
Inputs may be any that keep to these rules, and one draw needn't show every extreme that they name: magnetic has zero discrete divergence in every cell: the sum over c of b_c at i+1 minus b_c at i along c vanishes up to rounding.
All inputs are finite; a program needn't handle non-finite values.
Results may differ from a plain program's by a relative error of at most 0.0003.
Values sent between devices are 32-bit elements; how exact they have to be, the bound alone decides.
No kernel may reach another device: no remote copies, remote signals or barrier semaphores. Data moves between devices by JAX's collectives and lax.ppermute only.
A program may use at most 128 MiB of HBM per device.

v0:
```python
import jax
import jax.numpy as jnp
from jax import lax
from jax.sharding import PartitionSpec as P

SECTIONS = 4
SUPER_SECTIONS = 8


GAMMA_RATIO = 5.0 / 3.0
TIME_STEP = 0.04
SUPER_TIME = 0.08
DENSITY_FLOOR = 0.5
PRESSURE_FLOOR = 0.1
FIELD_FLOOR = 0.05


def extended_2(block, sides, width):
    for axis, dim in sides:
        count = lax.axis_size(axis)
        forward = [(i, i + 1) for i in range(count - 1)]
        forward.append((count - 1, 0))
        backward = [(target, source) for source, target in forward]
        low = lax.ppermute(
            lax.slice_in_dim(block, block.shape[dim] - width, None, axis=dim), axis, forward
        )
        high = lax.ppermute(lax.slice_in_dim(block, 0, width, axis=dim), axis, backward)
        block = jnp.concatenate([low, block, high], axis=dim)
    return block


def adjacent_zone(a, dimension, k):
    return jnp.roll(a, -k, dimension)


def minmod(lower, upper):
    return 0.5 * (jnp.sign(lower) + jnp.sign(upper)) * jnp.minimum(jnp.abs(lower), jnp.abs(upper))


def wave_fluxes(mass_per_volume, velocity, thermal_stress, magnetic, adjacent_quantities):
    magnetic_sq = magnetic[0] * magnetic[0] + magnetic[1] * magnetic[1] + magnetic[2] * magnetic[2]
    kinetic = velocity[0] * velocity[0] + velocity[1] * velocity[1] + velocity[2] * velocity[2]
    whole_work_content = (
        thermal_stress / (GAMMA_RATIO - 1.0) + 0.5 * mass_per_volume * kinetic + 0.5 * magnetic_sq
    )
    pressure_total = thermal_stress + 0.5 * magnetic_sq
    normal_speed = velocity[adjacent_quantities]
    normal_field = magnetic[adjacent_quantities]
    projection = velocity[0] * magnetic[0] + velocity[1] * magnetic[1] + velocity[2] * magnetic[2]
    others = [
        zone_quantities for zone_quantities in range(3) if zone_quantities != adjacent_quantities
    ]
    conserved = (
        [mass_per_volume]
        + [mass_per_volume * velocity[zone_quantities] for zone_quantities in range(3)]
        + [whole_work_content]
        + [magnetic[zone_quantities] for zone_quantities in others]
    )
    momentum_fluxes = []
    for zone_quantities in range(3):
        momentum_term = (
            mass_per_volume * normal_speed * velocity[zone_quantities]
            - normal_field * magnetic[zone_quantities]
        )
        if zone_quantities == adjacent_quantities:
            momentum_term = momentum_term + pressure_total
        momentum_fluxes.append(momentum_term)
    fluxes = [mass_per_volume * normal_speed] + momentum_fluxes
    fluxes = fluxes + [
        (whole_work_content + pressure_total) * normal_speed - normal_field * projection
    ]
    fluxes = fluxes + [
        normal_speed * magnetic[zone_quantities] - velocity[zone_quantities] * normal_field
        for zone_quantities in others
    ]
    signal = jnp.abs(normal_speed) + jnp.sqrt(
        (GAMMA_RATIO * thermal_stress + magnetic_sq) / mass_per_volume
    )
    return (conserved, fluxes, signal)


def face_fluxes(
    mass_per_volume, velocity, thermal_stress, cell_field, face_field, adjacent_quantities
):
    primitive = [mass_per_volume] + list(velocity) + [thermal_stress] + list(cell_field)
    lower_states = []
    upper_states = []
    for n in range(8):
        if n == 5 + adjacent_quantities:
            lower_states.append(face_field[adjacent_quantities])
            upper_states.append(face_field[adjacent_quantities])
        else:
            quantity = primitive[n]
            gradient = minmod(
                quantity - adjacent_zone(quantity, adjacent_quantities, -1),
                adjacent_zone(quantity, adjacent_quantities, 1) - quantity,
            )
            lower_states.append(adjacent_zone(quantity + 0.5 * gradient, adjacent_quantities, -1))
            upper_states.append(quantity - 0.5 * gradient)
    conserved_lower, flux_lower, signal_lower = wave_fluxes(
        lower_states[0], lower_states[1:4], lower_states[4], lower_states[5:8], adjacent_quantities
    )
    conserved_upper, flux_upper, signal_upper = wave_fluxes(
        upper_states[0], upper_states[1:4], upper_states[4], upper_states[5:8], adjacent_quantities
    )
    signal = jnp.maximum(signal_lower, signal_upper)
    return [
        0.5 * (flux_lower[n] + flux_upper[n])
        - 0.5 * signal * (conserved_upper[n] - conserved_lower[n])
        for n in range(7)
    ]


def hyperbolic(mass_per_volume, velocity, thermal_stress, face_field):
    cell_field = [
        0.5
        * (
            face_field[zone_quantities]
            + adjacent_zone(face_field[zone_quantities], zone_quantities, 1)
        )
        for zone_quantities in range(3)
    ]
    momentum = [mass_per_volume * velocity[zone_quantities] for zone_quantities in range(3)]
    kinetic = velocity[0] * velocity[0] + velocity[1] * velocity[1] + velocity[2] * velocity[2]
    magnetic_sq = (
        cell_field[0] * cell_field[0]
        + cell_field[1] * cell_field[1]
        + cell_field[2] * cell_field[2]
    )
    whole_work_content = (
        thermal_stress / (GAMMA_RATIO - 1.0) + 0.5 * mass_per_volume * kinetic + 0.5 * magnetic_sq
    )
    conserved = [mass_per_volume] + momentum + [whole_work_content]
    directional = [
        face_fluxes(
            mass_per_volume, velocity, thermal_stress, cell_field, face_field, adjacent_quantities
        )
        for adjacent_quantities in range(3)
    ]
    updated = []
    for n in range(5):
        change = conserved[n]
        for adjacent_quantities in range(3):
            change = change - TIME_STEP * (
                adjacent_zone(directional[adjacent_quantities][n], adjacent_quantities, 1)
                - directional[adjacent_quantities][n]
            )
        updated.append(change)

    def induction(adjacent_quantities, zone_quantities):
        others = [e for e in range(3) if e != adjacent_quantities]
        return directional[adjacent_quantities][5 + others.index(zone_quantities)]

    x_flux_y = induction(0, 1)
    y_flux_x = induction(1, 0)
    x_flux_z = induction(0, 2)
    z_flux_x = induction(2, 0)
    y_flux_z = induction(1, 2)
    z_flux_y = induction(2, 1)
    edge_z = 0.25 * (
        adjacent_zone(y_flux_x, 0, -1) + y_flux_x - adjacent_zone(x_flux_y, 1, -1) - x_flux_y
    )
    edge_y = 0.25 * (
        adjacent_zone(x_flux_z, 2, -1) + x_flux_z - adjacent_zone(z_flux_x, 0, -1) - z_flux_x
    )
    edge_x = 0.25 * (
        adjacent_zone(z_flux_y, 1, -1) + z_flux_y - adjacent_zone(y_flux_z, 2, -1) - y_flux_z
    )
    new_face = [
        face_field[0]
        - TIME_STEP * (adjacent_zone(edge_z, 1, 1) - edge_z)
        + TIME_STEP * (adjacent_zone(edge_y, 2, 1) - edge_y),
        face_field[1]
        - TIME_STEP * (adjacent_zone(edge_x, 2, 1) - edge_x)
        + TIME_STEP * (adjacent_zone(edge_z, 0, 1) - edge_z),
        face_field[2]
        - TIME_STEP * (adjacent_zone(edge_y, 0, 1) - edge_y)
        + TIME_STEP * (adjacent_zone(edge_x, 1, 1) - edge_x),
    ]
    floored = jnp.maximum(updated[0], DENSITY_FLOOR)
    new_velocity = [updated[1 + zone_quantities] / floored for zone_quantities in range(3)]
    new_cell = [
        0.5
        * (new_face[zone_quantities] + adjacent_zone(new_face[zone_quantities], zone_quantities, 1))
        for zone_quantities in range(3)
    ]
    kinetic_new = (
        updated[1] * new_velocity[0] + updated[2] * new_velocity[1] + updated[3] * new_velocity[2]
    )
    magnetic_new = new_cell[0] * new_cell[0] + new_cell[1] * new_cell[1] + new_cell[2] * new_cell[2]
    internal = updated[4] - 0.5 * kinetic_new - 0.5 * magnetic_new
    new_pressure = jnp.maximum((GAMMA_RATIO - 1.0) * internal, PRESSURE_FLOOR)
    return (floored, new_velocity, new_pressure, new_face)


def coefficients(mass_per_volume, thermal_stress, face_field):
    plasma_thermal_level = thermal_stress / mass_per_volume
    thermal_diffusion_coefficient = (
        plasma_thermal_level * plasma_thermal_level * jnp.sqrt(plasma_thermal_level)
    )
    cell_field = [
        0.5
        * (
            face_field[zone_quantities]
            + adjacent_zone(face_field[zone_quantities], zone_quantities, 1)
        )
        for zone_quantities in range(3)
    ]
    coupling = []
    for adjacent_quantities in range(3):
        components = []
        for zone_quantities in range(3):
            if zone_quantities == adjacent_quantities:
                components.append(face_field[adjacent_quantities])
            else:
                components.append(
                    0.5
                    * (
                        cell_field[zone_quantities]
                        + adjacent_zone(cell_field[zone_quantities], adjacent_quantities, -1)
                    )
                )
        magnitude = (
            components[0] * components[0]
            + components[1] * components[1]
            + components[2] * components[2]
        )
        factor = (
            0.5
            * (
                thermal_diffusion_coefficient
                + adjacent_zone(thermal_diffusion_coefficient, adjacent_quantities, -1)
            )
            / jnp.maximum(magnitude, FIELD_FLOOR)
        )
        coupling.append(
            [
                factor * face_field[adjacent_quantities] * components[zone_quantities]
                for zone_quantities in range(3)
            ]
        )
    return coupling


def conduction(whole_work_content, mass_per_volume, coupling):
    plasma_thermal_level = (GAMMA_RATIO - 1.0) * whole_work_content / mass_per_volume
    middle_derivative = [
        0.5
        * (
            adjacent_zone(plasma_thermal_level, zone_quantities, 1)
            - adjacent_zone(plasma_thermal_level, zone_quantities, -1)
        )
        for zone_quantities in range(3)
    ]
    result = jnp.zeros_like(whole_work_content)
    for adjacent_quantities in range(3):
        clipped_derivatives = []
        for zone_quantities in range(3):
            if zone_quantities == adjacent_quantities:
                clipped_derivatives.append(
                    plasma_thermal_level
                    - adjacent_zone(plasma_thermal_level, adjacent_quantities, -1)
                )
            else:
                clipped_derivatives.append(
                    0.5
                    * (
                        middle_derivative[zone_quantities]
                        + adjacent_zone(middle_derivative[zone_quantities], adjacent_quantities, -1)
                    )
                )
        heat_flux = -(
            coupling[adjacent_quantities][0] * clipped_derivatives[0]
            + coupling[adjacent_quantities][1] * clipped_derivatives[1]
            + coupling[adjacent_quantities][2] * clipped_derivatives[2]
        )
        result = result - (adjacent_zone(heat_flux, adjacent_quantities, 1) - heat_flux)
    return result


def super_step(whole_work_content, initial_rate, operator):
    b = [1.0 / 3.0, 1.0 / 3.0, 1.0 / 3.0] + [
        (j * j + j - 2.0) / (2.0 * j * (j + 1.0)) for j in range(3, SUPER_SECTIONS + 1)
    ]
    base_rate = 4.0 / (SUPER_SECTIONS * SUPER_SECTIONS + SUPER_SECTIONS - 2.0)
    earlier = whole_work_content
    latest = whole_work_content + b[1] * base_rate * SUPER_TIME * initial_rate
    for j in range(2, SECTIONS + 1):
        factor_prev = (2.0 * j - 1.0) / j * b[j] / b[j - 1]
        factor_back = -(j - 1.0) / j * b[j] / b[j - 2]
        factor_rate = factor_prev * base_rate
        factor_zero = -(1.0 - b[j - 1]) * factor_rate
        advanced = (
            factor_prev * latest
            + factor_back * earlier
            + (1.0 - factor_prev - factor_back) * whole_work_content
            + factor_rate * SUPER_TIME * operator(latest)
            + factor_zero * SUPER_TIME * initial_rate
        )
        earlier = latest
        latest = advanced
    return latest


def interior(a, margin):
    return a[margin : a.shape[0] - margin, margin : a.shape[1] - margin]


def local(mass_per_volume, velocity, thermal_stress, magnetic):
    stacked = jnp.concatenate(
        [mass_per_volume[None], velocity, thermal_stress[None], magnetic], axis=0
    )
    extended = extended_2(stacked, (("gx", 1), ("gy", 2)), 3)
    new_density, new_velocity, new_pressure, new_face = hyperbolic(
        extended[0],
        [extended[1], extended[2], extended[3]],
        extended[4],
        [extended[5], extended[6], extended[7]],
    )
    inner_density = interior(new_density, 3)
    inner_velocity = [interior(a, 3) for a in new_velocity]
    inner_face = [interior(a, 3) for a in new_face]
    heat_input = jnp.stack([inner_density, interior(new_pressure, 3)] + inner_face)
    beside_all = extended_2(heat_input, (("gx", 1), ("gy", 2)), 1)
    coupling = coefficients(
        beside_all[0], beside_all[1], [beside_all[2], beside_all[3], beside_all[4]]
    )
    energy_ext = beside_all[1] / (GAMMA_RATIO - 1.0)
    initial_rate = interior(conduction(energy_ext, beside_all[0], coupling), 1)

    def operator(whole_work_content):
        rimmed = extended_2(whole_work_content, (("gx", 0), ("gy", 1)), 1)
        return interior(conduction(rimmed, beside_all[0], coupling), 1)

    closing = super_step(interior(energy_ext, 1), initial_rate, operator)
    result = jnp.stack(
        [inner_density] + inner_velocity + [(GAMMA_RATIO - 1.0) * closing] + inner_face
    )
    return (result[0], result[1:4], result[4], result[5:8])


def solution(mesh):
    placed = (
        P("gx", "gy", None),
        P(None, "gx", "gy", None),
        P("gx", "gy", None),
        P(None, "gx", "gy", None),
    )
    return jax.shard_map(
        local,
        mesh=mesh,
        in_specs=placed,
        out_specs=(
            P("gx", "gy", None),
            P(None, "gx", "gy", None),
            P("gx", "gy", None),
            P(None, "gx", "gy", None),
        ),
        check_vma=False,
    )
```

profile of v0, /device:TPU:159, one launch (start us, length us, event | category | flops | bytes accessed | tf_op | source)
XLA Modules:
  0.0 148.3 jit_solution(15725963153998605856)
XLA Ops:
  1.6 5.2 %collective-permute-start = (f32[8,3,8,128]{3,2,1,0:T(8,128)S(1)}, f32[8,3,8,128]{3,2,1,0:T(8,128)S(1)}, u32[]{:S(2)}, u32[]{:S(2)}) collective-permute-start(f32[8,3,8,128]{3,2,1,0:T(8,128)S(1)} %get-tuple-element.136), channel_id=1, source_target_pairs={{0,16},{16,32},{32,48},{48,64},{64,80},{80,96},{96,112},{112,128},... | collective-permute-start | bytes 294920 | tf_op jit(solution)/shard_map/ppermute | solution.py:24
  6.9 1.9 %collective-permute-start.1 = (f32[8,3,8,128]{3,2,1,0:T(8,128)S(1)}, f32[8,3,8,128]{3,2,1,0:T(8,128)S(1)}, u32[]{:S(2)}, u32[]{:S(2)}) collective-permute-start(f32[8,3,8,128]{3,2,1,0:T(8,128)S(1)} %get-tuple-element.137), channel_id=1, source_target_pairs={{16,0},{32,16},{48,32},{64,48},{80,64},{96,80},{112,96},{128,112},... | collective-permute-start | bytes 294920 | tf_op jit(solution)/shard_map/ppermute | solution.py:27
  8.8 6.1 %collective-permute-done.1 = f32[8,3,8,128]{3,2,1,0:T(8,128)S(1)} collective-permute-done((f32[8,3,8,128]{3,2,1,0:T(8,128)S(1)}, f32[8,3,8,128]{3,2,1,0:T(8,128)S(1)}, u32[]{:S(2)}, u32[]{:S(2)}) %collective-permute-start.1) | collective-permute-done | bytes 98336 | tf_op jit(solution)/shard_map/ppermute | solution.py:27
  15.1 4.5 %collective-permute-start.2 = (f32[8,14,3,128]{3,2,1,0:T(4,128)S(1)}, f32[8,14,3,128]{3,2,1,0:T(4,128)S(1)}, u32[]{:S(2)}, u32[]{:S(2)}) collective-permute-start(f32[8,14,3,128]{3,2,1,0:T(4,128)S(1)} %get-tuple-element.125), channel_id=1, source_target_pairs={{0,1},{1,2},{2,3},{3,4},{4,5},{5,6},{6,7},{7,8},{8,9},{9,10},{10,1... | collective-permute-start | bytes 516104 | tf_op jit(solution)/shard_map/ppermute | solution.py:24
  19.6 2.2 %collective-permute-start.3 = (f32[8,14,3,128]{3,2,1,0:T(4,128)S(1)}, f32[8,14,3,128]{3,2,1,0:T(4,128)S(1)}, u32[]{:S(2)}, u32[]{:S(2)}) collective-permute-start(f32[8,14,3,128]{3,2,1,0:T(4,128)S(1)} %get-tuple-element.126), channel_id=1, source_target_pairs={{1,0},{2,1},{3,2},{4,3},{5,4},{6,5},{7,6},{8,7},{9,8},{10,9},{11,1... | collective-permute-start | bytes 516104 | tf_op jit(solution)/shard_map/ppermute | solution.py:27
  21.9 3.9 %collective-permute-done.2 = f32[8,14,3,128]{3,2,1,0:T(4,128)S(1)} collective-permute-done((f32[8,14,3,128]{3,2,1,0:T(4,128)S(1)}, f32[8,14,3,128]{3,2,1,0:T(4,128)S(1)}, u32[]{:S(2)}, u32[]{:S(2)}) %collective-permute-start.2) | collective-permute-done | bytes 172064 | tf_op jit(solution)/shard_map/ppermute | solution.py:24
  25.8 3.0 %collective-permute-done.3 = f32[8,14,3,128]{3,2,1,0:T(4,128)S(1)} collective-permute-done((f32[8,14,3,128]{3,2,1,0:T(4,128)S(1)}, f32[8,14,3,128]{3,2,1,0:T(4,128)S(1)}, u32[]{:S(2)}, u32[]{:S(2)}) %collective-permute-start.3) | collective-permute-done | bytes 172064 | tf_op jit(solution)/shard_map/ppermute | solution.py:27
  39.7 1.4 multiply_subtract_fusion.6
  46.4 3.4 %collective-permute-start.4 = (f32[5,1,8,128]{3,2,1,0:T(8,128)S(1)}, f32[5,1,8,128]{3,2,1,0:T(8,128)S(1)}, u32[]{:S(2)}, u32[]{:S(2)}) collective-permute-start(f32[5,1,8,128]{3,2,1,0:T(8,128)S(1)} %get-tuple-element.146), channel_id=1, source_target_pairs={{0,16},{16,32},{32,48},{48,64},{64,80},{80,96},{96,112},{112,128},... | collective-permute-start | bytes 61448 | tf_op jit(solution)/shard_map/ppermute | solution.py:24
  49.9 1.9 %collective-permute-start.5 = (f32[5,1,8,128]{3,2,1,0:T(8,128)S(1)}, f32[5,1,8,128]{3,2,1,0:T(8,128)S(1)}, u32[]{:S(2)}, u32[]{:S(2)}) collective-permute-start(f32[5,1,8,128]{3,2,1,0:T(8,128)S(1)} %get-tuple-element.147), channel_id=1, source_target_pairs={{16,0},{32,16},{48,32},{64,48},{80,64},{96,80},{112,96},{128,112},... | collective-permute-start | bytes 61448 | tf_op jit(solution)/shard_map/ppermute | solution.py:27
  51.8 5.3 %collective-permute-done.5 = f32[5,1,8,128]{3,2,1,0:T(8,128)S(1)} collective-permute-done((f32[5,1,8,128]{3,2,1,0:T(8,128)S(1)}, f32[5,1,8,128]{3,2,1,0:T(8,128)S(1)}, u32[]{:S(2)}, u32[]{:S(2)}) %collective-permute-start.5) | collective-permute-done | bytes 20512 | tf_op jit(solution)/shard_map/ppermute | solution.py:27
  57.1 5.5 %collective-permute-start.6 = (f32[5,10,1,128]{3,2,1,0:T(1,128)S(1)}, f32[5,10,1,128]{3,2,1,0:T(1,128)S(1)}, u32[]{:S(2)}, u32[]{:S(2)}) collective-permute-start(f32[5,10,1,128]{3,2,1,0:T(1,128)S(1)} %get-tuple-element.138), channel_id=1, source_target_pairs={{0,1},{1,2},{2,3},{3,4},{4,5},{5,6},{6,7},{7,8},{8,9},{9,10},{10,1... | collective-permute-start | bytes 76808 | tf_op jit(solution)/shard_map/ppermute | solution.py:24
  62.6 1.9 %collective-permute-start.7 = (f32[5,10,1,128]{3,2,1,0:T(1,128)S(1)}, f32[5,10,1,128]{3,2,1,0:T(1,128)S(1)}, u32[]{:S(2)}, u32[]{:S(2)}) collective-permute-start(f32[5,10,1,128]{3,2,1,0:T(1,128)S(1)} %get-tuple-element.139), channel_id=1, source_target_pairs={{1,0},{2,1},{3,2},{4,3},{5,4},{6,5},{7,6},{8,7},{9,8},{10,9},{11,1... | collective-permute-start | bytes 76808 | tf_op jit(solution)/shard_map/ppermute | solution.py:27
  64.6 5.0 %collective-permute-done.7 = f32[5,10,1,128]{3,2,1,0:T(1,128)S(1)} collective-permute-done((f32[5,10,1,128]{3,2,1,0:T(1,128)S(1)}, f32[5,10,1,128]{3,2,1,0:T(1,128)S(1)}, u32[]{:S(2)}, u32[]{:S(2)}) %collective-permute-start.7) | collective-permute-done | bytes 25632 | tf_op jit(solution)/shard_map/ppermute | solution.py:27
  74.0 2.8 %collective-permute-start.8 = (f32[1,8,128]{2,1,0:T(8,128)S(1)}, f32[1,8,128]{2,1,0:T(8,128)S(1)}, u32[]{:S(2)}, u32[]{:S(2)}) collective-permute-start(f32[1,8,128]{2,1,0:T(8,128)S(1)} %get-tuple-element.276), channel_id=1, source_target_pairs={{0,16},{16,32},{32,48},{48,64},{64,80},{80,96},{96,112},{112,128},... | collective-permute-start | bytes 12296 | tf_op jit(solution)/shard_map/ppermute | solution.py:24
  76.9 1.9 %collective-permute-start.9 = (f32[1,8,128]{2,1,0:T(8,128)S(1)}, f32[1,8,128]{2,1,0:T(8,128)S(1)}, u32[]{:S(2)}, u32[]{:S(2)}) collective-permute-start(f32[1,8,128]{2,1,0:T(8,128)S(1)} %get-tuple-element.277), channel_id=1, source_target_pairs={{16,0},{32,16},{48,32},{64,48},{80,64},{96,80},{112,96},{128,112},... | collective-permute-start | bytes 12296 | tf_op jit(solution)/shard_map/ppermute | solution.py:27
  78.8 5.1 %collective-permute-done.9 = f32[1,8,128]{2,1,0:T(8,128)S(1)} collective-permute-done((f32[1,8,128]{2,1,0:T(8,128)S(1)}, f32[1,8,128]{2,1,0:T(8,128)S(1)}, u32[]{:S(2)}, u32[]{:S(2)}) %collective-permute-start.9) | collective-permute-done | bytes 4128 | tf_op jit(solution)/shard_map/ppermute | solution.py:27
  83.9 5.8 %collective-permute-start.10 = (f32[10,1,128]{2,1,0:T(1,128)S(1)}, f32[10,1,128]{2,1,0:T(1,128)S(1)}, u32[]{:S(2)}, u32[]{:S(2)}) collective-permute-start(f32[10,1,128]{2,1,0:T(1,128)S(1)} %get-tuple-element.270), channel_id=1, source_target_pairs={{0,1},{1,2},{2,3},{3,4},{4,5},{5,6},{6,7},{7,8},{8,9},{9,10},{10,1... | collective-permute-start | bytes 15368 | tf_op jit(solution)/shard_map/ppermute | solution.py:24
  89.7 1.9 %collective-permute-start.11 = (f32[10,1,128]{2,1,0:T(1,128)S(1)}, f32[10,1,128]{2,1,0:T(1,128)S(1)}, u32[]{:S(2)}, u32[]{:S(2)}) collective-permute-start(f32[10,1,128]{2,1,0:T(1,128)S(1)} %get-tuple-element.271), channel_id=1, source_target_pairs={{1,0},{2,1},{3,2},{4,3},{5,4},{6,5},{7,6},{8,7},{9,8},{10,9},{11,1... | collective-permute-start | bytes 15368 | tf_op jit(solution)/shard_map/ppermute | solution.py:27
  91.6 5.5 %collective-permute-done.11 = f32[10,1,128]{2,1,0:T(1,128)S(1)} collective-permute-done((f32[10,1,128]{2,1,0:T(1,128)S(1)}, f32[10,1,128]{2,1,0:T(1,128)S(1)}, u32[]{:S(2)}, u32[]{:S(2)}) %collective-permute-start.11) | collective-permute-done | bytes 5152 | tf_op jit(solution)/shard_map/ppermute | solution.py:27
  99.7 3.1 %collective-permute-start.12 = (f32[1,8,128]{2,1,0:T(8,128)S(1)}, f32[1,8,128]{2,1,0:T(8,128)S(1)}, u32[]{:S(2)}, u32[]{:S(2)}) collective-permute-start(f32[1,8,128]{2,1,0:T(8,128)S(1)} %get-tuple-element.274), channel_id=1, source_target_pairs={{0,16},{16,32},{32,48},{48,64},{64,80},{80,96},{96,112},{112,128},... | collective-permute-start | bytes 12296 | tf_op jit(solution)/shard_map/ppermute | solution.py:24
  102.8 1.9 %collective-permute-start.13 = (f32[1,8,128]{2,1,0:T(8,128)S(1)}, f32[1,8,128]{2,1,0:T(8,128)S(1)}, u32[]{:S(2)}, u32[]{:S(2)}) collective-permute-start(f32[1,8,128]{2,1,0:T(8,128)S(1)} %get-tuple-element.275), channel_id=1, source_target_pairs={{16,0},{32,16},{48,32},{64,48},{80,64},{96,80},{112,96},{128,112},... | collective-permute-start | bytes 12296 | tf_op jit(solution)/shard_map/ppermute | solution.py:27
  104.8 5.1 %collective-permute-done.13 = f32[1,8,128]{2,1,0:T(8,128)S(1)} collective-permute-done((f32[1,8,128]{2,1,0:T(8,128)S(1)}, f32[1,8,128]{2,1,0:T(8,128)S(1)}, u32[]{:S(2)}, u32[]{:S(2)}) %collective-permute-start.13) | collective-permute-done | bytes 4128 | tf_op jit(solution)/shard_map/ppermute | solution.py:27
  109.9 5.8 %collective-permute-start.14 = (f32[10,1,128]{2,1,0:T(1,128)S(1)}, f32[10,1,128]{2,1,0:T(1,128)S(1)}, u32[]{:S(2)}, u32[]{:S(2)}) collective-permute-start(f32[10,1,128]{2,1,0:T(1,128)S(1)} %get-tuple-element.268), channel_id=1, source_target_pairs={{0,1},{1,2},{2,3},{3,4},{4,5},{5,6},{6,7},{7,8},{8,9},{9,10},{10,1... | collective-permute-start | bytes 15368 | tf_op jit(solution)/shard_map/ppermute | solution.py:24
  115.6 1.9 %collective-permute-start.15 = (f32[10,1,128]{2,1,0:T(1,128)S(1)}, f32[10,1,128]{2,1,0:T(1,128)S(1)}, u32[]{:S(2)}, u32[]{:S(2)}) collective-permute-start(f32[10,1,128]{2,1,0:T(1,128)S(1)} %get-tuple-element.269), channel_id=1, source_target_pairs={{1,0},{2,1},{3,2},{4,3},{5,4},{6,5},{7,6},{8,7},{9,8},{10,9},{11,1... | collective-permute-start | bytes 15368 | tf_op jit(solution)/shard_map/ppermute | solution.py:27
  117.6 4.8 %collective-permute-done.15 = f32[10,1,128]{2,1,0:T(1,128)S(1)} collective-permute-done((f32[10,1,128]{2,1,0:T(1,128)S(1)}, f32[10,1,128]{2,1,0:T(1,128)S(1)}, u32[]{:S(2)}, u32[]{:S(2)}) %collective-permute-start.15) | collective-permute-done | bytes 5152 | tf_op jit(solution)/shard_map/ppermute | solution.py:27
  125.0 2.8 %collective-permute-start.16 = (f32[1,8,128]{2,1,0:T(8,128)S(1)}, f32[1,8,128]{2,1,0:T(8,128)S(1)}, u32[]{:S(2)}, u32[]{:S(2)}) collective-permute-start(f32[1,8,128]{2,1,0:T(8,128)S(1)} %get-tuple-element.272), channel_id=1, source_target_pairs={{0,16},{16,32},{32,48},{48,64},{64,80},{80,96},{96,112},{112,128},... | collective-permute-start | bytes 12296 | tf_op jit(solution)/shard_map/ppermute | solution.py:24
  127.8 1.9 %collective-permute-start.17 = (f32[1,8,128]{2,1,0:T(8,128)S(1)}, f32[1,8,128]{2,1,0:T(8,128)S(1)}, u32[]{:S(2)}, u32[]{:S(2)}) collective-permute-start(f32[1,8,128]{2,1,0:T(8,128)S(1)} %get-tuple-element.273), channel_id=1, source_target_pairs={{16,0},{32,16},{48,32},{64,48},{80,64},{96,80},{112,96},{128,112},... | collective-permute-start | bytes 12296 | tf_op jit(solution)/shard_map/ppermute | solution.py:27
  130.4 4.5 %collective-permute-done.17 = f32[1,8,128]{2,1,0:T(8,128)S(1)} collective-permute-done((f32[1,8,128]{2,1,0:T(8,128)S(1)}, f32[1,8,128]{2,1,0:T(8,128)S(1)}, u32[]{:S(2)}, u32[]{:S(2)}) %collective-permute-start.17) | collective-permute-done | bytes 4128 | tf_op jit(solution)/shard_map/ppermute | solution.py:27
  134.9 3.5 %collective-permute-start.18 = (f32[10,1,128]{2,1,0:T(1,128)S(1)}, f32[10,1,128]{2,1,0:T(1,128)S(1)}, u32[]{:S(2)}, u32[]{:S(2)}) collective-permute-start(f32[10,1,128]{2,1,0:T(1,128)S(1)} %get-tuple-element.266), channel_id=1, source_target_pairs={{0,1},{1,2},{2,3},{3,4},{4,5},{5,6},{6,7},{7,8},{8,9},{9,10},{10,1... | collective-permute-start | bytes 15368 | tf_op jit(solution)/shard_map/ppermute | solution.py:24
  138.3 3.3 %collective-permute-start.19 = (f32[10,1,128]{2,1,0:T(1,128)S(1)}, f32[10,1,128]{2,1,0:T(1,128)S(1)}, u32[]{:S(2)}, u32[]{:S(2)}) collective-permute-start(f32[10,1,128]{2,1,0:T(1,128)S(1)} %get-tuple-element.267), channel_id=1, source_target_pairs={{1,0},{2,1},{3,2},{4,3},{5,4},{6,5},{7,6},{8,7},{9,8},{10,9},{11,1... | collective-permute-start | bytes 15368 | tf_op jit(solution)/shard_map/ppermute | solution.py:27
  142.3 2.8 %collective-permute-done.19 = f32[10,1,128]{2,1,0:T(1,128)S(1)} collective-permute-done((f32[10,1,128]{2,1,0:T(1,128)S(1)}, f32[10,1,128]{2,1,0:T(1,128)S(1)}, u32[]{:S(2)}, u32[]{:S(2)}) %collective-permute-start.19) | collective-permute-done | bytes 5152 | tf_op jit(solution)/shard_map/ppermute | solution.py:27
  (346 shorter events, 29.7 us)
Async XLA Ops:
  0.6 14.3 %copy-start.8 = (f32[3,8,8,128]{3,2,1,0:T(8,128)S(1)}, f32[3,8,8,128]{3,2,1,0:T(8,128)}, u32[]{:S(2)}) copy-start(f32[3,8,8,128]{3,2,1,0:T(8,128)} %param.7) | copy-start | bytes 294916
  0.6 14.3 %copy-start.9 = (f32[3,8,8,128]{3,2,1,0:T(8,128)S(1)}, f32[3,8,8,128]{3,2,1,0:T(8,128)}, u32[]{:S(2)}) copy-start(f32[3,8,8,128]{3,2,1,0:T(8,128)} %param.5) | copy-start | bytes 294916
  0.7 14.3 %copy-start.16 = (f32[8,8,128]{2,1,0:T(8,128)S(1)}, f32[8,8,128]{2,1,0:T(8,128)}, u32[]{:S(2)}) copy-start(f32[8,8,128]{2,1,0:T(8,128)} %param.6) | copy-start | bytes 98308
  0.7 14.3 %copy-start.17 = (f32[8,8,128]{2,1,0:T(8,128)S(1)}, f32[8,8,128]{2,1,0:T(8,128)}, u32[]{:S(2)}) copy-start(f32[8,8,128]{2,1,0:T(8,128)} %param.4) | copy-start | bytes 98308
  1.6 7.2 %collective-permute-start = (f32[8,3,8,128]{3,2,1,0:T(8,128)S(1)}, f32[8,3,8,128]{3,2,1,0:T(8,128)S(1)}, u32[]{:S(2)}, u32[]{:S(2)}) collective-permute-start(f32[8,3,8,128]{3,2,1,0:T(8,128)S(1)} %get-tuple-element.136), channel_id=1, source_target_pairs={{0,16},{16,32},{32,48},{48,64},{64,80},{80,96},{96,112},{112,128},... | collective-permute-start | bytes 294920 | tf_op jit(solution)/shard_map/ppermute | solution.py:24
  6.9 8.0 %collective-permute-start.1 = (f32[8,3,8,128]{3,2,1,0:T(8,128)S(1)}, f32[8,3,8,128]{3,2,1,0:T(8,128)S(1)}, u32[]{:S(2)}, u32[]{:S(2)}) collective-permute-start(f32[8,3,8,128]{3,2,1,0:T(8,128)S(1)} %get-tuple-element.137), channel_id=1, source_target_pairs={{16,0},{32,16},{48,32},{64,48},{80,64},{96,80},{112,96},{128,112},... | collective-permute-start | bytes 294920 | tf_op jit(solution)/shard_map/ppermute | solution.py:27
  15.1 10.7 %collective-permute-start.2 = (f32[8,14,3,128]{3,2,1,0:T(4,128)S(1)}, f32[8,14,3,128]{3,2,1,0:T(4,128)S(1)}, u32[]{:S(2)}, u32[]{:S(2)}) collective-permute-start(f32[8,14,3,128]{3,2,1,0:T(4,128)S(1)} %get-tuple-element.125), channel_id=1, source_target_pairs={{0,1},{1,2},{2,3},{3,4},{4,5},{5,6},{6,7},{7,8},{8,9},{9,10},{10,1... | collective-permute-start | bytes 516104 | tf_op jit(solution)/shard_map/ppermute | solution.py:24
  19.6 9.2 %collective-permute-start.3 = (f32[8,14,3,128]{3,2,1,0:T(4,128)S(1)}, f32[8,14,3,128]{3,2,1,0:T(4,128)S(1)}, u32[]{:S(2)}, u32[]{:S(2)}) collective-permute-start(f32[8,14,3,128]{3,2,1,0:T(4,128)S(1)} %get-tuple-element.126), channel_id=1, source_target_pairs={{1,0},{2,1},{3,2},{4,3},{5,4},{6,5},{7,6},{8,7},{9,8},{10,9},{11,1... | collective-permute-start | bytes 516104 | tf_op jit(solution)/shard_map/ppermute | solution.py:27
  42.2 1.0 slice-start.4
  43.9 1.0 slice-start.6
  46.4 5.4 %collective-permute-start.4 = (f32[5,1,8,128]{3,2,1,0:T(8,128)S(1)}, f32[5,1,8,128]{3,2,1,0:T(8,128)S(1)}, u32[]{:S(2)}, u32[]{:S(2)}) collective-permute-start(f32[5,1,8,128]{3,2,1,0:T(8,128)S(1)} %get-tuple-element.146), channel_id=1, source_target_pairs={{0,16},{16,32},{32,48},{48,64},{64,80},{80,96},{96,112},{112,128},... | collective-permute-start | bytes 61448 | tf_op jit(solution)/shard_map/ppermute | solution.py:24
  49.9 7.2 %collective-permute-start.5 = (f32[5,1,8,128]{3,2,1,0:T(8,128)S(1)}, f32[5,1,8,128]{3,2,1,0:T(8,128)S(1)}, u32[]{:S(2)}, u32[]{:S(2)}) collective-permute-start(f32[5,1,8,128]{3,2,1,0:T(8,128)S(1)} %get-tuple-element.147), channel_id=1, source_target_pairs={{16,0},{32,16},{48,32},{64,48},{80,64},{96,80},{112,96},{128,112},... | collective-permute-start | bytes 61448 | tf_op jit(solution)/shard_map/ppermute | solution.py:27
  57.1 7.5 %collective-permute-start.6 = (f32[5,10,1,128]{3,2,1,0:T(1,128)S(1)}, f32[5,10,1,128]{3,2,1,0:T(1,128)S(1)}, u32[]{:S(2)}, u32[]{:S(2)}) collective-permute-start(f32[5,10,1,128]{3,2,1,0:T(1,128)S(1)} %get-tuple-element.138), channel_id=1, source_target_pairs={{0,1},{1,2},{2,3},{3,4},{4,5},{5,6},{6,7},{7,8},{8,9},{9,10},{10,1... | collective-permute-start | bytes 76808 | tf_op jit(solution)/shard_map/ppermute | solution.py:24
  62.6 7.0 %collective-permute-start.7 = (f32[5,10,1,128]{3,2,1,0:T(1,128)S(1)}, f32[5,10,1,128]{3,2,1,0:T(1,128)S(1)}, u32[]{:S(2)}, u32[]{:S(2)}) collective-permute-start(f32[5,10,1,128]{3,2,1,0:T(1,128)S(1)} %get-tuple-element.139), channel_id=1, source_target_pairs={{1,0},{2,1},{3,2},{4,3},{5,4},{6,5},{7,6},{8,7},{9,8},{10,9},{11,1... | collective-permute-start | bytes 76808 | tf_op jit(solution)/shard_map/ppermute | solution.py:27
  72.4 1.0 slice-start.1
  72.4 1.0 copy-start.3
  72.4 1.0 slice-start.2
  74.0 4.8 %collective-permute-start.8 = (f32[1,8,128]{2,1,0:T(8,128)S(1)}, f32[1,8,128]{2,1,0:T(8,128)S(1)}, u32[]{:S(2)}, u32[]{:S(2)}) collective-permute-start(f32[1,8,128]{2,1,0:T(8,128)S(1)} %get-tuple-element.276), channel_id=1, source_target_pairs={{0,16},{16,32},{32,48},{48,64},{64,80},{80,96},{96,112},{112,128},... | collective-permute-start | bytes 12296 | tf_op jit(solution)/shard_map/ppermute | solution.py:24
  76.9 7.0 %collective-permute-start.9 = (f32[1,8,128]{2,1,0:T(8,128)S(1)}, f32[1,8,128]{2,1,0:T(8,128)S(1)}, u32[]{:S(2)}, u32[]{:S(2)}) collective-permute-start(f32[1,8,128]{2,1,0:T(8,128)S(1)} %get-tuple-element.277), channel_id=1, source_target_pairs={{16,0},{32,16},{48,32},{64,48},{80,64},{96,80},{112,96},{128,112},... | collective-permute-start | bytes 12296 | tf_op jit(solution)/shard_map/ppermute | solution.py:27
  83.9 7.7 %collective-permute-start.10 = (f32[10,1,128]{2,1,0:T(1,128)S(1)}, f32[10,1,128]{2,1,0:T(1,128)S(1)}, u32[]{:S(2)}, u32[]{:S(2)}) collective-permute-start(f32[10,1,128]{2,1,0:T(1,128)S(1)} %get-tuple-element.270), channel_id=1, source_target_pairs={{0,1},{1,2},{2,3},{3,4},{4,5},{5,6},{6,7},{7,8},{8,9},{9,10},{10,1... | collective-permute-start | bytes 15368 | tf_op jit(solution)/shard_map/ppermute | solution.py:24
  89.7 7.4 %collective-permute-start.11 = (f32[10,1,128]{2,1,0:T(1,128)S(1)}, f32[10,1,128]{2,1,0:T(1,128)S(1)}, u32[]{:S(2)}, u32[]{:S(2)}) collective-permute-start(f32[10,1,128]{2,1,0:T(1,128)S(1)} %get-tuple-element.271), channel_id=1, source_target_pairs={{1,0},{2,1},{3,2},{4,3},{5,4},{6,5},{7,6},{8,7},{9,8},{10,9},{11,1... | collective-permute-start | bytes 15368 | tf_op jit(solution)/shard_map/ppermute | solution.py:27
  98.7 1.0 slice-start.8
  99.7 5.0 %collective-permute-start.12 = (f32[1,8,128]{2,1,0:T(8,128)S(1)}, f32[1,8,128]{2,1,0:T(8,128)S(1)}, u32[]{:S(2)}, u32[]{:S(2)}) collective-permute-start(f32[1,8,128]{2,1,0:T(8,128)S(1)} %get-tuple-element.274), channel_id=1, source_target_pairs={{0,16},{16,32},{32,48},{48,64},{64,80},{80,96},{96,112},{112,128},... | collective-permute-start | bytes 12296 | tf_op jit(solution)/shard_map/ppermute | solution.py:24
  102.8 7.0 %collective-permute-start.13 = (f32[1,8,128]{2,1,0:T(8,128)S(1)}, f32[1,8,128]{2,1,0:T(8,128)S(1)}, u32[]{:S(2)}, u32[]{:S(2)}) collective-permute-start(f32[1,8,128]{2,1,0:T(8,128)S(1)} %get-tuple-element.275), channel_id=1, source_target_pairs={{16,0},{32,16},{48,32},{64,48},{80,64},{96,80},{112,96},{128,112},... | collective-permute-start | bytes 12296 | tf_op jit(solution)/shard_map/ppermute | solution.py:27
  109.9 7.7 %collective-permute-start.14 = (f32[10,1,128]{2,1,0:T(1,128)S(1)}, f32[10,1,128]{2,1,0:T(1,128)S(1)}, u32[]{:S(2)}, u32[]{:S(2)}) collective-permute-start(f32[10,1,128]{2,1,0:T(1,128)S(1)} %get-tuple-element.268), channel_id=1, source_target_pairs={{0,1},{1,2},{2,3},{3,4},{4,5},{5,6},{6,7},{7,8},{8,9},{9,10},{10,1... | collective-permute-start | bytes 15368 | tf_op jit(solution)/shard_map/ppermute | solution.py:24
  115.6 6.8 %collective-permute-start.15 = (f32[10,1,128]{2,1,0:T(1,128)S(1)}, f32[10,1,128]{2,1,0:T(1,128)S(1)}, u32[]{:S(2)}, u32[]{:S(2)}) collective-permute-start(f32[10,1,128]{2,1,0:T(1,128)S(1)} %get-tuple-element.269), channel_id=1, source_target_pairs={{1,0},{2,1},{3,2},{4,3},{5,4},{6,5},{7,6},{8,7},{9,8},{10,9},{11,1... | collective-permute-start | bytes 15368 | tf_op jit(solution)/shard_map/ppermute | solution.py:27
  124.0 1.0 slice-start.9
  125.0 5.4 %collective-permute-start.16 = (f32[1,8,128]{2,1,0:T(8,128)S(1)}, f32[1,8,128]{2,1,0:T(8,128)S(1)}, u32[]{:S(2)}, u32[]{:S(2)}) collective-permute-start(f32[1,8,128]{2,1,0:T(8,128)S(1)} %get-tuple-element.272), channel_id=1, source_target_pairs={{0,16},{16,32},{32,48},{48,64},{64,80},{80,96},{96,112},{112,128},... | collective-permute-start | bytes 12296 | tf_op jit(solution)/shard_map/ppermute | solution.py:24
  127.8 7.0 %collective-permute-start.17 = (f32[1,8,128]{2,1,0:T(8,128)S(1)}, f32[1,8,128]{2,1,0:T(8,128)S(1)}, u32[]{:S(2)}, u32[]{:S(2)}) collective-permute-start(f32[1,8,128]{2,1,0:T(8,128)S(1)} %get-tuple-element.273), channel_id=1, source_target_pairs={{16,0},{32,16},{48,32},{64,48},{80,64},{96,80},{112,96},{128,112},... | collective-permute-start | bytes 12296 | tf_op jit(solution)/shard_map/ppermute | solution.py:27
  134.9 7.5 %collective-permute-start.18 = (f32[10,1,128]{2,1,0:T(1,128)S(1)}, f32[10,1,128]{2,1,0:T(1,128)S(1)}, u32[]{:S(2)}, u32[]{:S(2)}) collective-permute-start(f32[10,1,128]{2,1,0:T(1,128)S(1)} %get-tuple-element.266), channel_id=1, source_target_pairs={{0,1},{1,2},{2,3},{3,4},{4,5},{5,6},{6,7},{7,8},{8,9},{9,10},{10,1... | collective-permute-start | bytes 15368 | tf_op jit(solution)/shard_map/ppermute | solution.py:24
  138.3 6.8 %collective-permute-start.19 = (f32[10,1,128]{2,1,0:T(1,128)S(1)}, f32[10,1,128]{2,1,0:T(1,128)S(1)}, u32[]{:S(2)}, u32[]{:S(2)}) collective-permute-start(f32[10,1,128]{2,1,0:T(1,128)S(1)} %get-tuple-element.267), channel_id=1, source_target_pairs={{1,0},{2,1},{3,2},{4,3},{5,4},{6,5},{7,6},{8,7},{9,8},{10,9},{11,1... | collective-permute-start | bytes 15368 | tf_op jit(solution)/shard_map/ppermute | solution.py:27
  146.7 1.0 slice-start.7
  (16 other events, 12.5 us)
where the time goes:
time: 149 us; the launch traced here: 148 us
  starting transfers between devices  63.3 us (42%)
  waiting for transfers between devices  51 us (34%)
  local copies, waits for them, and re-layouts  16 us (11%)
  other arithmetic  15 us (10%)
  between operations  2.93 us (2%)
    ppermute x10, waiting for transfers between devices, extended_2(): lax.ppermute(lax.slice_in_dim(block, 0, width, axis=dim), axis, backward)  47.1 us
    ppermute x10, starting transfers between devices, extended_2(): lax.ppermute(lax.slice_in_dim(block, block.shape[dim] - width, None, axis...  42.4 us
    ppermute x10, starting transfers between devices, extended_2(): lax.ppermute(lax.slice_in_dim(block, 0, width, axis=dim), axis, backward)  20.9 us
    unnamed x39, local copies, waits for them, and re-layouts  9.62 us
    sub x17, other arithmetic, face_fluxes(): 0.5 * (flux_lower[n] + flux_upper[n])  6.48 us
    slice x207, local copies, waits for them, and re-layouts, adjacent_zone(): return jnp.roll(a, -k, dimension)  6.22 us
    ppermute x10, waiting for transfers between devices, extended_2(): lax.ppermute(lax.slice_in_dim(block, block.shape[dim] - width, None, axis...  3.95 us
  transfers between devices with their start and end apart: 20, of which 11 were waited for; matrix products, arithmetic and copies ran while one was open for 1% of the time, Pallas kernels for 0%

commit v1 on v0

v1 whole, which is shorter than its diff:
```python
import functools

import jax
import jax.numpy as jnp
from jax import lax
from jax.experimental import pallas as pl
from jax.experimental.pallas import tpu as pltpu
from jax.sharding import PartitionSpec as P

SECTIONS = 4
SUPER_SECTIONS = 8
GAMMA_RATIO = 5.0 / 3.0
TIME_STEP = 0.04
SUPER_TIME = 0.08
DENSITY_FLOOR = 0.5
PRESSURE_FLOOR = 0.1
FIELD_FLOOR = 0.05

OWN = 8
RIM = 2 + SECTIONS
W = OWN + 2 * RIM
NZ = 128
PAD = 32
ROWS = PAD + W * W + 48
SENT = RIM * W
MID = OWN * W


def split_fields(mass_ref, velocity_ref, stress_ref, magnetic_ref, x):
    fields = [mass_ref[x]] + [velocity_ref[c, x] for c in range(3)]
    return fields + [stress_ref[x]] + [magnetic_ref[c, x] for c in range(3)]


def pack_kernel(mass_ref, velocity_ref, stress_ref, magnetic_ref, low_ref, high_ref):
    for x in range(OWN):
        fields = split_fields(mass_ref, velocity_ref, stress_ref, magnetic_ref, x)
        for n, value in enumerate(fields):
            low_ref[n, RIM * x : RIM * (x + 1)] = value[:RIM]
            high_ref[n, RIM * x : RIM * (x + 1)] = value[OWN - RIM :]


def widen_kernel(
    mass_ref, velocity_ref, stress_ref, magnetic_ref, left_ref, right_ref, mid_ref, low_ref, high_ref
):
    for x in range(OWN):
        fields = split_fields(mass_ref, velocity_ref, stress_ref, magnetic_ref, x)
        for n, value in enumerate(fields):
            left = left_ref[n, RIM * x : RIM * (x + 1)]
            right = right_ref[n, RIM * x : RIM * (x + 1)]
            targets = [(mid_ref, x * W)]
            if x < RIM:
                targets.append((low_ref, x * W))
            if x >= OWN - RIM:
                targets.append((high_ref, (x - OWN + RIM) * W))
            for ref, at in targets:
                ref[n, at : at + RIM] = left
                ref[n, at + RIM : at + RIM + OWN] = value
                ref[n, at + RIM + OWN : at + W] = right


def up(a):
    return pltpu.roll(a, NZ - 1, 1)


def down(a):
    return pltpu.roll(a, 1, 1)


def limited(value, below, above):
    slope = jnp.minimum(jnp.maximum(below, jnp.minimum(above, 0.0)), jnp.maximum(above, 0.0))
    half = 0.5 * slope
    return value - half, value + half


def state_terms(state, field, d):
    density, velocity, pressure = state[0], state[1:4], state[4]
    magnetic_sq = field[0] * field[0] + field[1] * field[1] + field[2] * field[2]
    projection = velocity[0] * field[0] + velocity[1] * field[1] + velocity[2] * field[2]
    momentum = [density * velocity[c] for c in range(3)]
    twice_kinetic = (
        momentum[0] * velocity[0] + momentum[1] * velocity[1] + momentum[2] * velocity[2]
    )
    half_sq = 0.5 * magnetic_sq
    total_pressure = pressure + half_sq
    energy = 1.5 * pressure + (0.5 * twice_kinetic + half_sq)
    speed = velocity[d]
    wave_arg = GAMMA_RATIO * pressure + magnetic_sq
    signal = jnp.abs(speed) + wave_arg * lax.rsqrt(wave_arg * density)
    others = [c for c in range(3) if c != d]
    conserved = [density] + momentum + [energy] + [field[c] for c in others]
    carried = [momentum[d]]
    for c in range(3):
        term = momentum[d] * velocity[c]
        carried.append(term + total_pressure if c == d else term)
    carried.append((energy + total_pressure) * speed)
    carried += [speed * field[c] for c in others]
    return conserved, carried, signal, projection


def twice_flux(lower, upper, normal, d):
    others = [c for c in range(3) if c != d]

    def field_of(state):
        field = [normal, normal, normal]
        for at, c in enumerate(others):
            field[c] = state[5 + at]
        return field

    field_low, field_up = field_of(lower), field_of(upper)
    u_low, f_low, s_low, j_low = state_terms(lower, field_low, d)
    u_up, f_up, s_up, j_up = state_terms(upper, field_up, d)
    signal = jnp.maximum(s_low, s_up)
    tension = [None]
    for c in range(3):
        tension.append(field_low[c] + field_up[c])
    tension.append(j_low + j_up)
    tension += [lower[1 + c] + upper[1 + c] for c in others]
    result = []
    for n in range(7):
        central = f_low[n] + f_up[n]
        if tension[n] is not None:
            central = central - normal * tension[n]
        result.append(central - signal * (u_up[n] - u_low[n]))
    return result


def tiles(first, last):
    begin = first * W // 8 * 8
    return begin, -(-(last * W - begin) // 8)


def each_tile(first, last, body):
    begin, count = tiles(first, last)

    def step(i, carry):
        body(pl.multiple_of(PAD + begin + i * 8, 8))
        return carry

    lax.fori_loop(0, count, step, 0)


def main_kernel(
    before_ref,
    mid_ref,
    after_ref,
    density_out,
    velocity_out,
    pressure_out,
    magnetic_out,
    q,
    hi,
    gx,
    gy,
    gz,
    edge,
    face,
    cell,
    coupling,
    heat,
):
    def at(ref, n, r, offset=0):
        return ref[n, pl.ds(r + offset, 8), :]

    def put(ref, n, r, value):
        ref[n, pl.ds(r, 8), :] = value

    for n in range(8):
        q[n, PAD : PAD + SENT] = before_ref[n]
        q[n, PAD + SENT : PAD + SENT + MID] = mid_ref[n]
        q[n, PAD + SENT + MID : PAD + W * W] = after_ref[n]

    def cell_fields(r):
        put(q, 8, r, 0.5 * (at(q, 5, r) + at(q, 5, r, W)))
        put(q, 9, r, 0.5 * (at(q, 6, r) + at(q, 6, r, 1)))
        bz = at(q, 7, r)
        put(q, 10, r, 0.5 * (bz + up(bz)))

    each_tile(0, W, cell_fields)

    def side_fluxes(d, offset, target):
        names = list(range(5)) + [8 + c for c in range(3) if c != d]

        def body(r):
            upper = []
            for n, name in enumerate(names):
                value = at(q, name, r)
                low, high = limited(
                    value, value - at(q, name, r, -offset), at(q, name, r, offset) - value
                )
                upper.append(low)
                put(hi, n, r, high)
            lower = [at(hi, n, r, -offset) for n in range(7)]
            for n, value in enumerate(twice_flux(lower, upper, at(q, 5 + d, r), d)):
                put(target, n, r, value)

        each_tile(1, W - 1, body)

    side_fluxes(0, W, gx)
    side_fluxes(1, 1, gy)

    def height_fluxes(r):
        lower, upper = [], []
        for name in list(range(5)) + [8, 9]:
            value = at(q, name, r)
            below = value - down(value)
            low, high = limited(value, below, up(below))
            upper.append(low)
            lower.append(down(high))
        flux = twice_flux(lower, upper, at(q, 7, r), 2)
        for n in range(5):
            put(gz, n, r, up(flux[n]) - flux[n])
        put(gz, 5, r, flux[5])
        put(gz, 6, r, flux[6])

    each_tile(1, W - 1, height_fluxes)

    quarter = 0.125 * TIME_STEP

    def edges(r):
        fx_z = at(gx, 6, r)
        fy_z = at(gy, 6, r)
        put(
            edge, 0, r, quarter * (at(gz, 6, r, -1) + at(gz, 6, r) - down(fy_z) - fy_z)
        )
        put(
            edge, 1, r, quarter * (down(fx_z) + fx_z - at(gz, 5, r, -W) - at(gz, 5, r))
        )
        put(
            edge,
            2,
            r,
            quarter * (at(gy, 5, r, -W) + at(gy, 5, r) - at(gx, 5, r, -1) - at(gx, 5, r)),
        )

    each_tile(2, W - 1, edges)

    def new_faces(r):
        ex, ey, ez = at(edge, 0, r), at(edge, 1, r), at(edge, 2, r)
        put(face, 0, r, at(q, 5, r) - (at(edge, 2, r, 1) - ez) + (up(ey) - ey))
        put(face, 1, r, at(q, 6, r) - (up(ex) - ex) + (at(edge, 2, r, W) - ez))
        put(face, 2, r, at(q, 7, r) - (at(edge, 1, r, W) - ey) + (at(edge, 0, r, 1) - ex))

    each_tile(2, W - 1, new_faces)

    def new_cells(r):
        density = at(q, 0, r)
        momentum = [density * at(q, 1 + c, r) for c in range(3)]
        twice_kinetic = (
            momentum[0] * at(q, 1, r) + momentum[1] * at(q, 2, r) + momentum[2] * at(q, 3, r)
        )
        field_sq = (
            at(q, 8, r) * at(q, 8, r) + at(q, 9, r) * at(q, 9, r) + at(q, 10, r) * at(q, 10, r)
        )
        energy = 1.5 * at(q, 4, r) + 0.5 * (twice_kinetic + field_sq)
        updated = []
        for n, value in enumerate([density] + momentum + [energy]):
            change = (at(gx, n, r, W) - at(gx, n, r)) + (at(gy, n, r, 1) - at(gy, n, r))
            updated.append(value - (0.5 * TIME_STEP) * (change + at(gz, n, r)))
        floored = jnp.maximum(updated[0], DENSITY_FLOOR)
        inverse = 1.0 / floored
        velocity = [updated[1 + c] * inverse for c in range(3)]
        bz = at(face, 2, r)
        field = [
            0.5 * (at(face, 0, r) + at(face, 0, r, W)),
            0.5 * (at(face, 1, r) + at(face, 1, r, 1)),
            0.5 * (bz + up(bz)),
        ]
        twice_kinetic = (
            updated[1] * velocity[0] + updated[2] * velocity[1] + updated[3] * velocity[2]
        )
        field_sq = field[0] * field[0] + field[1] * field[1] + field[2] * field[2]
        internal = updated[4] - 0.5 * (twice_kinetic + field_sq)
        pressure = jnp.maximum((GAMMA_RATIO - 1.0) * internal, PRESSURE_FLOOR)
        temperature = pressure * inverse
        put(cell, 0, r, floored)
        for c in range(3):
            put(cell, 1 + c, r, velocity[c])
            put(cell, 6 + c, r, field[c])
        put(cell, 4, r, inverse)
        put(cell, 5, r, temperature * temperature * jnp.sqrt(temperature))
        put(heat, 0, r, pressure)
        put(heat, 4, r, temperature)
        put(heat, 5, r, up(temperature) - down(temperature))

    each_tile(2, W - 2, new_cells)

    def couple(r):
        own_field = [at(cell, 6 + c, r) for c in range(3)]
        own_conduct = at(cell, 5, r)
        for d in range(3):
            if d < 2:
                offset = -W if d == 0 else -1
                beside = [at(cell, 6 + c, r, offset) for c in range(3)]
                conduct = at(cell, 5, r, offset)
            else:
                beside = [down(a) for a in own_field]
                conduct = down(own_conduct)
            normal = at(face, d, r)
            parts = [normal if c == d else 0.5 * (own_field[c] + beside[c]) for c in range(3)]
            size = parts[0] * parts[0] + parts[1] * parts[1] + parts[2] * parts[2]
            factor = 0.5 * (own_conduct + conduct) / jnp.maximum(size, FIELD_FLOOR) * normal
            mixed = 0.25 * factor
            for c in range(3):
                put(coupling, 3 * d + c, r, (factor if c == d else mixed) * parts[c])

    each_tile(3, W - 2, couple)

    def heat_fluxes(r):
        t = at(heat, 4, r)
        t_above_x = at(heat, 4, r, W)
        t_below_x = at(heat, 4, r, -W)
        t_above_y = at(heat, 4, r, 1)
        t_below_y = at(heat, 4, r, -1)
        along_x = t_above_x - t_below_x
        along_y = t_above_y - t_below_y
        along_z = at(heat, 5, r)
        beside_x = at(heat, 4, r, W - 1) - at(heat, 4, r, -W - 1)
        beside_y = at(heat, 4, r, 1 - W) - at(heat, 4, r, -1 - W)
        k = [at(coupling, n, r) for n in range(9)]
        qx = (
            k[0] * (t - t_below_x)
            + k[1] * (along_y + beside_y)
            + k[2] * (along_z + at(heat, 5, r, -W))
        )
        qy = (
            k[3] * (along_x + beside_x)
            + k[4] * (t - t_below_y)
            + k[5] * (along_z + at(heat, 5, r, -1))
        )
        qz = (
            k[6] * (along_x + down(along_x))
            + k[7] * (along_y + down(along_y))
            + k[8] * (t - down(t))
        )
        put(heat, 6, r, qx)
        put(heat, 7, r, qy)
        put(heat, 8, r, up(qz) - qz)

    def rate_at(r):
        return (
            (at(heat, 6, r, W) - at(heat, 6, r))
            + (at(heat, 7, r, 1) - at(heat, 7, r))
            + at(heat, 8, r)
        )

    b = [1.0 / 3.0] * 3 + [(j * j + j - 2.0) / (2.0 * j * (j + 1.0)) for j in range(3, SECTIONS + 1)]
    base_rate = 4.0 / (SUPER_SECTIONS * SUPER_SECTIONS + SUPER_SECTIONS - 2.0)
    scale = (GAMMA_RATIO - 1.0) * SUPER_TIME * base_rate

    def section(j, r):
        rate = rate_at(r)
        if j == 1:
            put(heat, 9, r, rate)
            return at(heat, 0, r) + (b[1] * scale) * rate
        mu = (2.0 * j - 1.0) / j * b[j] / b[j - 1]
        nu = -(j - 1.0) / j * b[j] / b[j - 2]
        if j == 2:
            base = (1.0 - mu) * at(heat, 0, r)
        else:
            base = nu * at(heat, j - 2, r) + (1.0 - mu - nu) * at(heat, 0, r)
        return (
            mu * at(heat, j - 1, r)
            + base
            + (mu * scale) * rate
            - ((1.0 - b[j - 1]) * mu * scale) * at(heat, 9, r)
        )

    for j in range(1, SECTIONS):
        each_tile(2 + j, W - 1 - j, heat_fluxes)

        def advance(r, j=j):
            pressure = section(j, r)
            put(heat, j, r, pressure)
            temperature = pressure * at(cell, 4, r)
            put(heat, 4, r, temperature)
            put(heat, 5, r, up(temperature) - down(temperature))

        each_tile(2 + j, W - 2 - j, advance)

    each_tile(2 + SECTIONS, W - 1 - SECTIONS, heat_fluxes)

    def finish(x, carry):
        r = PAD + (x + RIM) * W + RIM
        pressure_out[x] = section(SECTIONS, r)
        density_out[x] = at(cell, 0, r)
        for c in range(3):
            velocity_out[c, x] = at(cell, 1 + c, r)
            magnetic_out[c, x] = at(face, c, r)
        return carry

    lax.fori_loop(0, OWN, finish, 0)


def shift(a, axis, by):
    count = lax.axis_size(axis)
    return lax.ppermute(a, axis, [(i, (i + by) % count) for i in range(count)])


def local(mass_per_volume, velocity, thermal_stress, magnetic):
    f32 = jnp.float32
    shaped = functools.partial(jax.ShapeDtypeStruct, dtype=f32)
    own = (mass_per_volume, velocity, thermal_stress, magnetic)
    to_low, to_high = pl.pallas_call(
        pack_kernel, out_shape=(shaped((8, OWN * RIM, NZ)), shaped((8, OWN * RIM, NZ))), name="pack"
    )(*own)
    left = shift(to_high, "gy", 1)
    right = shift(to_low, "gy", -1)
    mid, to_low, to_high = pl.pallas_call(
        widen_kernel,
        out_shape=(shaped((8, MID, NZ)), shaped((8, SENT, NZ)), shaped((8, SENT, NZ))),
        name="widen",
    )(*own, left, right)
    before = shift(to_high, "gx", 1)
    after = shift(to_low, "gx", -1)

    def scratch(n):
        return pltpu.VMEM((n, ROWS, NZ), f32)

    block = (OWN, OWN, NZ)
    return pl.pallas_call(
        main_kernel,
        out_shape=(shaped(block), shaped((3, *block)), shaped(block), shaped((3, *block))),
        scratch_shapes=[scratch(n) for n in (11, 7, 7, 7, 7, 3, 3, 9, 9, 10)],
        compiler_params=pltpu.CompilerParams(vmem_limit_bytes=40 * 1024 * 1024),
        name="main",
    )(before, mid, after)


def solution(mesh):
    grid = P("gx", "gy", None)
    stacked = P(None, "gx", "gy", None)
    return jax.shard_map(
        local,
        mesh=mesh,
        in_specs=(grid, stacked, grid, stacked),
        out_specs=(grid, stacked, grid, stacked),
        check_vma=False,
    )
```

time: 149 us -> 109 us (0.73)
  the two profiles are of different devices: /device:TPU:159 before, /device:TPU:1 now
where the time goes in v1:
time: 109 us; the launch traced here: 108 us
  Pallas kernels  66.8 us (61%)
  starting transfers between devices  22 us (20%)
  waiting for transfers between devices  17 us (16%)
  local copies, waits for them, and re-layouts  1.77 us (2%)
    pallas_call x1, Pallas kernels, local(): pl.pallas_call(main_kernel, out_shape=(shaped(block), shaped((3, *block))...  62.6 us
    ppermute x4, starting transfers between devices, shift(): return lax.ppermute(a, axis, [(i, (i + by) % count) for i in range(count)])  22 us
    ppermute x4, waiting for transfers between devices, shift(): return lax.ppermute(a, axis, [(i, (i + by) % count) for i in range(count)])  17 us
    pallas_call x1, Pallas kernels, local(): pl.pallas_call(widen_kernel, out_shape=(shaped((8, MID, NZ)), shaped((8,...  2.44 us
  transfers between devices with their start and end apart: 4, of which 4 were waited for; matrix products, arithmetic and copies ran while one was open for 0% of the time, Pallas kernels for 0%

profile of v1, /device:TPU:1, one launch (start us, length us, event | category | flops | bytes accessed | tf_op | source)
XLA Modules:
  0.0 108.3 jit_solution(15040676421264699039)
XLA Ops:
  0.6 1.8 %pack.1 = (f32[8,48,128]{2,1,0:T(8,128)}, f32[8,48,128]{2,1,0:T(8,128)}) custom-call(f32[8,8,128]{2,1,0:T(8,128)} %mass_ref.3, f32[3,8,8,128]{3,2,1,0:T(8,128)} %velocity_ref.3, f32[8,8,128]{2,1,0:T(8,128)} %stress_ref.3, f32[3,8,8,128]{3,2,1,0:T(8,128)} %magnetic_ref.3), custom_call_target="tpu_custom_call" | custom-call | tf_op jit(solution)/shard_map/pack/pallas_call | solution.py:403
  2.4 5.5 %collective-permute-start = (f32[8,48,128]{2,1,0:T(8,128)}, f32[8,48,128]{2,1,0:T(8,128)S(1)}, u32[]{:S(2)}, u32[]{:S(2)}) collective-permute-start(f32[8,48,128]{2,1,0:T(8,128)} %get-tuple-element.9), channel_id=1, source_target_pairs={{0,1},{1,2},{2,3},{3,4},{4,5},{5,6},{6,7},{7,8},{8,9},{9,10},{10,1... | collective-permute-start | bytes 589832 | tf_op jit(solution)/shard_map/ppermute | solution.py:396
  7.9 10.4 %collective-permute-start.1 = (f32[8,48,128]{2,1,0:T(8,128)}, f32[8,48,128]{2,1,0:T(8,128)S(1)}, u32[]{:S(2)}, u32[]{:S(2)}) collective-permute-start(f32[8,48,128]{2,1,0:T(8,128)} %get-tuple-element.10), channel_id=1, source_target_pairs={{0,15},{1,0},{2,1},{3,2},{4,3},{5,4},{6,5},{7,6},{8,7},{9,8},{10,9... | collective-permute-start | bytes 589832 | tf_op jit(solution)/shard_map/ppermute | solution.py:396
  18.3 2.9 %collective-permute-done.left_ref = f32[8,48,128]{2,1,0:T(8,128)S(1)} collective-permute-done((f32[8,48,128]{2,1,0:T(8,128)}, f32[8,48,128]{2,1,0:T(8,128)S(1)}, u32[]{:S(2)}, u32[]{:S(2)}) %collective-permute-start) | collective-permute-done | bytes 196640 | tf_op jit(solution)/shard_map/ppermute | solution.py:396
  21.2 0.0 copy-start.1
  21.2 1.0 collective-permute-done.1.right_ref
  22.2 0.0 copy-done.1
  22.2 0.0 copy-start.2
  22.2 0.7 copy-done.2
  22.9 2.4 %widen.1 = (f32[8,160,128]{2,1,0:T(8,128)}, f32[8,120,128]{2,1,0:T(8,128)}, f32[8,120,128]{2,1,0:T(8,128)}) custom-call(f32[8,8,128]{2,1,0:T(8,128)} %mass_ref.3, f32[3,8,8,128]{3,2,1,0:T(8,128)} %velocity_ref.3, f32[8,8,128]{2,1,0:T(8,128)} %stress_ref.3, f32[3,8,8,128]{3,2,1,0:T(8,128)} %magnetic_ref.3, f32[8,48,128]{2,1,0:T(8,128)} %copy-done.1, ...), custom_call_target="tpu_custom_call" | custom-call | tf_op jit(solution)/shard_map/widen/pallas_call | solution.py:408
  25.3 3.6 %collective-permute-start.2 = (f32[8,120,128]{2,1,0:T(8,128)}, f32[8,120,128]{2,1,0:T(8,128)S(1)}, u32[]{:S(2)}, u32[]{:S(2)}) collective-permute-start(f32[8,120,128]{2,1,0:T(8,128)} %get-tuple-element.11), channel_id=1, source_target_pairs={{0,16},{16,32},{32,48},{48,64},{64,80},{80,96},{96,112},{112,128},... | collective-permute-start | bytes 1474568 | tf_op jit(solution)/shard_map/ppermute | solution.py:396
  28.9 2.5 %collective-permute-start.3 = (f32[8,120,128]{2,1,0:T(8,128)}, f32[8,120,128]{2,1,0:T(8,128)S(1)}, u32[]{:S(2)}, u32[]{:S(2)}) collective-permute-start(f32[8,120,128]{2,1,0:T(8,128)} %get-tuple-element.13), channel_id=1, source_target_pairs={{0,496},{16,0},{32,16},{48,32},{64,48},{80,64},{96,80},{112,96},{1... | collective-permute-start | bytes 1474568 | tf_op jit(solution)/shard_map/ppermute | solution.py:396
  31.4 3.6 %collective-permute-done.2.before_ref = f32[8,120,128]{2,1,0:T(8,128)S(1)} collective-permute-done((f32[8,120,128]{2,1,0:T(8,128)}, f32[8,120,128]{2,1,0:T(8,128)S(1)}, u32[]{:S(2)}, u32[]{:S(2)}) %collective-permute-start.2) | collective-permute-done | bytes 491552 | tf_op jit(solution)/shard_map/ppermute | solution.py:396
  35.0 9.6 %collective-permute-done.3.after_ref = f32[8,120,128]{2,1,0:T(8,128)S(1)} collective-permute-done((f32[8,120,128]{2,1,0:T(8,128)}, f32[8,120,128]{2,1,0:T(8,128)S(1)}, u32[]{:S(2)}, u32[]{:S(2)}) %collective-permute-start.3) | collective-permute-done | bytes 491552 | tf_op jit(solution)/shard_map/ppermute | solution.py:396
  44.6 0.0 copy-start
  44.6 1.1 %copy-done = f32[8,160,128]{2,1,0:T(8,128)S(1)} copy-done((f32[8,160,128]{2,1,0:T(8,128)S(1)}, f32[8,160,128]{2,1,0:T(8,128)}, u32[]{:S(2)}) %copy-start) | copy-done | bytes 655384
  45.7 62.6 %main.1 = (f32[8,8,128]{2,1,0:T(8,128)}, f32[3,8,8,128]{3,2,1,0:T(8,128)}, f32[8,8,128]{2,1,0:T(8,128)}, f32[3,8,8,128]{3,2,1,0:T(8,128)}) custom-call(f32[8,120,128]{2,1,0:T(8,128)S(1)} %collective-permute-done.2.before_ref, f32[8,160,128]{2,1,0:T(8,128)S(1)} %copy-done, f32[8,120,128]{2,1,0:T(8,128)S(1)} %collective-permute-done.3.after_ref), custom_call_target="tpu_custom_call" | custom-call | tf_op jit(solution)/shard_map/main/pallas_call | solution.py:420
Async XLA Ops:
  2.4 18.8 %collective-permute-start = (f32[8,48,128]{2,1,0:T(8,128)}, f32[8,48,128]{2,1,0:T(8,128)S(1)}, u32[]{:S(2)}, u32[]{:S(2)}) collective-permute-start(f32[8,48,128]{2,1,0:T(8,128)} %get-tuple-element.9), channel_id=1, source_target_pairs={{0,1},{1,2},{2,3},{3,4},{4,5},{5,6},{6,7},{7,8},{8,9},{9,10},{10,1... | collective-permute-start | bytes 589832 | tf_op jit(solution)/shard_map/ppermute | solution.py:396
  7.9 14.3 %collective-permute-start.1 = (f32[8,48,128]{2,1,0:T(8,128)}, f32[8,48,128]{2,1,0:T(8,128)S(1)}, u32[]{:S(2)}, u32[]{:S(2)}) collective-permute-start(f32[8,48,128]{2,1,0:T(8,128)} %get-tuple-element.10), channel_id=1, source_target_pairs={{0,15},{1,0},{2,1},{3,2},{4,3},{5,4},{6,5},{7,6},{8,7},{9,8},{10,9... | collective-permute-start | bytes 589832 | tf_op jit(solution)/shard_map/ppermute | solution.py:396
  21.2 1.0 copy-start.1
  22.2 0.7 copy-start.2
  25.3 9.7 %collective-permute-start.2 = (f32[8,120,128]{2,1,0:T(8,128)}, f32[8,120,128]{2,1,0:T(8,128)S(1)}, u32[]{:S(2)}, u32[]{:S(2)}) collective-permute-start(f32[8,120,128]{2,1,0:T(8,128)} %get-tuple-element.11), channel_id=1, source_target_pairs={{0,16},{16,32},{32,48},{48,64},{64,80},{80,96},{96,112},{112,128},... | collective-permute-start | bytes 1474568 | tf_op jit(solution)/shard_map/ppermute | solution.py:396
  28.9 15.6 %collective-permute-start.3 = (f32[8,120,128]{2,1,0:T(8,128)}, f32[8,120,128]{2,1,0:T(8,128)S(1)}, u32[]{:S(2)}, u32[]{:S(2)}) collective-permute-start(f32[8,120,128]{2,1,0:T(8,128)} %get-tuple-element.13), channel_id=1, source_target_pairs={{0,496},{16,0},{32,16},{48,32},{64,48},{80,64},{96,80},{112,96},{1... | collective-permute-start | bytes 1474568 | tf_op jit(solution)/shard_map/ppermute | solution.py:396
  44.6 1.1 %copy-start = (f32[8,160,128]{2,1,0:T(8,128)S(1)}, f32[8,160,128]{2,1,0:T(8,128)}, u32[]{:S(2)}) copy-start(f32[8,160,128]{2,1,0:T(8,128)} %get-tuple-element.12.mid_ref) | copy-start | bytes 1966084

commit v2 on v1

--- a/solution.py
+++ b/solution.py
@@ -21,9 +21,10 @@
 W = OWN + 2 * RIM
 NZ = 128
 PAD = 32
-ROWS = PAD + W * W + 48
+ROWS = PAD + W * W + 96
 SENT = RIM * W
 MID = OWN * W
+STATES, CELLS, COUPLE, FLOWS, ADVANCE = 184, 160, 152, 48, 184
 
 
 def split_fields(mass_ref, velocity_ref, stress_ref, magnetic_ref, x):
@@ -62,14 +63,13 @@
     return pltpu.roll(a, NZ - 1, 1)
 
 
-def down(a):
-    return pltpu.roll(a, 1, 1)
-
-
-def limited(value, below, above):
+def down(a, by=1):
+    return pltpu.roll(a, by, 1)
+
+
+def half_slope(below, above):
     slope = jnp.minimum(jnp.maximum(below, jnp.minimum(above, 0.0)), jnp.maximum(above, 0.0))
-    half = 0.5 * slope
-    return value - half, value + half
+    return 0.5 * slope
 
 
 def state_terms(state, field, d):
@@ -124,16 +124,12 @@
     return result
 
 
-def tiles(first, last):
+def each_block(first, last, rows, body):
     begin = first * W // 8 * 8
-    return begin, -(-(last * W - begin) // 8)
-
-
-def each_tile(first, last, body):
-    begin, count = tiles(first, last)
+    count = -(-(last * W - begin) // rows)
 
     def step(i, carry):
-        body(pl.multiple_of(PAD + begin + i * 8, 8))
+        body((pl.multiple_of(PAD + begin + i * rows, 8), rows))
         return carry
 
     lax.fori_loop(0, count, step, 0)
@@ -159,10 +155,10 @@
     heat,
 ):
     def at(ref, n, r, offset=0):
-        return ref[n, pl.ds(r + offset, 8), :]
+        return ref[n, pl.ds(r[0] + offset, r[1]), :]
 
     def put(ref, n, r, value):
-        ref[n, pl.ds(r, 8), :] = value
+        ref[n, pl.ds(r[0], r[1]), :] = value
 
     for n in range(8):
         q[n, PAD : PAD + SENT] = before_ref[n]
@@ -175,7 +171,7 @@
         bz = at(q, 7, r)
         put(q, 10, r, 0.5 * (bz + up(bz)))
 
-    each_tile(0, W, cell_fields)
+    each_block(0, W, 400, cell_fields)
 
     def side_fluxes(d, offset, target):
         names = list(range(5)) + [8 + c for c in range(3) if c != d]
@@ -184,35 +180,35 @@
             upper = []
             for n, name in enumerate(names):
                 value = at(q, name, r)
-                low, high = limited(
-                    value, value - at(q, name, r, -offset), at(q, name, r, offset) - value
-                )
-                upper.append(low)
-                put(hi, n, r, high)
+                half = half_slope(value - at(q, name, r, -offset), at(q, name, r, offset) - value)
+                upper.append(value - half)
+                put(hi, n, r, value + half)
             lower = [at(hi, n, r, -offset) for n in range(7)]
             for n, value in enumerate(twice_flux(lower, upper, at(q, 5 + d, r), d)):
                 put(target, n, r, value)
 
-        each_tile(1, W - 1, body)
+        each_block(1, W - 1, 16, body)
 
     side_fluxes(0, W, gx)
     side_fluxes(1, 1, gy)
 
+    def height_states(r):
+        for n, name in enumerate(list(range(5)) + [8, 9]):
+            value = at(q, name, r)
+            before, earlier, after = down(value), down(value, 2), up(value)
+            below = value - before
+            put(hi, n, r, value - half_slope(below, after - value))
+            put(hi, 7 + n, r, before + half_slope(before - earlier, below))
+
+    each_block(1, W - 1, STATES, height_states)
+
     def height_fluxes(r):
-        lower, upper = [], []
-        for name in list(range(5)) + [8, 9]:
-            value = at(q, name, r)
-            below = value - down(value)
-            low, high = limited(value, below, up(below))
-            upper.append(low)
-            lower.append(down(high))
-        flux = twice_flux(lower, upper, at(q, 7, r), 2)
-        for n in range(5):
-            put(gz, n, r, up(flux[n]) - flux[n])
-        put(gz, 5, r, flux[5])
-        put(gz, 6, r, flux[6])
-
-    each_tile(1, W - 1, height_fluxes)
+        upper = [at(hi, n, r) for n in range(7)]
+        lower = [at(hi, 7 + n, r) for n in range(7)]
+        for n, value in enumerate(twice_flux(lower, upper, at(q, 7, r), 2)):
+            put(gz, n, r, value)
+
+    each_block(1, W - 1, 16, height_fluxes)
 
     quarter = 0.125 * TIME_STEP
 
@@ -232,7 +228,7 @@
             quarter * (at(gy, 5, r, -W) + at(gy, 5, r) - at(gx, 5, r, -1) - at(gx, 5, r)),
         )
 
-    each_tile(2, W - 1, edges)
+    each_block(2, W - 1, 344, edges)
 
     def new_faces(r):
         ex, ey, ez = at(edge, 0, r), at(edge, 1, r), at(edge, 2, r)
@@ -240,7 +236,14 @@
         put(face, 1, r, at(q, 6, r) - (up(ex) - ex) + (at(edge, 2, r, W) - ez))
         put(face, 2, r, at(q, 7, r) - (at(edge, 1, r, W) - ey) + (at(edge, 0, r, 1) - ex))
 
-    each_tile(2, W - 1, new_faces)
+    each_block(2, W - 1, 344, new_faces)
+
+    def put_temperature(r, temperature):
+        above, below = up(temperature), down(temperature)
+        put(heat, 4, r, temperature)
+        put(heat, 5, r, temperature + below)
+        put(heat, 6, r, temperature - below)
+        put(heat, 7, r, above - below)
 
     def new_cells(r):
         density = at(q, 0, r)
@@ -255,7 +258,8 @@
         updated = []
         for n, value in enumerate([density] + momentum + [energy]):
             change = (at(gx, n, r, W) - at(gx, n, r)) + (at(gy, n, r, 1) - at(gy, n, r))
-            updated.append(value - (0.5 * TIME_STEP) * (change + at(gz, n, r)))
+            above = at(gz, n, r)
+            updated.append(value - (0.5 * TIME_STEP) * (change + (up(above) - above)))
         floored = jnp.maximum(updated[0], DENSITY_FLOOR)
         inverse = 1.0 / floored
         velocity = [updated[1 + c] * inverse for c in range(3)]
@@ -279,10 +283,9 @@
         put(cell, 4, r, inverse)
         put(cell, 5, r, temperature * temperature * jnp.sqrt(temperature))
         put(heat, 0, r, pressure)
-        put(heat, 4, r, temperature)
-        put(heat, 5, r, up(temperature) - down(temperature))
-
-    each_tile(2, W - 2, new_cells)
+        put_temperature(r, temperature)
+
+    each_block(2, W - 2, CELLS, new_cells)
 
     def couple(r):
         own_field = [at(cell, 6 + c, r) for c in range(3)]
@@ -303,44 +306,41 @@
             for c in range(3):
                 put(coupling, 3 * d + c, r, (factor if c == d else mixed) * parts[c])
 
-    each_tile(3, W - 2, couple)
+    each_block(3, W - 2, COUPLE, couple)
 
     def heat_fluxes(r):
         t = at(heat, 4, r)
-        t_above_x = at(heat, 4, r, W)
         t_below_x = at(heat, 4, r, -W)
-        t_above_y = at(heat, 4, r, 1)
         t_below_y = at(heat, 4, r, -1)
-        along_x = t_above_x - t_below_x
-        along_y = t_above_y - t_below_y
-        along_z = at(heat, 5, r)
+        along_x = at(heat, 4, r, W) - t_below_x
+        along_y = at(heat, 4, r, 1) - t_below_y
+        along_z = at(heat, 7, r)
         beside_x = at(heat, 4, r, W - 1) - at(heat, 4, r, -W - 1)
         beside_y = at(heat, 4, r, 1 - W) - at(heat, 4, r, -1 - W)
         k = [at(coupling, n, r) for n in range(9)]
         qx = (
             k[0] * (t - t_below_x)
             + k[1] * (along_y + beside_y)
-            + k[2] * (along_z + at(heat, 5, r, -W))
+            + k[2] * (along_z + at(heat, 7, r, -W))
         )
         qy = (
             k[3] * (along_x + beside_x)
             + k[4] * (t - t_below_y)
-            + k[5] * (along_z + at(heat, 5, r, -1))
+            + k[5] * (along_z + at(heat, 7, r, -1))
         )
         qz = (
-            k[6] * (along_x + down(along_x))
-            + k[7] * (along_y + down(along_y))
-            + k[8] * (t - down(t))
-        )
-        put(heat, 6, r, qx)
-        put(heat, 7, r, qy)
-        put(heat, 8, r, up(qz) - qz)
+            k[6] * (at(heat, 5, r, W) - at(heat, 5, r, -W))
+            + k[7] * (at(heat, 5, r, 1) - at(heat, 5, r, -1))
+            + k[8] * at(heat, 6, r)
+        )
+        put(heat, 8, r, qx)
+        put(heat, 9, r, qy)
+        put(heat, 10, r, qz)
 
     def rate_at(r):
+        qz = at(heat, 10, r)
         return (
-            (at(heat, 6, r, W) - at(heat, 6, r))
-            + (at(heat, 7, r, 1) - at(heat, 7, r))
-            + at(heat, 8, r)
+            (at(heat, 8, r, W) - at(heat, 8, r)) + (at(heat, 9, r, 1) - at(heat, 9, r)) + (up(qz) - qz)
         )
 
     b = [1.0 / 3.0] * 3 + [(j * j + j - 2.0) / (2.0 * j * (j + 1.0)) for j in range(3, SECTIONS + 1)]
@@ -350,7 +350,7 @@
     def section(j, r):
         rate = rate_at(r)
         if j == 1:
-            put(heat, 9, r, rate)
+            put(heat, 11, r, rate)
             return at(heat, 0, r) + (b[1] * scale) * rate
         mu = (2.0 * j - 1.0) / j * b[j] / b[j - 1]
         nu = -(j - 1.0) / j * b[j] / b[j - 2]
@@ -362,33 +362,44 @@
             mu * at(heat, j - 1, r)
             + base
             + (mu * scale) * rate
-            - ((1.0 - b[j - 1]) * mu * scale) * at(heat, 9, r)
+            - ((1.0 - b[j - 1]) * mu * scale) * at(heat, 11, r)
         )
 
     for j in range(1, SECTIONS):
-        each_tile(2 + j, W - 1 - j, heat_fluxes)
+        each_block(2 + j, W - 1 - j, FLOWS, heat_fluxes)
 
         def advance(r, j=j):
             pressure = section(j, r)
             put(heat, j, r, pressure)
-            temperature = pressure * at(cell, 4, r)
-            put(heat, 4, r, temperature)
-            put(heat, 5, r, up(temperature) - down(temperature))
-
-        each_tile(2 + j, W - 2 - j, advance)
-
-    each_tile(2 + SECTIONS, W - 1 - SECTIONS, heat_fluxes)
-
-    def finish(x, carry):
-        r = PAD + (x + RIM) * W + RIM
+            put_temperature(r, pressure * at(cell, 4, r))
+
+        each_block(2 + j, W - 2 - j, ADVANCE, advance)
+
+    each_block(2 + SECTIONS, W - 1 - SECTIONS, FLOWS, heat_fluxes)
+
+    for x in range(OWN):
+        r = (PAD + (x + RIM) * W + RIM, OWN)
         pressure_out[x] = section(SECTIONS, r)
         density_out[x] = at(cell, 0, r)
         for c in range(3):
             velocity_out[c, x] = at(cell, 1 + c, r)
             magnetic_out[c, x] = at(face, c, r)
-        return carry
-
-    lax.fori_loop(0, OWN, finish, 0)
+
+
+def main_call(before, mid, after, kernel=main_kernel, name="main"):
+    def shaped(*shape):
+        return jax.ShapeDtypeStruct(shape, jnp.float32)
+
+    block = (OWN, OWN, NZ)
+    return pl.pallas_call(
+        kernel,
+        out_shape=(shaped(*block), shaped(3, *block), shaped(*block), shaped(3, *block)),
+        scratch_shapes=[
+            pltpu.VMEM((n, ROWS, NZ), jnp.float32) for n in (11, 14, 7, 7, 7, 3, 3, 9, 9, 12)
+        ],
+        compiler_params=pltpu.CompilerParams(vmem_limit_bytes=40 * 1024 * 1024),
+        name=name,
+    )(before, mid, after)
 
 
 def shift(a, axis, by):
@@ -413,17 +424,7 @@
     before = shift(to_high, "gx", 1)
     after = shift(to_low, "gx", -1)
 
-    def scratch(n):
-        return pltpu.VMEM((n, ROWS, NZ), f32)
-
-    block = (OWN, OWN, NZ)
-    return pl.pallas_call(
-        main_kernel,
-        out_shape=(shaped(block), shaped((3, *block)), shaped(block), shaped((3, *block))),
-        scratch_shapes=[scratch(n) for n in (11, 7, 7, 7, 7, 3, 3, 9, 9, 10)],
-        compiler_params=pltpu.CompilerParams(vmem_limit_bytes=40 * 1024 * 1024),
-        name="main",
-    )(before, mid, after)
+    return main_call(before, mid, after)
 
 
 def solution(mesh):

time: 109 us -> 55.2 us (0.51)
  Pallas kernels: 66.8 us -> 13.5 us
    pallas_call x1, Pallas kernels: 62.6 us -> 9.28 us  [main_call(): pl.pallas_call(kernel, out_shape=(shaped(*block), shaped(3, *block), shap...]
where the time goes in v2:
time: 55.2 us; the launch traced here: 54.9 us
  starting transfers between devices  22 us (40%)
  waiting for transfers between devices  17 us (31%)
  Pallas kernels  13.5 us (24%)
  local copies, waits for them, and re-layouts  1.77 us (3%)
  between operations  0.67 us (1%)
    ppermute x4, starting transfers between devices, shift(): return lax.ppermute(a, axis, [(i, (i + by) % count) for i in range(count)])  22 us
    ppermute x4, waiting for transfers between devices, shift(): return lax.ppermute(a, axis, [(i, (i + by) % count) for i in range(count)])  17 us
    pallas_call x1, Pallas kernels, main_call(): pl.pallas_call(kernel, out_shape=(shaped(*block), shaped(3, *block), shap...  9.28 us
    pallas_call x1, Pallas kernels, local(): pl.pallas_call(widen_kernel, out_shape=(shaped((8, MID, NZ)), shaped((8,...  2.44 us
    unnamed x6, local copies, waits for them, and re-layouts  1.77 us
    pallas_call x1, Pallas kernels, local(): pl.pallas_call(pack_kernel, out_shape=(shaped((8, OWN * RIM, NZ)), shaped...  1.76 us
  transfers between devices with their start and end apart: 4, of which 4 were waited for; matrix products, arithmetic and copies ran while one was open for 0% of the time, Pallas kernels for 0%

profile of v2, /device:TPU:1, one launch (start us, length us, event | category | flops | bytes accessed | tf_op | source)
XLA Modules:
  0.0 54.9 jit_solution(18259063952523511389)
XLA Ops:
  0.6 1.8 %pack.1 = (f32[8,48,128]{2,1,0:T(8,128)}, f32[8,48,128]{2,1,0:T(8,128)}) custom-call(f32[8,8,128]{2,1,0:T(8,128)} %mass_ref.3, f32[3,8,8,128]{3,2,1,0:T(8,128)} %velocity_ref.3, f32[8,8,128]{2,1,0:T(8,128)} %stress_ref.3, f32[3,8,8,128]{3,2,1,0:T(8,128)} %magnetic_ref.3), custom_call_target="tpu_custom_call" | custom-call | tf_op jit(solution)/shard_map/pack/pallas_call | solution.py:414
  2.4 5.5 %collective-permute-start = (f32[8,48,128]{2,1,0:T(8,128)}, f32[8,48,128]{2,1,0:T(8,128)S(1)}, u32[]{:S(2)}, u32[]{:S(2)}) collective-permute-start(f32[8,48,128]{2,1,0:T(8,128)} %get-tuple-element.9), channel_id=1, source_target_pairs={{0,1},{1,2},{2,3},{3,4},{4,5},{5,6},{6,7},{7,8},{8,9},{9,10},{10,1... | collective-permute-start | bytes 589832 | tf_op jit(solution)/shard_map/ppermute | solution.py:407
  7.9 10.4 %collective-permute-start.1 = (f32[8,48,128]{2,1,0:T(8,128)}, f32[8,48,128]{2,1,0:T(8,128)S(1)}, u32[]{:S(2)}, u32[]{:S(2)}) collective-permute-start(f32[8,48,128]{2,1,0:T(8,128)} %get-tuple-element.10), channel_id=1, source_target_pairs={{0,15},{1,0},{2,1},{3,2},{4,3},{5,4},{6,5},{7,6},{8,7},{9,8},{10,9... | collective-permute-start | bytes 589832 | tf_op jit(solution)/shard_map/ppermute | solution.py:407
  18.3 2.9 %collective-permute-done.left_ref = f32[8,48,128]{2,1,0:T(8,128)S(1)} collective-permute-done((f32[8,48,128]{2,1,0:T(8,128)}, f32[8,48,128]{2,1,0:T(8,128)S(1)}, u32[]{:S(2)}, u32[]{:S(2)}) %collective-permute-start) | collective-permute-done | bytes 196640 | tf_op jit(solution)/shard_map/ppermute | solution.py:407
  21.2 0.0 copy-start.1
  21.2 1.0 %collective-permute-done.1.right_ref = f32[8,48,128]{2,1,0:T(8,128)S(1)} collective-permute-done((f32[8,48,128]{2,1,0:T(8,128)}, f32[8,48,128]{2,1,0:T(8,128)S(1)}, u32[]{:S(2)}, u32[]{:S(2)}) %collective-permute-start.1) | collective-permute-done | bytes 196640 | tf_op jit(solution)/shard_map/ppermute | solution.py:407
  22.2 0.0 copy-done.1
  22.2 0.0 copy-start.2
  22.2 0.7 %copy-done.2 = f32[8,48,128]{2,1,0:T(8,128)} copy-done((f32[8,48,128]{2,1,0:T(8,128)}, f32[8,48,128]{2,1,0:T(8,128)S(1)}, u32[]{:S(2)}) %copy-start.2) | copy-done | bytes 196632
  22.9 2.4 %widen.1 = (f32[8,160,128]{2,1,0:T(8,128)}, f32[8,120,128]{2,1,0:T(8,128)}, f32[8,120,128]{2,1,0:T(8,128)}) custom-call(f32[8,8,128]{2,1,0:T(8,128)} %mass_ref.3, f32[3,8,8,128]{3,2,1,0:T(8,128)} %velocity_ref.3, f32[8,8,128]{2,1,0:T(8,128)} %stress_ref.3, f32[3,8,8,128]{3,2,1,0:T(8,128)} %magnetic_ref.3, f32[8,48,128]{2,1,0:T(8,128)} %copy-done.1, ...), custom_call_target="tpu_custom_call" | custom-call | tf_op jit(solution)/shard_map/widen/pallas_call | solution.py:419
  25.3 3.6 %collective-permute-start.2 = (f32[8,120,128]{2,1,0:T(8,128)}, f32[8,120,128]{2,1,0:T(8,128)S(1)}, u32[]{:S(2)}, u32[]{:S(2)}) collective-permute-start(f32[8,120,128]{2,1,0:T(8,128)} %get-tuple-element.11), channel_id=1, source_target_pairs={{0,16},{16,32},{32,48},{48,64},{64,80},{80,96},{96,112},{112,128},... | collective-permute-start | bytes 1474568 | tf_op jit(solution)/shard_map/ppermute | solution.py:407
  28.9 2.5 %collective-permute-start.3 = (f32[8,120,128]{2,1,0:T(8,128)}, f32[8,120,128]{2,1,0:T(8,128)S(1)}, u32[]{:S(2)}, u32[]{:S(2)}) collective-permute-start(f32[8,120,128]{2,1,0:T(8,128)} %get-tuple-element.13), channel_id=1, source_target_pairs={{0,496},{16,0},{32,16},{48,32},{64,48},{80,64},{96,80},{112,96},{1... | collective-permute-start | bytes 1474568 | tf_op jit(solution)/shard_map/ppermute | solution.py:407
  31.4 3.6 %collective-permute-done.2.before_ref = f32[8,120,128]{2,1,0:T(8,128)S(1)} collective-permute-done((f32[8,120,128]{2,1,0:T(8,128)}, f32[8,120,128]{2,1,0:T(8,128)S(1)}, u32[]{:S(2)}, u32[]{:S(2)}) %collective-permute-start.2) | collective-permute-done | bytes 491552 | tf_op jit(solution)/shard_map/ppermute | solution.py:407
  35.0 9.6 %collective-permute-done.3.after_ref = f32[8,120,128]{2,1,0:T(8,128)S(1)} collective-permute-done((f32[8,120,128]{2,1,0:T(8,128)}, f32[8,120,128]{2,1,0:T(8,128)S(1)}, u32[]{:S(2)}, u32[]{:S(2)}) %collective-permute-start.3) | collective-permute-done | bytes 491552 | tf_op jit(solution)/shard_map/ppermute | solution.py:407
  44.6 0.0 copy-start
  44.6 1.1 %copy-done = f32[8,160,128]{2,1,0:T(8,128)S(1)} copy-done((f32[8,160,128]{2,1,0:T(8,128)S(1)}, f32[8,160,128]{2,1,0:T(8,128)}, u32[]{:S(2)}) %copy-start) | copy-done | bytes 655384
  45.7 9.3 %main.1 = (f32[8,8,128]{2,1,0:T(8,128)}, f32[3,8,8,128]{3,2,1,0:T(8,128)}, f32[8,8,128]{2,1,0:T(8,128)}, f32[3,8,8,128]{3,2,1,0:T(8,128)}) custom-call(f32[8,120,128]{2,1,0:T(8,128)S(1)} %collective-permute-done.2.before_ref, f32[8,160,128]{2,1,0:T(8,128)S(1)} %copy-done, f32[8,120,128]{2,1,0:T(8,128)S(1)} %collective-permute-done.3.after_ref), custom_call_target="tpu_custom_call" | custom-call | tf_op jit(solution)/shard_map/main/pallas_call | solution.py:394
Async XLA Ops:
  2.4 18.8 %collective-permute-start = (f32[8,48,128]{2,1,0:T(8,128)}, f32[8,48,128]{2,1,0:T(8,128)S(1)}, u32[]{:S(2)}, u32[]{:S(2)}) collective-permute-start(f32[8,48,128]{2,1,0:T(8,128)} %get-tuple-element.9), channel_id=1, source_target_pairs={{0,1},{1,2},{2,3},{3,4},{4,5},{5,6},{6,7},{7,8},{8,9},{9,10},{10,1... | collective-permute-start | bytes 589832 | tf_op jit(solution)/shard_map/ppermute | solution.py:407
  7.9 14.3 %collective-permute-start.1 = (f32[8,48,128]{2,1,0:T(8,128)}, f32[8,48,128]{2,1,0:T(8,128)S(1)}, u32[]{:S(2)}, u32[]{:S(2)}) collective-permute-start(f32[8,48,128]{2,1,0:T(8,128)} %get-tuple-element.10), channel_id=1, source_target_pairs={{0,15},{1,0},{2,1},{3,2},{4,3},{5,4},{6,5},{7,6},{8,7},{9,8},{10,9... | collective-permute-start | bytes 589832 | tf_op jit(solution)/shard_map/ppermute | solution.py:407
  21.2 1.0 %copy-start.1 = (f32[8,48,128]{2,1,0:T(8,128)}, f32[8,48,128]{2,1,0:T(8,128)S(1)}, u32[]{:S(2)}) copy-start(f32[8,48,128]{2,1,0:T(8,128)S(1)} %collective-permute-done.left_ref) | copy-start | bytes 589828
  22.2 0.7 %copy-start.2 = (f32[8,48,128]{2,1,0:T(8,128)}, f32[8,48,128]{2,1,0:T(8,128)S(1)}, u32[]{:S(2)}) copy-start(f32[8,48,128]{2,1,0:T(8,128)S(1)} %collective-permute-done.1.right_ref) | copy-start | bytes 589828
  25.3 9.7 %collective-permute-start.2 = (f32[8,120,128]{2,1,0:T(8,128)}, f32[8,120,128]{2,1,0:T(8,128)S(1)}, u32[]{:S(2)}, u32[]{:S(2)}) collective-permute-start(f32[8,120,128]{2,1,0:T(8,128)} %get-tuple-element.11), channel_id=1, source_target_pairs={{0,16},{16,32},{32,48},{48,64},{64,80},{80,96},{96,112},{112,128},... | collective-permute-start | bytes 1474568 | tf_op jit(solution)/shard_map/ppermute | solution.py:407
  28.9 15.6 %collective-permute-start.3 = (f32[8,120,128]{2,1,0:T(8,128)}, f32[8,120,128]{2,1,0:T(8,128)S(1)}, u32[]{:S(2)}, u32[]{:S(2)}) collective-permute-start(f32[8,120,128]{2,1,0:T(8,128)} %get-tuple-element.13), channel_id=1, source_target_pairs={{0,496},{16,0},{32,16},{48,32},{64,48},{80,64},{96,80},{112,96},{1... | collective-permute-start | bytes 1474568 | tf_op jit(solution)/shard_map/ppermute | solution.py:407
  44.6 1.1 %copy-start = (f32[8,160,128]{2,1,0:T(8,128)S(1)}, f32[8,160,128]{2,1,0:T(8,128)}, u32[]{:S(2)}) copy-start(f32[8,160,128]{2,1,0:T(8,128)} %get-tuple-element.12.mid_ref) | copy-start | bytes 1966084

commit v3 on v2

--- a/solution.py
+++ b/solution.py
@@ -1,5 +1,3 @@
-import functools
-
 import jax
 import jax.numpy as jnp
 from jax import lax
@@ -27,32 +25,27 @@
 STATES, CELLS, COUPLE, FLOWS, ADVANCE = 184, 160, 152, 48, 184
 
 
-def split_fields(mass_ref, velocity_ref, stress_ref, magnetic_ref, x):
-    fields = [mass_ref[x]] + [velocity_ref[c, x] for c in range(3)]
-    return fields + [stress_ref[x]] + [magnetic_ref[c, x] for c in range(3)]
-
-
-def pack_kernel(mass_ref, velocity_ref, stress_ref, magnetic_ref, low_ref, high_ref):
+def pack_kernel(mass_ref, velocity_ref, stress_ref, magnetic_ref, own_ref, low_ref, high_ref):
     for x in range(OWN):
-        fields = split_fields(mass_ref, velocity_ref, stress_ref, magnetic_ref, x)
+        fields = [mass_ref[x]] + [velocity_ref[c, x] for c in range(3)]
+        fields += [stress_ref[x]] + [magnetic_ref[c, x] for c in range(3)]
         for n, value in enumerate(fields):
+            own_ref[n, OWN * x : OWN * (x + 1)] = value
             low_ref[n, RIM * x : RIM * (x + 1)] = value[:RIM]
             high_ref[n, RIM * x : RIM * (x + 1)] = value[OWN - RIM :]
 
 
-def widen_kernel(
-    mass_ref, velocity_ref, stress_ref, magnetic_ref, left_ref, right_ref, mid_ref, low_ref, high_ref
-):
+def widen_kernel(own_ref, left_ref, right_ref, mid_ref, low_ref, high_ref):
     for x in range(OWN):
-        fields = split_fields(mass_ref, velocity_ref, stress_ref, magnetic_ref, x)
-        for n, value in enumerate(fields):
+        targets = [(mid_ref, x * W)]
+        if x < RIM:
+            targets.append((low_ref, x * W))
+        if x >= OWN - RIM:
+            targets.append((high_ref, (x - OWN + RIM) * W))
+        for n in range(8):
             left = left_ref[n, RIM * x : RIM * (x + 1)]
+            value = own_ref[n, OWN * x : OWN * (x + 1)]
             right = right_ref[n, RIM * x : RIM * (x + 1)]
-            targets = [(mid_ref, x * W)]
-            if x < RIM:
-                targets.append((low_ref, x * W))
-            if x >= OWN - RIM:
-                targets.append((high_ref, (x - OWN + RIM) * W))
             for ref, at in targets:
                 ref[n, at : at + RIM] = left
                 ref[n, at + RIM : at + RIM + OWN] = value
@@ -402,28 +395,36 @@
     )(before, mid, after)
 
 
+def in_vmem(kernel, name, arguments, *shapes):
+    spec = pl.BlockSpec(memory_space=pltpu.VMEM)
+    results = pl.pallas_call(
+        kernel,
+        in_specs=[spec] * len(arguments),
+        out_specs=[spec] * len(shapes),
+        out_shape=[pltpu.VMEM(shape, jnp.float32) for shape in shapes],
+        name=name,
+    )(*arguments)
+    return [pltpu.with_memory_space_constraint(a, pltpu.VMEM) for a in results]
+
+
 def shift(a, axis, by):
     count = lax.axis_size(axis)
-    return lax.ppermute(a, axis, [(i, (i + by) % count) for i in range(count)])
-
-
-def local(mass_per_volume, velocity, thermal_stress, magnetic):
-    f32 = jnp.float32
-    shaped = functools.partial(jax.ShapeDtypeStruct, dtype=f32)
-    own = (mass_per_volume, velocity, thermal_stress, magnetic)
-    to_low, to_high = pl.pallas_call(
-        pack_kernel, out_shape=(shaped((8, OWN * RIM, NZ)), shaped((8, OWN * RIM, NZ))), name="pack"
-    )(*own)
+    moved = lax.ppermute(a, axis, [(i, (i + by) % count) for i in range(count)])
+    return pltpu.with_memory_space_constraint(moved, pltpu.VMEM)
+
+
+def local(*arguments):
+    packed, sent = (8, OWN * RIM, NZ), (8, SENT, NZ)
+    own, to_low, to_high = in_vmem(
+        pack_kernel, "pack", arguments, (8, OWN * OWN, NZ), packed, packed
+    )
     left = shift(to_high, "gy", 1)
     right = shift(to_low, "gy", -1)
-    mid, to_low, to_high = pl.pallas_call(
-        widen_kernel,
-        out_shape=(shaped((8, MID, NZ)), shaped((8, SENT, NZ)), shaped((8, SENT, NZ))),
-        name="widen",
-    )(*own, left, right)
+    mid, to_low, to_high = in_vmem(
+        widen_kernel, "widen", (own, left, right), (8, MID, NZ), sent, sent
+    )
     before = shift(to_high, "gx", 1)
     after = shift(to_low, "gx", -1)
-
     return main_call(before, mid, after)
 
 

time: 55.2 us -> 49.9 us (0.904)
  Pallas kernels: 13.5 us -> 10.4 us
  local copies, waits for them, and re-layouts: 1.77 us -> 0 us
  waiting for transfers between devices: 17 us -> 16.4 us
    pallas_call x2, Pallas kernels: 4.19 us -> 1.16 us  [in_vmem(): pl.pallas_call(kernel, in_specs=[spec] * len(arguments), out_specs=[spec]...]
    unnamed x6 -> x0, local copies, waits for them, and re-layouts: 1.77 us -> none
    ppermute x4, waiting for transfers between devices: 17 us -> 16.4 us  [shift(): moved = lax.ppermute(a, axis, [(i, (i + by) % count) for i in range(count)])]
where the time goes in v3:
time: 49.9 us; the launch traced here: 49.7 us
  starting transfers between devices  22.1 us (44%)
  waiting for transfers between devices  16.4 us (33%)
  Pallas kernels  10.4 us (21%)
  between operations  0.68 us (1%)
    ppermute x4, starting transfers between devices, shift(): moved = lax.ppermute(a, axis, [(i, (i + by) % count) for i in range(count)])  22.1 us
    ppermute x4, waiting for transfers between devices, shift(): moved = lax.ppermute(a, axis, [(i, (i + by) % count) for i in range(count)])  16.4 us
    pallas_call x1, Pallas kernels, main_call(): pl.pallas_call(kernel, out_shape=(shaped(*block), shaped(3, *block), shap...  9.28 us
    pallas_call x2, Pallas kernels, in_vmem(): pl.pallas_call(kernel, in_specs=[spec] * len(arguments), out_specs=[spec]...  1.16 us
  transfers between devices with their start and end apart: 4, of which 4 were waited for; matrix products, arithmetic and copies ran while one was open for 0% of the time, Pallas kernels for 0%

profile of v3, /device:TPU:1, one launch (start us, length us, event | category | flops | bytes accessed | tf_op | source)
XLA Modules:
  0.0 49.7 jit_solution(15310857661340025812)
XLA Ops:
  0.6 1.0 %pack.1 = (f32[8,64,128]{2,1,0:T(8,128)S(1)}, f32[8,48,128]{2,1,0:T(8,128)S(1)}, f32[8,48,128]{2,1,0:T(8,128)S(1)}) custom-call(f32[8,8,128]{2,1,0:T(8,128)} %mass_ref.1, f32[3,8,8,128]{3,2,1,0:T(8,128)} %velocity_ref.1, f32[8,8,128]{2,1,0:T(8,128)} %stress_ref.1, f32[3,8,8,128]{3,2,1,0:T(8,128)} %magnetic_ref.1), custom_call_target="tpu_custom_call" | custom-call | tf_op jit(solution)/shard_map/pack/pallas_call | solution.py:400
  1.7 5.5 %collective-permute-start = (f32[8,48,128]{2,1,0:T(8,128)S(1)}, f32[8,48,128]{2,1,0:T(8,128)S(1)}, u32[]{:S(2)}, u32[]{:S(2)}) collective-permute-start(f32[8,48,128]{2,1,0:T(8,128)S(1)} %get-tuple-element.11), channel_id=1, source_target_pairs={{0,1},{1,2},{2,3},{3,4},{4,5},{5,6},{6,7},{7,8},{8,9},{9,10},{10,1... | collective-permute-start | bytes 589832 | tf_op jit(solution)/shard_map/ppermute | solution.py:412
  7.2 10.4 %collective-permute-start.1 = (f32[8,48,128]{2,1,0:T(8,128)S(1)}, f32[8,48,128]{2,1,0:T(8,128)S(1)}, u32[]{:S(2)}, u32[]{:S(2)}) collective-permute-start(f32[8,48,128]{2,1,0:T(8,128)S(1)} %get-tuple-element.12), channel_id=1, source_target_pairs={{0,15},{1,0},{2,1},{3,2},{4,3},{5,4},{6,5},{7,6},{8,7},{9,8},{10,9... | collective-permute-start | bytes 589832 | tf_op jit(solution)/shard_map/ppermute | solution.py:412
  17.6 2.7 %collective-permute-done.left_ref = f32[8,48,128]{2,1,0:T(8,128)S(1)} collective-permute-done((f32[8,48,128]{2,1,0:T(8,128)S(1)}, f32[8,48,128]{2,1,0:T(8,128)S(1)}, u32[]{:S(2)}, u32[]{:S(2)}) %collective-permute-start) | collective-permute-done | bytes 196640 | tf_op jit(solution)/shard_map/ppermute | solution.py:412
  20.3 0.9 %collective-permute-done.1.right_ref = f32[8,48,128]{2,1,0:T(8,128)S(1)} collective-permute-done((f32[8,48,128]{2,1,0:T(8,128)S(1)}, f32[8,48,128]{2,1,0:T(8,128)S(1)}, u32[]{:S(2)}, u32[]{:S(2)}) %collective-permute-start.1) | collective-permute-done | bytes 196640 | tf_op jit(solution)/shard_map/ppermute | solution.py:412
  21.2 0.1 widen.1
  21.3 3.7 %collective-permute-start.2 = (f32[8,120,128]{2,1,0:T(8,128)S(1)}, f32[8,120,128]{2,1,0:T(8,128)S(1)}, u32[]{:S(2)}, u32[]{:S(2)}) collective-permute-start(f32[8,120,128]{2,1,0:T(8,128)S(1)} %get-tuple-element.13), channel_id=1, source_target_pairs={{0,16},{16,32},{32,48},{48,64},{64,80},{80,96},{96,112},{112,128},... | collective-permute-start | bytes 1474568 | tf_op jit(solution)/shard_map/ppermute | solution.py:412
  25.0 2.6 %collective-permute-start.3 = (f32[8,120,128]{2,1,0:T(8,128)S(1)}, f32[8,120,128]{2,1,0:T(8,128)S(1)}, u32[]{:S(2)}, u32[]{:S(2)}) collective-permute-start(f32[8,120,128]{2,1,0:T(8,128)S(1)} %get-tuple-element.15), channel_id=1, source_target_pairs={{0,496},{16,0},{32,16},{48,32},{64,48},{80,64},{96,80},{112,96},{1... | collective-permute-start | bytes 1474568 | tf_op jit(solution)/shard_map/ppermute | solution.py:412
  27.6 3.1 %collective-permute-done.2.before_ref = f32[8,120,128]{2,1,0:T(8,128)S(1)} collective-permute-done((f32[8,120,128]{2,1,0:T(8,128)S(1)}, f32[8,120,128]{2,1,0:T(8,128)S(1)}, u32[]{:S(2)}, u32[]{:S(2)}) %collective-permute-start.2) | collective-permute-done | bytes 491552 | tf_op jit(solution)/shard_map/ppermute | solution.py:412
  30.7 9.7 %collective-permute-done.3.after_ref = f32[8,120,128]{2,1,0:T(8,128)S(1)} collective-permute-done((f32[8,120,128]{2,1,0:T(8,128)S(1)}, f32[8,120,128]{2,1,0:T(8,128)S(1)}, u32[]{:S(2)}, u32[]{:S(2)}) %collective-permute-start.3) | collective-permute-done | bytes 491552 | tf_op jit(solution)/shard_map/ppermute | solution.py:412
  40.4 9.3 %main.1 = (f32[8,8,128]{2,1,0:T(8,128)}, f32[3,8,8,128]{3,2,1,0:T(8,128)}, f32[8,8,128]{2,1,0:T(8,128)}, f32[3,8,8,128]{3,2,1,0:T(8,128)}) custom-call(f32[8,120,128]{2,1,0:T(8,128)S(1)} %collective-permute-done.2.before_ref, f32[8,160,128]{2,1,0:T(8,128)S(1)} %get-tuple-element.14.mid_ref, f32[8,120,128]{2,1,0:T(8,128)S(1)} %collective-permute-done.3.after_ref), custom_call_target="tpu_custom_call" | custom-call | tf_op jit(solution)/shard_map/main/pallas_call | solution.py:387
Async XLA Ops:
  1.7 18.6 %collective-permute-start = (f32[8,48,128]{2,1,0:T(8,128)S(1)}, f32[8,48,128]{2,1,0:T(8,128)S(1)}, u32[]{:S(2)}, u32[]{:S(2)}) collective-permute-start(f32[8,48,128]{2,1,0:T(8,128)S(1)} %get-tuple-element.11), channel_id=1, source_target_pairs={{0,1},{1,2},{2,3},{3,4},{4,5},{5,6},{6,7},{7,8},{8,9},{9,10},{10,1... | collective-permute-start | bytes 589832 | tf_op jit(solution)/shard_map/ppermute | solution.py:412
  7.2 14.0 %collective-permute-start.1 = (f32[8,48,128]{2,1,0:T(8,128)S(1)}, f32[8,48,128]{2,1,0:T(8,128)S(1)}, u32[]{:S(2)}, u32[]{:S(2)}) collective-permute-start(f32[8,48,128]{2,1,0:T(8,128)S(1)} %get-tuple-element.12), channel_id=1, source_target_pairs={{0,15},{1,0},{2,1},{3,2},{4,3},{5,4},{6,5},{7,6},{8,7},{9,8},{10,9... | collective-permute-start | bytes 589832 | tf_op jit(solution)/shard_map/ppermute | solution.py:412
  21.3 9.4 %collective-permute-start.2 = (f32[8,120,128]{2,1,0:T(8,128)S(1)}, f32[8,120,128]{2,1,0:T(8,128)S(1)}, u32[]{:S(2)}, u32[]{:S(2)}) collective-permute-start(f32[8,120,128]{2,1,0:T(8,128)S(1)} %get-tuple-element.13), channel_id=1, source_target_pairs={{0,16},{16,32},{32,48},{48,64},{64,80},{80,96},{96,112},{112,128},... | collective-permute-start | bytes 1474568 | tf_op jit(solution)/shard_map/ppermute | solution.py:412
  25.0 15.4 %collective-permute-start.3 = (f32[8,120,128]{2,1,0:T(8,128)S(1)}, f32[8,120,128]{2,1,0:T(8,128)S(1)}, u32[]{:S(2)}, u32[]{:S(2)}) collective-permute-start(f32[8,120,128]{2,1,0:T(8,128)S(1)} %get-tuple-element.15), channel_id=1, source_target_pairs={{0,496},{16,0},{32,16},{48,32},{64,48},{80,64},{96,80},{112,96},{1... | collective-permute-start | bytes 1474568 | tf_op jit(solution)/shard_map/ppermute | solution.py:412

commit v4 on v3

--- a/solution.py
+++ b/solution.py
@@ -22,34 +22,38 @@
 ROWS = PAD + W * W + 96
 SENT = RIM * W
 MID = OWN * W
-STATES, CELLS, COUPLE, FLOWS, ADVANCE = 184, 160, 152, 48, 184
-
-
-def pack_kernel(mass_ref, velocity_ref, stress_ref, magnetic_ref, own_ref, low_ref, high_ref):
+CELLS, COUPLE, FLOWS, ADVANCE = 320, 152, 48, 288
+
+
+def is_even(axis):
+    return lax.axis_index(axis) % 2 == 0
+
+
+def pack_kernel(mass_ref, velocity_ref, stress_ref, magnetic_ref, own_ref, near_ref, far_ref):
+    even = is_even("gy")
     for x in range(OWN):
         fields = [mass_ref[x]] + [velocity_ref[c, x] for c in range(3)]
         fields += [stress_ref[x]] + [magnetic_ref[c, x] for c in range(3)]
         for n, value in enumerate(fields):
+            low, high = value[:RIM], value[OWN - RIM :]
             own_ref[n, OWN * x : OWN * (x + 1)] = value
-            low_ref[n, RIM * x : RIM * (x + 1)] = value[:RIM]
-            high_ref[n, RIM * x : RIM * (x + 1)] = value[OWN - RIM :]
-
-
-def widen_kernel(own_ref, left_ref, right_ref, mid_ref, low_ref, high_ref):
+            near_ref[n, RIM * x : RIM * (x + 1)] = jnp.where(even, high, low)
+            far_ref[n, RIM * x : RIM * (x + 1)] = jnp.where(even, low, high)
+
+
+def widen_kernel(own_ref, near_ref, far_ref, mid_ref, sent_ref):
+    even = is_even("gy")
     for x in range(OWN):
-        targets = [(mid_ref, x * W)]
-        if x < RIM:
-            targets.append((low_ref, x * W))
-        if x >= OWN - RIM:
-            targets.append((high_ref, (x - OWN + RIM) * W))
         for n in range(8):
-            left = left_ref[n, RIM * x : RIM * (x + 1)]
-            value = own_ref[n, OWN * x : OWN * (x + 1)]
-            right = right_ref[n, RIM * x : RIM * (x + 1)]
-            for ref, at in targets:
-                ref[n, at : at + RIM] = left
-                ref[n, at + RIM : at + RIM + OWN] = value
-                ref[n, at + RIM + OWN : at + W] = right
+            near = near_ref[n, RIM * x : RIM * (x + 1)]
+            far = far_ref[n, RIM * x : RIM * (x + 1)]
+            at = x * W
+            mid_ref[n, at : at + RIM] = jnp.where(even, far, near)
+            mid_ref[n, at + RIM : at + RIM + OWN] = own_ref[n, OWN * x : OWN * (x + 1)]
+            mid_ref[n, at + RIM + OWN : at + W] = jnp.where(even, near, far)
+    first = pl.multiple_of(jnp.where(is_even("gx"), 0, MID - SENT), 8)
+    for n in range(8):
+        sent_ref[n] = mid_ref[n, pl.ds(first, SENT), :]
 
 
 def up(a):
@@ -117,91 +121,125 @@
     return result
 
 
-def each_block(first, last, rows, body):
-    begin = first * W // 8 * 8
-    count = -(-(last * W - begin) // rows)
-
+def at(ref, n, r, offset=0):
+    return ref[n, pl.ds(r[0] + offset, r[1]), :]
+
+
+def put(ref, n, r, value):
+    ref[n, pl.ds(r[0], r[1]), :] = value
+
+
+def blocks(begin, rows, count, body):
     def step(i, carry):
         body((pl.multiple_of(PAD + begin + i * rows, 8), rows))
         return carry
 
-    lax.fori_loop(0, count, step, 0)
+    if count == 1:
+        step(0, 0)
+    else:
+        lax.fori_loop(0, count, step, 0)
+
+
+def each_block(first, last, rows, body):
+    begin = first * W // 8 * 8
+    blocks(begin, rows, -(-(last * W - begin) // rows), body)
+
+
+def cell_fields(q, r):
+    put(q, 8, r, 0.5 * (at(q, 5, r) + at(q, 5, r, W)))
+    put(q, 9, r, 0.5 * (at(q, 6, r) + at(q, 6, r, 1)))
+    bz = at(q, 7, r)
+    put(q, 10, r, 0.5 * (bz + up(bz)))
+
+
+def changing(d):
+    return list(range(5)) + [8 + c for c in range(3) if c != d]
+
+
+def side_states(q, hi, d, offset, r, n, name):
+    value = at(q, name, r)
+    half = half_slope(value - at(q, name, r, -offset), at(q, name, r, offset) - value)
+    put(hi, n, r, value + half)
+    return value - half
+
+
+def side_fluxes(q, hi, d, offset, target, r):
+    upper = [side_states(q, hi, d, offset, r, n, name) for n, name in enumerate(changing(d))]
+    lower = [at(hi, n, r, -offset) for n in range(7)]
+    for n, value in enumerate(twice_flux(lower, upper, at(q, 5 + d, r), d)):
+        put(target, n, r, value)
+
+
+def stored_states(q, hi, d, offset, r):
+    for n, name in enumerate(changing(d)):
+        put(hi, 7 + n, r, side_states(q, hi, d, offset, r, n, name))
+
+
+def stored_fluxes(q, hi, d, offset, target, r):
+    upper = [at(hi, 7 + n, r) for n in range(7)]
+    lower = [at(hi, n, r, -offset) for n in range(7)]
+    for n, value in enumerate(twice_flux(lower, upper, at(q, 5 + d, r), d)):
+        put(target, n, r, value)
+
+
+def height_states(q, hi, r):
+    for n, name in enumerate(changing(2)):
+        value = at(q, name, r)
+        before, earlier, after = down(value), down(value, 2), up(value)
+        below = value - before
+        put(hi, 7 + n, r, value - half_slope(below, after - value))
+        put(hi, n, r, before + half_slope(before - earlier, below))
+
+
+def early_kernel(mid_ref, near_ref, q, gx, gy, gz, hi):
+    even = is_even("gx")
+    source = pl.multiple_of(jnp.where(even, 0, MID - SENT), 8)
+    target = pl.multiple_of(PAD + jnp.where(even, SENT + MID, 0), 8)
+    for n in range(8):
+        q[n, PAD + SENT : PAD + SENT + MID] = mid_ref[n]
+        q[n, pl.ds(target, SENT), :] = near_ref[n, pl.ds(source, SENT), :]
+    base = jnp.where(even, SENT, 0)
+    blocks(base, SENT + MID, 1, lambda r: cell_fields(q, r))
+    blocks(base, 136, 2, lambda r: height_states(q, hi, r))
+    blocks(base, 16, 17, lambda r: stored_fluxes(q, hi, 2, 0, gz, r))
+    blocks(base, 16, 17, lambda r: side_fluxes(q, hi, 1, 1, gy, r))
+    blocks(base + 16, 16, 16, lambda r: side_fluxes(q, hi, 0, W, gx, r))
 
 
 def main_kernel(
-    before_ref,
-    mid_ref,
-    after_ref,
+    far_ref,
+    q_in,
+    gx_in,
+    gy_in,
+    gz_in,
     density_out,
     velocity_out,
     pressure_out,
     magnetic_out,
     q,
-    hi,
     gx,
     gy,
     gz,
+    hi,
     edge,
     face,
     cell,
     coupling,
     heat,
 ):
-    def at(ref, n, r, offset=0):
-        return ref[n, pl.ds(r[0] + offset, r[1]), :]
-
-    def put(ref, n, r, value):
-        ref[n, pl.ds(r[0], r[1]), :] = value
-
+    even = is_even("gx")
+    target = pl.multiple_of(PAD + jnp.where(even, 0, SENT + MID), 8)
     for n in range(8):
-        q[n, PAD : PAD + SENT] = before_ref[n]
-        q[n, PAD + SENT : PAD + SENT + MID] = mid_ref[n]
-        q[n, PAD + SENT + MID : PAD + W * W] = after_ref[n]
-
-    def cell_fields(r):
-        put(q, 8, r, 0.5 * (at(q, 5, r) + at(q, 5, r, W)))
-        put(q, 9, r, 0.5 * (at(q, 6, r) + at(q, 6, r, 1)))
-        bz = at(q, 7, r)
-        put(q, 10, r, 0.5 * (bz + up(bz)))
-
-    each_block(0, W, 400, cell_fields)
-
-    def side_fluxes(d, offset, target):
-        names = list(range(5)) + [8 + c for c in range(3) if c != d]
-
-        def body(r):
-            upper = []
-            for n, name in enumerate(names):
-                value = at(q, name, r)
-                half = half_slope(value - at(q, name, r, -offset), at(q, name, r, offset) - value)
-                upper.append(value - half)
-                put(hi, n, r, value + half)
-            lower = [at(hi, n, r, -offset) for n in range(7)]
-            for n, value in enumerate(twice_flux(lower, upper, at(q, 5 + d, r), d)):
-                put(target, n, r, value)
-
-        each_block(1, W - 1, 16, body)
-
-    side_fluxes(0, W, gx)
-    side_fluxes(1, 1, gy)
-
-    def height_states(r):
-        for n, name in enumerate(list(range(5)) + [8, 9]):
-            value = at(q, name, r)
-            before, earlier, after = down(value), down(value, 2), up(value)
-            below = value - before
-            put(hi, n, r, value - half_slope(below, after - value))
-            put(hi, 7 + n, r, before + half_slope(before - earlier, below))
-
-    each_block(1, W - 1, STATES, height_states)
-
-    def height_fluxes(r):
-        upper = [at(hi, n, r) for n in range(7)]
-        lower = [at(hi, 7 + n, r) for n in range(7)]
-        for n, value in enumerate(twice_flux(lower, upper, at(q, 7, r), 2)):
-            put(gz, n, r, value)
-
-    each_block(1, W - 1, 16, height_fluxes)
+        q[n, pl.ds(target, SENT), :] = far_ref[n]
+    base = jnp.where(even, 0, 256)
+    blocks(base, 144, 1, lambda r: cell_fields(q, r))
+    blocks(base, 128, 1, lambda r: height_states(q, hi, r))
+    blocks(base, 16, 8, lambda r: stored_fluxes(q, hi, 2, 0, gz, r))
+    base = jnp.where(even, 0, 240)
+    blocks(base, 16, 9, lambda r: side_fluxes(q, hi, 1, 1, gy, r))
+    base = jnp.where(even, 16, 232)
+    blocks(base, 152, 1, lambda r: stored_states(q, hi, 0, W, r))
+    blocks(base + 24, 16, 8, lambda r: stored_fluxes(q, hi, 0, W, gx, r))
 
     quarter = 0.125 * TIME_STEP
 
@@ -379,53 +417,63 @@
             magnetic_out[c, x] = at(face, c, r)
 
 
-def main_call(before, mid, after, kernel=main_kernel, name="main"):
-    def shaped(*shape):
-        return jax.ShapeDtypeStruct(shape, jnp.float32)
-
-    block = (OWN, OWN, NZ)
-    return pl.pallas_call(
-        kernel,
-        out_shape=(shaped(*block), shaped(3, *block), shaped(*block), shaped(3, *block)),
-        scratch_shapes=[
-            pltpu.VMEM((n, ROWS, NZ), jnp.float32) for n in (11, 14, 7, 7, 7, 3, 3, 9, 9, 12)
-        ],
-        compiler_params=pltpu.CompilerParams(vmem_limit_bytes=40 * 1024 * 1024),
-        name=name,
-    )(before, mid, after)
-
-
-def in_vmem(kernel, name, arguments, *shapes):
+def kept(a):
+    return pltpu.with_memory_space_constraint(a, pltpu.VMEM)
+
+
+def in_vmem(*shape):
+    return pltpu.VMEM(shape, jnp.float32)
+
+
+def on_chip(kernel, name, arguments, shapes, scratch=(), limit=None):
     spec = pl.BlockSpec(memory_space=pltpu.VMEM)
     results = pl.pallas_call(
         kernel,
         in_specs=[spec] * len(arguments),
         out_specs=[spec] * len(shapes),
-        out_shape=[pltpu.VMEM(shape, jnp.float32) for shape in shapes],
+        out_shape=[in_vmem(*shape) for shape in shapes],
+        scratch_shapes=[pltpu.VMEM(shape, jnp.float32) for shape in scratch],
+        compiler_params=pltpu.CompilerParams(vmem_limit_bytes=limit),
         name=name,
     )(*arguments)
-    return [pltpu.with_memory_space_constraint(a, pltpu.VMEM) for a in results]
-
-
-def shift(a, axis, by):
+    return [kept(a) for a in results]
+
+
+def swapped(a, axis, near):
     count = lax.axis_size(axis)
-    moved = lax.ppermute(a, axis, [(i, (i + by) % count) for i in range(count)])
-    return pltpu.with_memory_space_constraint(moved, pltpu.VMEM)
+    step = 1 if near else count - 1
+    pairs = [(i, (i + (step if i % 2 == 0 else count - step)) % count) for i in range(count)]
+    return kept(lax.ppermute(a, axis, pairs))
+
+
+def main_call(far, buffers):
+    spec = pl.BlockSpec(memory_space=pltpu.VMEM)
+    block = (OWN, OWN, NZ)
+    shapes = (block, (3, *block), block, (3, *block))
+    return pl.pallas_call(
+        main_kernel,
+        in_specs=[spec] * 5,
+        out_specs=[spec] * 8,
+        out_shape=[jax.ShapeDtypeStruct(shape, jnp.float32) for shape in shapes]
+        + [in_vmem(*a.shape) for a in buffers],
+        input_output_aliases={1 + n: 4 + n for n in range(4)},
+        scratch_shapes=[pltpu.VMEM((n, ROWS, NZ), jnp.float32) for n in (14, 3, 3, 9, 9, 12)],
+        compiler_params=pltpu.CompilerParams(vmem_limit_bytes=24 * 1024 * 1024),
+        name="main",
+    )(far, *buffers)[:4]
 
 
 def local(*arguments):
-    packed, sent = (8, OWN * RIM, NZ), (8, SENT, NZ)
-    own, to_low, to_high = in_vmem(
-        pack_kernel, "pack", arguments, (8, OWN * OWN, NZ), packed, packed
-    )
-    left = shift(to_high, "gy", 1)
-    right = shift(to_low, "gy", -1)
-    mid, to_low, to_high = in_vmem(
-        widen_kernel, "widen", (own, left, right), (8, MID, NZ), sent, sent
-    )
-    before = shift(to_high, "gx", 1)
-    after = shift(to_low, "gx", -1)
-    return main_call(before, mid, after)
+    packed = (8, OWN * RIM, NZ)
+    own, near, far = on_chip(pack_kernel, "pack", arguments, [(8, OWN * OWN, NZ), packed, packed])
+    far = swapped(far, "gy", False)
+    near = swapped(near, "gy", True)
+    mid, sent = on_chip(widen_kernel, "widen", (own, near, far), [(8, MID, NZ), (8, SENT, NZ)])
+    far = swapped(sent, "gx", False)
+    near = swapped(mid, "gx", True)
+    shapes = [(n, ROWS, NZ) for n in (11, 7, 7, 7)]
+    buffers = on_chip(early_kernel, "early", (mid, near), shapes, [(14, ROWS, NZ)], 24 << 20)
+    return tuple(main_call(far, buffers))
 
 
 def solution(mesh):

time: 49.9 us -> 46.9 us (0.940)
  waiting for transfers between devices: 16.4 us -> 13 us
  starting transfers between devices: 22.1 us -> 22.6 us
    ppermute x4, waiting for transfers between devices: 16.4 us -> 13 us  [swapped(): return kept(lax.ppermute(a, axis, pairs))]
    pallas_call x3 -> x4, Pallas kernels: 10.4 us -> 10.4 us  [the longest x1 5.57 us: main_call(): pl.pallas_call(main_kernel, in_specs=[spec] * 5, out_specs=[spec] * 8, ou...]
  transfers between devices with their start and end apart: 4 -> 4, of which waited for: 4 -> 2; matrix products, arithmetic and copies ran while one was open for 0% -> 0% of each run, Pallas kernels for 0% -> 8%
where the time goes in v4:
time: 46.9 us; the launch traced here: 46.6 us
  starting transfers between devices  22.6 us (48%)
  waiting for transfers between devices  13 us (28%)
  Pallas kernels  10.4 us (22%)
  between operations  0.7 us (1%)
    ppermute x4, starting transfers between devices, swapped(): return kept(lax.ppermute(a, axis, pairs))  22.6 us
    ppermute x4, waiting for transfers between devices, swapped(): return kept(lax.ppermute(a, axis, pairs))  13 us
    pallas_call x1, Pallas kernels, main_call(): pl.pallas_call(main_kernel, in_specs=[spec] * 5, out_specs=[spec] * 8, ou...  5.57 us
    pallas_call x3, Pallas kernels, on_chip(): pl.pallas_call(kernel, in_specs=[spec] * len(arguments), out_specs=[spec]...  4.84 us
  transfers between devices with their start and end apart: 4, of which 2 were waited for; matrix products, arithmetic and copies ran while one was open for 0% of the time, Pallas kernels for 8%

profile of v4, /device:TPU:1, one launch (start us, length us, event | category | flops | bytes accessed | tf_op | source)
XLA Modules:
  0.0 46.6 jit_solution(1435706075579914368)
XLA Ops:
  0.6 1.0 %pack.1 = (f32[8,64,128]{2,1,0:T(8,128)S(1)}, f32[8,48,128]{2,1,0:T(8,128)S(1)}, f32[8,48,128]{2,1,0:T(8,128)S(1)}) custom-call(f32[8,8,128]{2,1,0:T(8,128)} %mass_ref.1, f32[3,8,8,128]{3,2,1,0:T(8,128)} %velocity_ref.1, f32[8,8,128]{2,1,0:T(8,128)} %stress_ref.1, f32[3,8,8,128]{3,2,1,0:T(8,128)} %magnetic_ref.1), custom_call_target="tpu_custom_call" | custom-call | tf_op jit(solution)/shard_map/pack/pallas_call | solution.py:430
  1.7 5.5 %collective-permute-start = (f32[8,48,128]{2,1,0:T(8,128)S(1)}, f32[8,48,128]{2,1,0:T(8,128)S(1)}, u32[]{:S(2)}, u32[]{:S(2)}) collective-permute-start(f32[8,48,128]{2,1,0:T(8,128)S(1)} %get-tuple-element.18), channel_id=1, source_target_pairs={{0,1},{1,0},{2,3},{3,2},{4,5},{5,4},{6,7},{7,6},{8,9},{9,8},{10,11... | collective-permute-start | bytes 589832 | tf_op jit(solution)/shard_map/ppermute | solution.py:446
  7.2 10.6 %collective-permute-start.1 = (f32[8,48,128]{2,1,0:T(8,128)S(1)}, f32[8,48,128]{2,1,0:T(8,128)S(1)}, u32[]{:S(2)}, u32[]{:S(2)}) collective-permute-start(f32[8,48,128]{2,1,0:T(8,128)S(1)} %get-tuple-element.19), channel_id=1, source_target_pairs={{0,15},{1,2},{2,1},{3,4},{4,3},{5,6},{6,5},{7,8},{8,7},{9,10},{10,... | collective-permute-start | bytes 589832 | tf_op jit(solution)/shard_map/ppermute | solution.py:446
  17.8 0.0 collective-permute-done.near_ref
  17.8 4.3 %collective-permute-done.1.far_ref = f32[8,48,128]{2,1,0:T(8,128)S(1)} collective-permute-done((f32[8,48,128]{2,1,0:T(8,128)S(1)}, f32[8,48,128]{2,1,0:T(8,128)S(1)}, u32[]{:S(2)}, u32[]{:S(2)}) %collective-permute-start.1) | collective-permute-done | bytes 196640 | tf_op jit(solution)/shard_map/ppermute | solution.py:446
  22.1 0.1 widen.1
  22.2 3.5 %collective-permute-start.3 = (f32[8,160,128]{2,1,0:T(8,128)S(1)}, f32[8,160,128]{2,1,0:T(8,128)S(1)}, u32[]{:S(2)}, u32[]{:S(2)}) collective-permute-start(f32[8,160,128]{2,1,0:T(8,128)S(1)} %get-tuple-element.21.mid_ref), channel_id=1, source_target_pairs={{0,16},{16,0},{32,48},{48,32},{64,80},{80,64},{96,112},{112,96},{1... | collective-permute-start | bytes 1966088 | tf_op jit(solution)/shard_map/ppermute | solution.py:446
  25.6 3.0 %collective-permute-start.2 = (f32[8,120,128]{2,1,0:T(8,128)S(1)}, f32[8,120,128]{2,1,0:T(8,128)S(1)}, u32[]{:S(2)}, u32[]{:S(2)}) collective-permute-start(f32[8,120,128]{2,1,0:T(8,128)S(1)} %get-tuple-element.20), channel_id=1, source_target_pairs={{0,496},{16,32},{32,16},{48,64},{64,48},{80,96},{96,80},{112,128},... | collective-permute-start | bytes 1474568 | tf_op jit(solution)/shard_map/ppermute | solution.py:446
  28.7 0.0 collective-permute-done.3.near_ref
  28.7 3.7 %early.1 = (f32[11,528,128]{2,1,0:T(8,128)S(1)}, f32[7,528,128]{2,1,0:T(8,128)S(1)}, f32[7,528,128]{2,1,0:T(8,128)S(1)}, f32[7,528,128]{2,1,0:T(8,128)S(1)}) custom-call(f32[8,160,128]{2,1,0:T(8,128)S(1)} %get-tuple-element.21.mid_ref, f32[8,160,128]{2,1,0:T(8,128)S(1)} %collective-permute-done.3.near_ref), custom_call_target="tpu_custom_call" | custom-call | tf_op jit(solution)/shard_map/early/pallas_call | solution.py:430
  32.4 8.7 %collective-permute-done.2.far_ref = f32[8,120,128]{2,1,0:T(8,128)S(1)} collective-permute-done((f32[8,120,128]{2,1,0:T(8,128)S(1)}, f32[8,120,128]{2,1,0:T(8,128)S(1)}, u32[]{:S(2)}, u32[]{:S(2)}) %collective-permute-start.2) | collective-permute-done | bytes 491552 | tf_op jit(solution)/shard_map/ppermute | solution.py:446
  41.1 5.6 %main.1 = (f32[8,8,128]{2,1,0:T(8,128)}, f32[3,8,8,128]{3,2,1,0:T(8,128)}, f32[8,8,128]{2,1,0:T(8,128)}, f32[3,8,8,128]{3,2,1,0:T(8,128)}, f32[11,528,128]{2,1,0...) custom-call(f32[8,120,128]{2,1,0:T(8,128)S(1)} %collective-permute-d, ...), custom_call_target="tpu_custom_call", output_to_operand_aliasing={{4}: (1, {}), {5}: (2, {}), {6}: (3, {}), {7}: (4, {})} | custom-call | tf_op jit(solution)/shard_map/main/pallas_call | solution.py:453
Async XLA Ops:
  1.7 16.1 %collective-permute-start = (f32[8,48,128]{2,1,0:T(8,128)S(1)}, f32[8,48,128]{2,1,0:T(8,128)S(1)}, u32[]{:S(2)}, u32[]{:S(2)}) collective-permute-start(f32[8,48,128]{2,1,0:T(8,128)S(1)} %get-tuple-element.18), channel_id=1, source_target_pairs={{0,1},{1,0},{2,3},{3,2},{4,5},{5,4},{6,7},{7,6},{8,9},{9,8},{10,11... | collective-permute-start | bytes 589832 | tf_op jit(solution)/shard_map/ppermute | solution.py:446
  7.2 14.9 %collective-permute-start.1 = (f32[8,48,128]{2,1,0:T(8,128)S(1)}, f32[8,48,128]{2,1,0:T(8,128)S(1)}, u32[]{:S(2)}, u32[]{:S(2)}) collective-permute-start(f32[8,48,128]{2,1,0:T(8,128)S(1)} %get-tuple-element.19), channel_id=1, source_target_pairs={{0,15},{1,2},{2,1},{3,4},{4,3},{5,6},{6,5},{7,8},{8,7},{9,10},{10,... | collective-permute-start | bytes 589832 | tf_op jit(solution)/shard_map/ppermute | solution.py:446
  22.2 6.5 %collective-permute-start.3 = (f32[8,160,128]{2,1,0:T(8,128)S(1)}, f32[8,160,128]{2,1,0:T(8,128)S(1)}, u32[]{:S(2)}, u32[]{:S(2)}) collective-permute-start(f32[8,160,128]{2,1,0:T(8,128)S(1)} %get-tuple-element.21.mid_ref), channel_id=1, source_target_pairs={{0,16},{16,0},{32,48},{48,32},{64,80},{80,64},{96,112},{112,96},{1... | collective-permute-start | bytes 1966088 | tf_op jit(solution)/shard_map/ppermute | solution.py:446
  25.6 15.4 %collective-permute-start.2 = (f32[8,120,128]{2,1,0:T(8,128)S(1)}, f32[8,120,128]{2,1,0:T(8,128)S(1)}, u32[]{:S(2)}, u32[]{:S(2)}) collective-permute-start(f32[8,120,128]{2,1,0:T(8,128)S(1)} %get-tuple-element.20), channel_id=1, source_target_pairs={{0,496},{16,32},{32,16},{48,64},{64,48},{80,96},{96,80},{112,128},... | collective-permute-start | bytes 1474568 | tf_op jit(solution)/shard_map/ppermute | solution.py:446

commit v5 on v4

--- a/solution.py
+++ b/solution.py
@@ -22,7 +22,7 @@
 ROWS = PAD + W * W + 96
 SENT = RIM * W
 MID = OWN * W
-CELLS, COUPLE, FLOWS, ADVANCE = 320, 152, 48, 288
+FZ, FY, FX, FLOWS, ADVANCE = 16, 16, 16, 48, 288
 
 
 def is_even(axis):
@@ -191,7 +191,103 @@
         put(hi, n, r, before + half_slope(before - earlier, below))
 
 
-def early_kernel(mid_ref, near_ref, q, gx, gy, gz, hi):
+QUARTER = 0.125 * TIME_STEP
+
+
+def edges(gx, gy, gz, edge, r):
+    fx_z = at(gx, 6, r)
+    fy_z = at(gy, 6, r)
+    put(
+        edge, 0, r, QUARTER * (at(gz, 6, r, -1) + at(gz, 6, r) - down(fy_z) - fy_z)
+    )
+    put(
+        edge, 1, r, QUARTER * (down(fx_z) + fx_z - at(gz, 5, r, -W) - at(gz, 5, r))
+    )
+    put(
+        edge,
+        2,
+        r,
+        QUARTER * (at(gy, 5, r, -W) + at(gy, 5, r) - at(gx, 5, r, -1) - at(gx, 5, r)),
+    )
+
+
+def new_faces(q, edge, face, r):
+    ex, ey, ez = at(edge, 0, r), at(edge, 1, r), at(edge, 2, r)
+    put(face, 0, r, at(q, 5, r) - (at(edge, 2, r, 1) - ez) + (up(ey) - ey))
+    put(face, 1, r, at(q, 6, r) - (up(ex) - ex) + (at(edge, 2, r, W) - ez))
+    put(face, 2, r, at(q, 7, r) - (at(edge, 1, r, W) - ey) + (at(edge, 0, r, 1) - ex))
+
+
+def put_temperature(heat, r, temperature):
+    above, below = up(temperature), down(temperature)
+    put(heat, 4, r, temperature)
+    put(heat, 5, r, temperature + below)
+    put(heat, 6, r, temperature - below)
+    put(heat, 7, r, above - below)
+
+
+def new_cells(q, gx, gy, gz, face, cell, heat, r):
+    density = at(q, 0, r)
+    momentum = [density * at(q, 1 + c, r) for c in range(3)]
+    twice_kinetic = (
+        momentum[0] * at(q, 1, r) + momentum[1] * at(q, 2, r) + momentum[2] * at(q, 3, r)
+    )
+    field_sq = (
+        at(q, 8, r) * at(q, 8, r) + at(q, 9, r) * at(q, 9, r) + at(q, 10, r) * at(q, 10, r)
+    )
+    energy = 1.5 * at(q, 4, r) + 0.5 * (twice_kinetic + field_sq)
+    updated = []
+    for n, value in enumerate([density] + momentum + [energy]):
+        change = (at(gx, n, r, W) - at(gx, n, r)) + (at(gy, n, r, 1) - at(gy, n, r))
+        above = at(gz, n, r)
+        updated.append(value - (0.5 * TIME_STEP) * (change + (up(above) - above)))
+    floored = jnp.maximum(updated[0], DENSITY_FLOOR)
+    inverse = 1.0 / floored
+    velocity = [updated[1 + c] * inverse for c in range(3)]
+    bz = at(face, 2, r)
+    field = [
+        0.5 * (at(face, 0, r) + at(face, 0, r, W)),
+        0.5 * (at(face, 1, r) + at(face, 1, r, 1)),
+        0.5 * (bz + up(bz)),
+    ]
+    twice_kinetic = (
+        updated[1] * velocity[0] + updated[2] * velocity[1] + updated[3] * velocity[2]
+    )
+    field_sq = field[0] * field[0] + field[1] * field[1] + field[2] * field[2]
+    internal = updated[4] - 0.5 * (twice_kinetic + field_sq)
+    pressure = jnp.maximum((GAMMA_RATIO - 1.0) * internal, PRESSURE_FLOOR)
+    temperature = pressure * inverse
+    put(cell, 0, r, floored)
+    for c in range(3):
+        put(cell, 1 + c, r, velocity[c])
+        put(cell, 6 + c, r, field[c])
+    put(cell, 4, r, inverse)
+    put(cell, 5, r, temperature * temperature * jnp.sqrt(temperature))
+    put(heat, 0, r, pressure)
+    put_temperature(heat, r, temperature)
+
+
+def couple(face, cell, coupling, r):
+    own_field = [at(cell, 6 + c, r) for c in range(3)]
+    own_conduct = at(cell, 5, r)
+    for d in range(3):
+        if d < 2:
+            offset = -W if d == 0 else -1
+            beside = [at(cell, 6 + c, r, offset) for c in range(3)]
+            conduct = at(cell, 5, r, offset)
+        else:
+            beside = [down(a) for a in own_field]
+            conduct = down(own_conduct)
+        normal = at(face, d, r)
+        parts = [normal if c == d else 0.5 * (own_field[c] + beside[c]) for c in range(3)]
+        size = parts[0] * parts[0] + parts[1] * parts[1] + parts[2] * parts[2]
+        factor = 0.5 * (own_conduct + conduct) / jnp.maximum(size, FIELD_FLOOR) * normal
+        mixed = 0.25 * factor
+        for c in range(3):
+            put(coupling, 3 * d + c, r, (factor if c == d else mixed) * parts[c])
+
+
+def early_kernel(mid_ref, near_ref, q, gx, gy, gz, edge, face, cell, coupling, heat, hi):
     even = is_even("gx")
     source = pl.multiple_of(jnp.where(even, 0, MID - SENT), 8)
     target = pl.multiple_of(PAD + jnp.where(even, SENT + MID, 0), 8)
@@ -204,140 +300,33 @@
     blocks(base, 16, 17, lambda r: stored_fluxes(q, hi, 2, 0, gz, r))
     blocks(base, 16, 17, lambda r: side_fluxes(q, hi, 1, 1, gy, r))
     blocks(base + 16, 16, 16, lambda r: side_fluxes(q, hi, 0, W, gx, r))
-
-
-def main_kernel(
-    far_ref,
-    q_in,
-    gx_in,
-    gy_in,
-    gz_in,
-    density_out,
-    velocity_out,
-    pressure_out,
-    magnetic_out,
-    q,
-    gx,
-    gy,
-    gz,
-    hi,
-    edge,
-    face,
-    cell,
-    coupling,
-    heat,
-):
+    blocks(base + 40, 224, 1, lambda r: edges(gx, gy, gz, edge, r))
+    blocks(base + 40, 224, 1, lambda r: new_faces(q, edge, face, r))
+    blocks(base + 40, 200, 1, lambda r: new_cells(q, gx, gy, gz, face, cell, heat, r))
+    blocks(base + 56, 184, 1, lambda r: couple(face, cell, coupling, r))
+
+
+def main_kernel(far_ref, *refs):
+    density_out, velocity_out, pressure_out, magnetic_out = refs[9:13]
+    q, gx, gy, gz, edge, face, cell, coupling, heat, hi = refs[13:]
     even = is_even("gx")
     target = pl.multiple_of(PAD + jnp.where(even, 0, SENT + MID), 8)
     for n in range(8):
         q[n, pl.ds(target, SENT), :] = far_ref[n]
-    base = jnp.where(even, 0, 256)
-    blocks(base, 144, 1, lambda r: cell_fields(q, r))
-    blocks(base, 128, 1, lambda r: height_states(q, hi, r))
-    blocks(base, 16, 8, lambda r: stored_fluxes(q, hi, 2, 0, gz, r))
-    base = jnp.where(even, 0, 240)
-    blocks(base, 16, 9, lambda r: side_fluxes(q, hi, 1, 1, gy, r))
-    base = jnp.where(even, 16, 232)
-    blocks(base, 152, 1, lambda r: stored_states(q, hi, 0, W, r))
-    blocks(base + 24, 16, 8, lambda r: stored_fluxes(q, hi, 0, W, gx, r))
-
-    quarter = 0.125 * TIME_STEP
-
-    def edges(r):
-        fx_z = at(gx, 6, r)
-        fy_z = at(gy, 6, r)
-        put(
-            edge, 0, r, quarter * (at(gz, 6, r, -1) + at(gz, 6, r) - down(fy_z) - fy_z)
-        )
-        put(
-            edge, 1, r, quarter * (down(fx_z) + fx_z - at(gz, 5, r, -W) - at(gz, 5, r))
-        )
-        put(
-            edge,
-            2,
-            r,
-            quarter * (at(gy, 5, r, -W) + at(gy, 5, r) - at(gx, 5, r, -1) - at(gx, 5, r)),
-        )
-
-    each_block(2, W - 1, 344, edges)
-
-    def new_faces(r):
-        ex, ey, ez = at(edge, 0, r), at(edge, 1, r), at(edge, 2, r)
-        put(face, 0, r, at(q, 5, r) - (at(edge, 2, r, 1) - ez) + (up(ey) - ey))
-        put(face, 1, r, at(q, 6, r) - (up(ex) - ex) + (at(edge, 2, r, W) - ez))
-        put(face, 2, r, at(q, 7, r) - (at(edge, 1, r, W) - ey) + (at(edge, 0, r, 1) - ex))
-
-    each_block(2, W - 1, 344, new_faces)
-
-    def put_temperature(r, temperature):
-        above, below = up(temperature), down(temperature)
-        put(heat, 4, r, temperature)
-        put(heat, 5, r, temperature + below)
-        put(heat, 6, r, temperature - below)
-        put(heat, 7, r, above - below)
-
-    def new_cells(r):
-        density = at(q, 0, r)
-        momentum = [density * at(q, 1 + c, r) for c in range(3)]
-        twice_kinetic = (
-            momentum[0] * at(q, 1, r) + momentum[1] * at(q, 2, r) + momentum[2] * at(q, 3, r)
-        )
-        field_sq = (
-            at(q, 8, r) * at(q, 8, r) + at(q, 9, r) * at(q, 9, r) + at(q, 10, r) * at(q, 10, r)
-        )
-        energy = 1.5 * at(q, 4, r) + 0.5 * (twice_kinetic + field_sq)
-        updated = []
-        for n, value in enumerate([density] + momentum + [energy]):
-            change = (at(gx, n, r, W) - at(gx, n, r)) + (at(gy, n, r, 1) - at(gy, n, r))
-            above = at(gz, n, r)
-            updated.append(value - (0.5 * TIME_STEP) * (change + (up(above) - above)))
-        floored = jnp.maximum(updated[0], DENSITY_FLOOR)
-        inverse = 1.0 / floored
-        velocity = [updated[1 + c] * inverse for c in range(3)]
-        bz = at(face, 2, r)
-        field = [
-            0.5 * (at(face, 0, r) + at(face, 0, r, W)),
-            0.5 * (at(face, 1, r) + at(face, 1, r, 1)),
-            0.5 * (bz + up(bz)),
-        ]
-        twice_kinetic = (
-            updated[1] * velocity[0] + updated[2] * velocity[1] + updated[3] * velocity[2]
-        )
-        field_sq = field[0] * field[0] + field[1] * field[1] + field[2] * field[2]
-        internal = updated[4] - 0.5 * (twice_kinetic + field_sq)
-        pressure = jnp.maximum((GAMMA_RATIO - 1.0) * internal, PRESSURE_FLOOR)
-        temperature = pressure * inverse
-        put(cell, 0, r, floored)
-        for c in range(3):
-            put(cell, 1 + c, r, velocity[c])
-            put(cell, 6 + c, r, field[c])
-        put(cell, 4, r, inverse)
-        put(cell, 5, r, temperature * temperature * jnp.sqrt(temperature))
-        put(heat, 0, r, pressure)
-        put_temperature(r, temperature)
-
-    each_block(2, W - 2, CELLS, new_cells)
-
-    def couple(r):
-        own_field = [at(cell, 6 + c, r) for c in range(3)]
-        own_conduct = at(cell, 5, r)
-        for d in range(3):
-            if d < 2:
-                offset = -W if d == 0 else -1
-                beside = [at(cell, 6 + c, r, offset) for c in range(3)]
-                conduct = at(cell, 5, r, offset)
-            else:
-                beside = [down(a) for a in own_field]
-                conduct = down(own_conduct)
-            normal = at(face, d, r)
-            parts = [normal if c == d else 0.5 * (own_field[c] + beside[c]) for c in range(3)]
-            size = parts[0] * parts[0] + parts[1] * parts[1] + parts[2] * parts[2]
-            factor = 0.5 * (own_conduct + conduct) / jnp.maximum(size, FIELD_FLOOR) * normal
-            mixed = 0.25 * factor
-            for c in range(3):
-                put(coupling, 3 * d + c, r, (factor if c == d else mixed) * parts[c])
-
-    each_block(3, W - 2, COUPLE, couple)
+
+    def begin(of_even, of_odd):
+        return jnp.where(even, of_even, of_odd)
+
+    blocks(begin(0, 256), 144, 1, lambda r: cell_fields(q, r))
+    blocks(begin(0, 256), 128, 1, lambda r: height_states(q, hi, r))
+    blocks(begin(0, 256), FZ, 128 // FZ, lambda r: stored_fluxes(q, hi, 2, 0, gz, r))
+    blocks(begin(0, 240), FY, 144 // FY, lambda r: side_fluxes(q, hi, 1, 1, gy, r))
+    blocks(begin(16, 232), 152, 1, lambda r: stored_states(q, hi, 0, W, r))
+    blocks(begin(40, 256), FX, 128 // FX, lambda r: stored_fluxes(q, hi, 0, W, gx, r))
+    blocks(begin(40, 256), 128, 1, lambda r: edges(gx, gy, gz, edge, r))
+    blocks(begin(40, 240), 144, 1, lambda r: new_faces(q, edge, face, r))
+    blocks(begin(40, 240), 120, 1, lambda r: new_cells(q, gx, gy, gz, face, cell, heat, r))
+    blocks(begin(56, 240), 128, 1, lambda r: couple(face, cell, coupling, r))
 
     def heat_fluxes(r):
         t = at(heat, 4, r)
@@ -402,7 +391,7 @@
         def advance(r, j=j):
             pressure = section(j, r)
             put(heat, j, r, pressure)
-            put_temperature(r, pressure * at(cell, 4, r))
+            put_temperature(heat, r, pressure * at(cell, 4, r))
 
         each_block(2 + j, W - 2 - j, ADVANCE, advance)
 
@@ -452,13 +441,13 @@
     shapes = (block, (3, *block), block, (3, *block))
     return pl.pallas_call(
         main_kernel,
-        in_specs=[spec] * 5,
-        out_specs=[spec] * 8,
+        in_specs=[spec] * (1 + len(buffers)),
+        out_specs=[spec] * (4 + len(buffers)),
         out_shape=[jax.ShapeDtypeStruct(shape, jnp.float32) for shape in shapes]
         + [in_vmem(*a.shape) for a in buffers],
-        input_output_aliases={1 + n: 4 + n for n in range(4)},
-        scratch_shapes=[pltpu.VMEM((n, ROWS, NZ), jnp.float32) for n in (14, 3, 3, 9, 9, 12)],
-        compiler_params=pltpu.CompilerParams(vmem_limit_bytes=24 * 1024 * 1024),
+        input_output_aliases={1 + n: 4 + n for n in range(len(buffers))},
+        scratch_shapes=[pltpu.VMEM((14, ROWS, NZ), jnp.float32)],
+        compiler_params=pltpu.CompilerParams(vmem_limit_bytes=16 << 20),
         name="main",
     )(far, *buffers)[:4]
 
@@ -471,8 +460,8 @@
     mid, sent = on_chip(widen_kernel, "widen", (own, near, far), [(8, MID, NZ), (8, SENT, NZ)])
     far = swapped(sent, "gx", False)
     near = swapped(mid, "gx", True)
-    shapes = [(n, ROWS, NZ) for n in (11, 7, 7, 7)]
-    buffers = on_chip(early_kernel, "early", (mid, near), shapes, [(14, ROWS, NZ)], 24 << 20)
+    shapes = [(n, ROWS, NZ) for n in (11, 7, 7, 7, 3, 3, 9, 9, 12)]
+    buffers = on_chip(early_kernel, "early", (mid, near), shapes, [(14, ROWS, NZ)], 16 << 20)
     return tuple(main_call(far, buffers))
 
 

time: 46.9 us -> 45.9 us (0.979)
  waiting for transfers between devices: 13 us -> 12 us
    pallas_call x3, Pallas kernels: 4.84 us -> 5.8 us  [on_chip(): pl.pallas_call(kernel, in_specs=[spec] * len(arguments), out_specs=[spec]...]
    ppermute x4, waiting for transfers between devices: 13 us -> 12 us  [swapped(): return kept(lax.ppermute(a, axis, pairs))]
    pallas_call x1, Pallas kernels: 5.57 us -> 4.62 us  [main_call(): pl.pallas_call(main_kernel, in_specs=[spec] * (1 + len(buffers)), out_spe...]
  transfers between devices with their start and end apart: 4 -> 4, of which waited for: 2 -> 2; matrix products, arithmetic and copies ran while one was open for 0% -> 0% of each run, Pallas kernels for 8% -> 10%
where the time goes in v5:
time: 45.9 us; the launch traced here: 45.7 us
  starting transfers between devices  22.6 us (49%)
  waiting for transfers between devices  12 us (26%)
  Pallas kernels  10.4 us (23%)
  between operations  0.7 us (2%)
    ppermute x4, starting transfers between devices, swapped(): return kept(lax.ppermute(a, axis, pairs))  22.6 us
    ppermute x4, waiting for transfers between devices, swapped(): return kept(lax.ppermute(a, axis, pairs))  12 us
    pallas_call x3, Pallas kernels, on_chip(): pl.pallas_call(kernel, in_specs=[spec] * len(arguments), out_specs=[spec]...  5.8 us
    pallas_call x1, Pallas kernels, main_call(): pl.pallas_call(main_kernel, in_specs=[spec] * (1 + len(buffers)), out_spe...  4.62 us
  transfers between devices with their start and end apart: 4, of which 2 were waited for; matrix products, arithmetic and copies ran while one was open for 0% of the time, Pallas kernels for 10%

profile of v5, /device:TPU:1, one launch (start us, length us, event | category | flops | bytes accessed | tf_op | source)
XLA Modules:
  0.0 45.7 jit_solution(10362940892189600205)
XLA Ops:
  0.6 1.0 %pack.1 = (f32[8,64,128]{2,1,0:T(8,128)S(1)}, f32[8,48,128]{2,1,0:T(8,128)S(1)}, f32[8,48,128]{2,1,0:T(8,128)S(1)}) custom-call(f32[8,8,128]{2,1,0:T(8,128)} %mass_ref.1, f32[3,8,8,128]{3,2,1,0:T(8,128)} %velocity_ref.1, f32[8,8,128]{2,1,0:T(8,128)} %stress_ref.1, f32[3,8,8,128]{3,2,1,0:T(8,128)} %magnetic_ref.1), custom_call_target="tpu_custom_call" | custom-call | tf_op jit(solution)/shard_map/pack/pallas_call | solution.py:419
  1.7 5.5 %collective-permute-start = (f32[8,48,128]{2,1,0:T(8,128)S(1)}, f32[8,48,128]{2,1,0:T(8,128)S(1)}, u32[]{:S(2)}, u32[]{:S(2)}) collective-permute-start(f32[8,48,128]{2,1,0:T(8,128)S(1)} %get-tuple-element.23), channel_id=1, source_target_pairs={{0,1},{1,0},{2,3},{3,2},{4,5},{5,4},{6,7},{7,6},{8,9},{9,8},{10,11... | collective-permute-start | bytes 589832 | tf_op jit(solution)/shard_map/ppermute | solution.py:435
  7.2 10.6 %collective-permute-start.1 = (f32[8,48,128]{2,1,0:T(8,128)S(1)}, f32[8,48,128]{2,1,0:T(8,128)S(1)}, u32[]{:S(2)}, u32[]{:S(2)}) collective-permute-start(f32[8,48,128]{2,1,0:T(8,128)S(1)} %get-tuple-element.24), channel_id=1, source_target_pairs={{0,15},{1,2},{2,1},{3,4},{4,3},{5,6},{6,5},{7,8},{8,7},{9,10},{10,... | collective-permute-start | bytes 589832 | tf_op jit(solution)/shard_map/ppermute | solution.py:435
  17.8 0.0 collective-permute-done.near_ref
  17.8 4.3 %collective-permute-done.1.far_ref = f32[8,48,128]{2,1,0:T(8,128)S(1)} collective-permute-done((f32[8,48,128]{2,1,0:T(8,128)S(1)}, f32[8,48,128]{2,1,0:T(8,128)S(1)}, u32[]{:S(2)}, u32[]{:S(2)}) %collective-permute-start.1) | collective-permute-done | bytes 196640 | tf_op jit(solution)/shard_map/ppermute | solution.py:435
  22.1 0.1 widen.1
  22.2 3.5 %collective-permute-start.3 = (f32[8,160,128]{2,1,0:T(8,128)S(1)}, f32[8,160,128]{2,1,0:T(8,128)S(1)}, u32[]{:S(2)}, u32[]{:S(2)}) collective-permute-start(f32[8,160,128]{2,1,0:T(8,128)S(1)} %get-tuple-element.26.mid_ref), channel_id=1, source_target_pairs={{0,16},{16,0},{32,48},{48,32},{64,80},{80,64},{96,112},{112,96},{1... | collective-permute-start | bytes 1966088 | tf_op jit(solution)/shard_map/ppermute | solution.py:435
  25.6 3.0 %collective-permute-start.2 = (f32[8,120,128]{2,1,0:T(8,128)S(1)}, f32[8,120,128]{2,1,0:T(8,128)S(1)}, u32[]{:S(2)}, u32[]{:S(2)}) collective-permute-start(f32[8,120,128]{2,1,0:T(8,128)S(1)} %get-tuple-element.25), channel_id=1, source_target_pairs={{0,496},{16,32},{32,16},{48,64},{64,48},{80,96},{96,80},{112,128},... | collective-permute-start | bytes 1474568 | tf_op jit(solution)/shard_map/ppermute | solution.py:435
  28.7 0.0 collective-permute-done.3.near_ref
  28.7 4.7 %early.1 = (f32[11,528,128]{2,1,0:T(8,128)S(1)}, f32[7,528,128]{2,1,0:T(8,128)S(1)}, f32[7,528,128]{2,1,0:T(8,128)S(1)}, f32[7,528,128]{2,1,0:T(8,128)S(1)}, f32...) custom-call(f32[8,160,128]{2,1,0:T(8,128)S(1)} %get-tuple-element.26, ...), custom_call_target="tpu_custom_call" | custom-call | tf_op jit(solution)/shard_map/early/pallas_call | solution.py:419
  33.3 7.7 %collective-permute-done.2.far_ref = f32[8,120,128]{2,1,0:T(8,128)S(1)} collective-permute-done((f32[8,120,128]{2,1,0:T(8,128)S(1)}, f32[8,120,128]{2,1,0:T(8,128)S(1)}, u32[]{:S(2)}, u32[]{:S(2)}) %collective-permute-start.2) | collective-permute-done | bytes 491552 | tf_op jit(solution)/shard_map/ppermute | solution.py:435
  41.1 4.6 %main.1 = (f32[8,8,128]{2,1,0:T(8,128)}, f32[3,8,8,128]{3,2,1,0:T(8,128)}, f32[8,8,128]{2,1,0:T(8,128)}, f32[3,8,8,128]{3,2,1,0:T(8,128)}, f32[11,528,128]{2,1,0...) custom-call(f32[8,120,128]{2,1,0:T(8,128)S(1)} %collective-permute-d, ...), custom_call_target="tpu_custom_call", output_to_operand_aliasing={{4}: (1, {}), {5}: (2, {}), {6}: (3, {}), {7}: (4, {}), {8}... | custom-call | tf_op jit(solution)/shard_map/main/pallas_call | solution.py:442
Async XLA Ops:
  1.7 16.1 %collective-permute-start = (f32[8,48,128]{2,1,0:T(8,128)S(1)}, f32[8,48,128]{2,1,0:T(8,128)S(1)}, u32[]{:S(2)}, u32[]{:S(2)}) collective-permute-start(f32[8,48,128]{2,1,0:T(8,128)S(1)} %get-tuple-element.23), channel_id=1, source_target_pairs={{0,1},{1,0},{2,3},{3,2},{4,5},{5,4},{6,7},{7,6},{8,9},{9,8},{10,11... | collective-permute-start | bytes 589832 | tf_op jit(solution)/shard_map/ppermute | solution.py:435
  7.2 14.9 %collective-permute-start.1 = (f32[8,48,128]{2,1,0:T(8,128)S(1)}, f32[8,48,128]{2,1,0:T(8,128)S(1)}, u32[]{:S(2)}, u32[]{:S(2)}) collective-permute-start(f32[8,48,128]{2,1,0:T(8,128)S(1)} %get-tuple-element.24), channel_id=1, source_target_pairs={{0,15},{1,2},{2,1},{3,4},{4,3},{5,6},{6,5},{7,8},{8,7},{9,10},{10,... | collective-permute-start | bytes 589832 | tf_op jit(solution)/shard_map/ppermute | solution.py:435
  22.2 6.5 %collective-permute-start.3 = (f32[8,160,128]{2,1,0:T(8,128)S(1)}, f32[8,160,128]{2,1,0:T(8,128)S(1)}, u32[]{:S(2)}, u32[]{:S(2)}) collective-permute-start(f32[8,160,128]{2,1,0:T(8,128)S(1)} %get-tuple-element.26.mid_ref), channel_id=1, source_target_pairs={{0,16},{16,0},{32,48},{48,32},{64,80},{80,64},{96,112},{112,96},{1... | collective-permute-start | bytes 1966088 | tf_op jit(solution)/shard_map/ppermute | solution.py:435
  25.6 15.4 %collective-permute-start.2 = (f32[8,120,128]{2,1,0:T(8,128)S(1)}, f32[8,120,128]{2,1,0:T(8,128)S(1)}, u32[]{:S(2)}, u32[]{:S(2)}) collective-permute-start(f32[8,120,128]{2,1,0:T(8,128)S(1)} %get-tuple-element.25), channel_id=1, source_target_pairs={{0,496},{16,32},{32,16},{48,64},{64,48},{80,96},{96,80},{112,128},... | collective-permute-start | bytes 1474568 | tf_op jit(solution)/shard_map/ppermute | solution.py:435

commit v6 on v5

--- a/solution.py
+++ b/solution.py
@@ -22,7 +22,7 @@
 ROWS = PAD + W * W + 96
 SENT = RIM * W
 MID = OWN * W
-FZ, FY, FX, FLOWS, ADVANCE = 16, 16, 16, 48, 288
+FZ, FY, FX, FLOWS, ADVANCE = 32, 48, 32, 304, 288
 
 
 def is_even(axis):
@@ -414,7 +414,7 @@
     return pltpu.VMEM(shape, jnp.float32)
 
 
-def on_chip(kernel, name, arguments, shapes, scratch=(), limit=None):
+def on_chip(kernel, name, arguments, shapes, scratch=(), limit=None, cost=None):
     spec = pl.BlockSpec(memory_space=pltpu.VMEM)
     results = pl.pallas_call(
         kernel,
@@ -423,6 +423,7 @@
         out_shape=[in_vmem(*shape) for shape in shapes],
         scratch_shapes=[pltpu.VMEM(shape, jnp.float32) for shape in scratch],
         compiler_params=pltpu.CompilerParams(vmem_limit_bytes=limit),
+        cost_estimate=cost,
         name=name,
     )(*arguments)
     return [kept(a) for a in results]
@@ -459,9 +460,12 @@
     near = swapped(near, "gy", True)
     mid, sent = on_chip(widen_kernel, "widen", (own, near, far), [(8, MID, NZ), (8, SENT, NZ)])
     far = swapped(sent, "gx", False)
-    near = swapped(mid, "gx", True)
+    near = lax.cond(
+        lax.axis_index("gx") >= 0, lambda a: swapped(a, "gx", True), lambda a: a, mid
+    )
+    near = kept(near)
     shapes = [(n, ROWS, NZ) for n in (11, 7, 7, 7, 3, 3, 9, 9, 12)]
-    buffers = on_chip(early_kernel, "early", (mid, near), shapes, [(14, ROWS, NZ)], 16 << 20)
+    buffers = on_chip(early_kernel, "early", (mid, near), shapes, [(14, ROWS, NZ)], 16 << 20, pl.CostEstimate(flops=0, bytes_accessed=1024, transcendentals=0))
     return tuple(main_call(far, buffers))
 
 

time: 45.9 us -> 43.2 us (0.941)
  waiting for transfers between devices: 12 us -> 6.56 us
  starting transfers between devices: 22.6 us -> 24.4 us
  Pallas kernels: 10.4 us -> 11.3 us
    ppermute x4, waiting for transfers between devices: 12 us -> 6.56 us  [swapped(): return kept(lax.ppermute(a, axis, pairs))]
    ppermute x4, starting transfers between devices: 22.6 us -> 24.4 us  [swapped(): return kept(lax.ppermute(a, axis, pairs))]
    pallas_call x3, Pallas kernels: 5.8 us -> 6.87 us  [on_chip(): pl.pallas_call(kernel, in_specs=[spec] * len(arguments), out_specs=[spec]...]
  transfers between devices with their start and end apart: 4 -> 4, of which waited for: 2 -> 3; matrix products, arithmetic and copies ran while one was open for 0% -> 0% of each run, Pallas kernels for 10% -> 13%
where the time goes in v6:
time: 43.2 us; the launch traced here: 43 us
  starting transfers between devices  24.4 us (56%)
  Pallas kernels  11.3 us (26%)
  waiting for transfers between devices  6.56 us (15%)
  between operations  0.68 us (2%)
    ppermute x4, starting transfers between devices, swapped(): return kept(lax.ppermute(a, axis, pairs))  24.4 us
    pallas_call x3, Pallas kernels, on_chip(): pl.pallas_call(kernel, in_specs=[spec] * len(arguments), out_specs=[spec]...  6.87 us
    ppermute x4, waiting for transfers between devices, swapped(): return kept(lax.ppermute(a, axis, pairs))  6.56 us
    pallas_call x1, Pallas kernels, main_call(): pl.pallas_call(main_kernel, in_specs=[spec] * (1 + len(buffers)), out_spe...  4.4 us
  transfers between devices with their start and end apart: 4, of which 3 were waited for; matrix products, arithmetic and copies ran while one was open for 0% of the time, Pallas kernels for 13%

profile of v6, /device:TPU:1, one launch (start us, length us, event | category | flops | bytes accessed | tf_op | source)
XLA Modules:
  0.0 43.0 jit_solution(13437678543203847730)
XLA Ops:
  0.6 1.0 %pack.1 = (f32[8,64,128]{2,1,0:T(8,128)S(1)}, f32[8,48,128]{2,1,0:T(8,128)S(1)}, f32[8,48,128]{2,1,0:T(8,128)S(1)}) custom-call(f32[8,8,128]{2,1,0:T(8,128)} %mass_ref.1, f32[3,8,8,128]{3,2,1,0:T(8,128)} %velocity_ref.1, f32[8,8,128]{2,1,0:T(8,128)} %stress_ref.1, f32[3,8,8,128]{3,2,1,0:T(8,128)} %magnetic_ref.1), custom_call_target="tpu_custom_call" | custom-call | tf_op jit(solution)/shard_map/pack/pallas_call | solution.py:419
  1.7 5.5 %collective-permute-start.1 = (f32[8,48,128]{2,1,0:T(8,128)S(1)}, f32[8,48,128]{2,1,0:T(8,128)S(1)}, u32[]{:S(2)}, u32[]{:S(2)}) collective-permute-start(f32[8,48,128]{2,1,0:T(8,128)S(1)} %get-tuple-element.28), channel_id=1, source_target_pairs={{0,1},{1,0},{2,3},{3,2},{4,5},{5,4},{6,7},{7,6},{8,9},{9,8},{10,11... | collective-permute-start | bytes 589832 | tf_op jit(solution)/shard_map/ppermute | solution.py:436
  7.2 10.6 %collective-permute-start.2 = (f32[8,48,128]{2,1,0:T(8,128)S(1)}, f32[8,48,128]{2,1,0:T(8,128)S(1)}, u32[]{:S(2)}, u32[]{:S(2)}) collective-permute-start(f32[8,48,128]{2,1,0:T(8,128)S(1)} %get-tuple-element.29), channel_id=1, source_target_pairs={{0,15},{1,2},{2,1},{3,4},{4,3},{5,6},{6,5},{7,8},{8,7},{9,10},{10,... | collective-permute-start | bytes 589832 | tf_op jit(solution)/shard_map/ppermute | solution.py:436
  17.8 0.0 collective-permute-done.1.near_ref
  17.8 4.3 %collective-permute-done.2.far_ref = f32[8,48,128]{2,1,0:T(8,128)S(1)} collective-permute-done((f32[8,48,128]{2,1,0:T(8,128)S(1)}, f32[8,48,128]{2,1,0:T(8,128)S(1)}, u32[]{:S(2)}, u32[]{:S(2)}) %collective-permute-start.2) | collective-permute-done | bytes 196640 | tf_op jit(solution)/shard_map/ppermute | solution.py:436
  22.1 0.1 widen.1
  22.2 4.6 %collective-permute-start.3 = (f32[8,120,128]{2,1,0:T(8,128)S(1)}, f32[8,120,128]{2,1,0:T(8,128)S(1)}, u32[]{:S(2)}, u32[]{:S(2)}) collective-permute-start(f32[8,120,128]{2,1,0:T(8,128)S(1)} %get-tuple-element.30), channel_id=1, source_target_pairs={{0,496},{16,32},{32,16},{48,64},{64,48},{80,96},{96,80},{112,128},... | collective-permute-start | bytes 1474568 | tf_op jit(solution)/shard_map/ppermute | solution.py:436
  26.8 5.6 %conditional.1 = (f32[8,160,128]{2,1,0:T(8,128)}) conditional(s32[]{:T(128)} %convert_element_type.3, f32[8,160,128]{2,1,0:T(8,128)S(1)} %get-tuple-element.31.mid_ref, f32[8,160,128]{2,1,0:T(8,128)S(1)} %get-tuple-element.31.mid_ref), branch_computations={%region_0.0_spmd, %region_1.0_spmd} | conditional | bytes 2621488 | solution.py:463
  26.8 3.7 %collective-permute-start = (f32[8,160,128]{2,1,0:T(8,128)S(1)}, f32[8,160,128]{2,1,0:T(8,128)}, u32[]{:S(2)}, u32[]{:S(2)}) collective-permute-start(f32[8,160,128]{2,1,0:T(8,128)S(1)} %param.1), channel_id=1, source_target_pairs={{0,16},{16,0},{32,48},{48,32},{64,80},{80,64},{96,112},{112,96},{1... | collective-permute-start | bytes 1966088 | tf_op jit(solution)/shard_map/cond/branch_1_fun/ppermute | solution.py:436
  30.5 1.8 %collective-permute-done = f32[8,160,128]{2,1,0:T(8,128)} collective-permute-done((f32[8,160,128]{2,1,0:T(8,128)S(1)}, f32[8,160,128]{2,1,0:T(8,128)}, u32[]{:S(2)}, u32[]{:S(2)}) %collective-permute-start) | collective-permute-done | bytes 655392 | tf_op jit(solution)/shard_map/cond/branch_1_fun/ppermute | solution.py:436
  32.4 5.7 %early.1 = (f32[11,528,128]{2,1,0:T(8,128)S(1)}, f32[7,528,128]{2,1,0:T(8,128)S(1)}, f32[7,528,128]{2,1,0:T(8,128)S(1)}, f32[7,528,128]{2,1,0:T(8,128)S(1)}, f32...) custom-call(f32[8,160,128]{2,1,0:T(8,128)S(1)} %get-tuple-element.31, ...), custom_call_target="tpu_custom_call" | custom-call | bytes 1024 | tf_op jit(solution)/shard_map/early/pallas_call | solution.py:419
  38.1 0.4 %collective-permute-done.3.far_ref = f32[8,120,128]{2,1,0:T(8,128)S(1)} collective-permute-done((f32[8,120,128]{2,1,0:T(8,128)S(1)}, f32[8,120,128]{2,1,0:T(8,128)S(1)}, u32[]{:S(2)}, u32[]{:S(2)}) %collective-permute-start.3) | collective-permute-done | bytes 491552 | tf_op jit(solution)/shard_map/ppermute | solution.py:436
  38.6 4.4 %main.1 = (f32[8,8,128]{2,1,0:T(8,128)}, f32[3,8,8,128]{3,2,1,0:T(8,128)}, f32[8,8,128]{2,1,0:T(8,128)}, f32[3,8,8,128]{3,2,1,0:T(8,128)}, f32[11,528,128]{2,1,0...) custom-call(f32[8,120,128]{2,1,0:T(8,128)S(1)} %collective-permute-d, ...), custom_call_target="tpu_custom_call", output_to_operand_aliasing={{4}: (1, {}), {5}: (2, {}), {6}: (3, {}), {7}: (4, {}), {8}... | custom-call | tf_op jit(solution)/shard_map/main/pallas_call | solution.py:443
Async XLA Ops:
  1.7 16.1 %collective-permute-start.1 = (f32[8,48,128]{2,1,0:T(8,128)S(1)}, f32[8,48,128]{2,1,0:T(8,128)S(1)}, u32[]{:S(2)}, u32[]{:S(2)}) collective-permute-start(f32[8,48,128]{2,1,0:T(8,128)S(1)} %get-tuple-element.28), channel_id=1, source_target_pairs={{0,1},{1,0},{2,3},{3,2},{4,5},{5,4},{6,7},{7,6},{8,9},{9,8},{10,11... | collective-permute-start | bytes 589832 | tf_op jit(solution)/shard_map/ppermute | solution.py:436
  7.2 14.9 %collective-permute-start.2 = (f32[8,48,128]{2,1,0:T(8,128)S(1)}, f32[8,48,128]{2,1,0:T(8,128)S(1)}, u32[]{:S(2)}, u32[]{:S(2)}) collective-permute-start(f32[8,48,128]{2,1,0:T(8,128)S(1)} %get-tuple-element.29), channel_id=1, source_target_pairs={{0,15},{1,2},{2,1},{3,4},{4,3},{5,6},{6,5},{7,8},{8,7},{9,10},{10,... | collective-permute-start | bytes 589832 | tf_op jit(solution)/shard_map/ppermute | solution.py:436
  22.2 16.4 %collective-permute-start.3 = (f32[8,120,128]{2,1,0:T(8,128)S(1)}, f32[8,120,128]{2,1,0:T(8,128)S(1)}, u32[]{:S(2)}, u32[]{:S(2)}) collective-permute-start(f32[8,120,128]{2,1,0:T(8,128)S(1)} %get-tuple-element.30), channel_id=1, source_target_pairs={{0,496},{16,32},{32,16},{48,64},{64,48},{80,96},{96,80},{112,128},... | collective-permute-start | bytes 1474568 | tf_op jit(solution)/shard_map/ppermute | solution.py:436
  26.8 5.6 %collective-permute-start = (f32[8,160,128]{2,1,0:T(8,128)S(1)}, f32[8,160,128]{2,1,0:T(8,128)}, u32[]{:S(2)}, u32[]{:S(2)}) collective-permute-start(f32[8,160,128]{2,1,0:T(8,128)S(1)} %param.1), channel_id=1, source_target_pairs={{0,16},{16,0},{32,48},{48,32},{64,80},{80,64},{96,112},{112,96},{1... | collective-permute-start | bytes 1966088 | tf_op jit(solution)/shard_map/cond/branch_1_fun/ppermute | solution.py:436

commit v7 on v6

--- a/solution.py
+++ b/solution.py
@@ -30,30 +30,30 @@
 
 
 def pack_kernel(mass_ref, velocity_ref, stress_ref, magnetic_ref, own_ref, near_ref, far_ref):
-    even = is_even("gy")
     for x in range(OWN):
         fields = [mass_ref[x]] + [velocity_ref[c, x] for c in range(3)]
         fields += [stress_ref[x]] + [magnetic_ref[c, x] for c in range(3)]
         for n, value in enumerate(fields):
             low, high = value[:RIM], value[OWN - RIM :]
             own_ref[n, OWN * x : OWN * (x + 1)] = value
-            near_ref[n, RIM * x : RIM * (x + 1)] = jnp.where(even, high, low)
-            far_ref[n, RIM * x : RIM * (x + 1)] = jnp.where(even, low, high)
-
-
-def widen_kernel(own_ref, near_ref, far_ref, mid_ref, sent_ref):
-    even = is_even("gy")
+            near_ref[n, RIM * x : RIM * (x + 1)] = high
+            far_ref[n, RIM * x : RIM * (x + 1)] = low
+
+
+def widen_kernel(own_ref, near_ref, far_ref, mid_ref, sent_ref, beside_ref):
     for x in range(OWN):
         for n in range(8):
             near = near_ref[n, RIM * x : RIM * (x + 1)]
             far = far_ref[n, RIM * x : RIM * (x + 1)]
             at = x * W
-            mid_ref[n, at : at + RIM] = jnp.where(even, far, near)
+            mid_ref[n, at : at + RIM] = near
             mid_ref[n, at + RIM : at + RIM + OWN] = own_ref[n, OWN * x : OWN * (x + 1)]
-            mid_ref[n, at + RIM + OWN : at + W] = jnp.where(even, near, far)
-    first = pl.multiple_of(jnp.where(is_even("gx"), 0, MID - SENT), 8)
+            mid_ref[n, at + RIM + OWN : at + W] = far
+    low = pl.multiple_of(jnp.where(is_even("gx"), 0, MID - SENT), 8)
+    high = pl.multiple_of(jnp.where(is_even("gx"), MID - SENT, 0), 8)
     for n in range(8):
-        sent_ref[n] = mid_ref[n, pl.ds(first, SENT), :]
+        sent_ref[n] = mid_ref[n, pl.ds(low, SENT), :]
+        beside_ref[n] = mid_ref[n, pl.ds(high, SENT), :]
 
 
 def up(a):
@@ -287,18 +287,26 @@
             put(coupling, 3 * d + c, r, (factor if c == d else mixed) * parts[c])
 
 
-def early_kernel(mid_ref, near_ref, q, gx, gy, gz, edge, face, cell, coupling, heat, hi):
+def early_kernel(mid_ref, near_ref, q, gx, gy, gz, edge, face, cell, coupling, heat, hi, landed, arrived):
     even = is_even("gx")
-    source = pl.multiple_of(jnp.where(even, 0, MID - SENT), 8)
     target = pl.multiple_of(PAD + jnp.where(even, SENT + MID, 0), 8)
+    copy = pltpu.make_async_copy(near_ref, landed, arrived)
+    copy.start()
     for n in range(8):
         q[n, PAD + SENT : PAD + SENT + MID] = mid_ref[n]
-        q[n, pl.ds(target, SENT), :] = near_ref[n, pl.ds(source, SENT), :]
+
+    def upright(begin):
+        blocks(begin, MID, 1, lambda r: cell_fields(q, r))
+        blocks(begin, 144, 1, lambda r: height_states(q, hi, r))
+        blocks(begin, 48, 3, lambda r: stored_fluxes(q, hi, 2, 0, gz, r))
+        blocks(begin, 48, 3, lambda r: side_fluxes(q, hi, 1, 1, gy, r))
+
+    upright(SENT)
+    copy.wait()
+    for n in range(8):
+        q[n, pl.ds(target, SENT), :] = landed[n]
+    upright(jnp.where(even, 256, 0))
     base = jnp.where(even, SENT, 0)
-    blocks(base, SENT + MID, 1, lambda r: cell_fields(q, r))
-    blocks(base, 136, 2, lambda r: height_states(q, hi, r))
-    blocks(base, 16, 17, lambda r: stored_fluxes(q, hi, 2, 0, gz, r))
-    blocks(base, 16, 17, lambda r: side_fluxes(q, hi, 1, 1, gy, r))
     blocks(base + 16, 16, 16, lambda r: side_fluxes(q, hi, 0, W, gx, r))
     blocks(base + 40, 224, 1, lambda r: edges(gx, gy, gz, edge, r))
     blocks(base + 40, 224, 1, lambda r: new_faces(q, edge, face, r))
@@ -414,14 +422,16 @@
     return pltpu.VMEM(shape, jnp.float32)
 
 
-def on_chip(kernel, name, arguments, shapes, scratch=(), limit=None, cost=None):
+def on_chip(kernel, name, arguments, shapes, scratch=(), limit=None, cost=None, anywhere=0):
     spec = pl.BlockSpec(memory_space=pltpu.VMEM)
     results = pl.pallas_call(
         kernel,
-        in_specs=[spec] * len(arguments),
+        in_specs=[spec] * (len(arguments) - anywhere)
+        + [pl.BlockSpec(memory_space=pl.ANY)] * anywhere,
         out_specs=[spec] * len(shapes),
         out_shape=[in_vmem(*shape) for shape in shapes],
-        scratch_shapes=[pltpu.VMEM(shape, jnp.float32) for shape in scratch],
+        scratch_shapes=[pltpu.VMEM(shape, jnp.float32) for shape in scratch]
+        + [pltpu.SemaphoreType.DMA] * anywhere,
         compiler_params=pltpu.CompilerParams(vmem_limit_bytes=limit),
         cost_estimate=cost,
         name=name,
@@ -456,16 +466,19 @@
 def local(*arguments):
     packed = (8, OWN * RIM, NZ)
     own, near, far = on_chip(pack_kernel, "pack", arguments, [(8, OWN * OWN, NZ), packed, packed])
-    far = swapped(far, "gy", False)
-    near = swapped(near, "gy", True)
-    mid, sent = on_chip(widen_kernel, "widen", (own, near, far), [(8, MID, NZ), (8, SENT, NZ)])
+    count = lax.axis_size("gy")
+    far = kept(lax.ppermute(far, "gy", [(i, (i - 1) % count) for i in range(count)]))
+    near = kept(lax.ppermute(near, "gy", [(i, (i + 1) % count) for i in range(count)]))
+    message = (8, SENT, NZ)
+    mid, sent, beside = on_chip(
+        widen_kernel, "widen", (own, near, far), [(8, MID, NZ), message, message]
+    )
     far = swapped(sent, "gx", False)
     near = lax.cond(
-        lax.axis_index("gx") >= 0, lambda a: swapped(a, "gx", True), lambda a: a, mid
-    )
-    near = kept(near)
+        lax.axis_index("gx") >= 0, lambda a: swapped(a, "gx", True), lambda a: a, beside
+    )
     shapes = [(n, ROWS, NZ) for n in (11, 7, 7, 7, 3, 3, 9, 9, 12)]
-    buffers = on_chip(early_kernel, "early", (mid, near), shapes, [(14, ROWS, NZ)], 16 << 20, pl.CostEstimate(flops=0, bytes_accessed=1024, transcendentals=0))
+    buffers = on_chip(early_kernel, "early", (mid, near), shapes, [(14, ROWS, NZ), message], 16 << 20, pl.CostEstimate(flops=0, bytes_accessed=1024, transcendentals=0), 1)
     return tuple(main_call(far, buffers))
 
 

time: 43.2 us -> 41.4 us (0.958)
  starting transfers between devices: 24.4 us -> 23.3 us
  Pallas kernels: 11.3 us -> 10.6 us
    ppermute x4 -> x2, starting transfers between devices: 24.4 us -> 7.43 us  [swapped(): return kept(lax.ppermute(a, axis, pairs))]
    ppermute x0 -> x2, starting transfers between devices: none -> 15.9 us  [the longest x1 10.4 us: local(): lax.ppermute(far, 'gy', [(i, (i - 1) % count) for i in range(count)])]
    ppermute x4 -> x2, waiting for transfers between devices: 6.56 us -> 2.92 us  [swapped(): return kept(lax.ppermute(a, axis, pairs))]
    ppermute x0 -> x2, waiting for transfers between devices: none -> 3.59 us  [the longest x1 2.72 us: local(): lax.ppermute(near, 'gy', [(i, (i + 1) % count) for i in range(count)])]
    pallas_call x3, Pallas kernels: 6.87 us -> 6.17 us  [on_chip(): pl.pallas_call(kernel, in_specs=[spec] * (len(arguments) - anywhere) + [p...]
  transfers between devices with their start and end apart: 4 -> 4, of which waited for: 3 -> 4; matrix products, arithmetic and copies ran while one was open for 0% -> 0% of each run, Pallas kernels for 13% -> 12%
where the time goes in v7:
time: 41.4 us; the launch traced here: 41.1 us
  starting transfers between devices  23.3 us (56%)
  Pallas kernels  10.6 us (26%)
  waiting for transfers between devices  6.51 us (16%)
  between operations  0.68 us (2%)
    ppermute x1, starting transfers between devices, local(): lax.ppermute(far, 'gy', [(i, (i - 1) % count) for i in range(count)])  10.4 us
    ppermute x2, starting transfers between devices, swapped(): return kept(lax.ppermute(a, axis, pairs))  7.43 us
    pallas_call x3, Pallas kernels, on_chip(): pl.pallas_call(kernel, in_specs=[spec] * (len(arguments) - anywhere) + [p...  6.17 us
    ppermute x1, starting transfers between devices, local(): lax.ppermute(near, 'gy', [(i, (i + 1) % count) for i in range(count)])  5.48 us
    pallas_call x1, Pallas kernels, main_call(): pl.pallas_call(main_kernel, in_specs=[spec] * (1 + len(buffers)), out_spe...  4.4 us
    ppermute x2, waiting for transfers between devices, swapped(): return kept(lax.ppermute(a, axis, pairs))  2.92 us
    ppermute x1, waiting for transfers between devices, local(): lax.ppermute(near, 'gy', [(i, (i + 1) % count) for i in range(count)])  2.72 us
    ppermute x1, waiting for transfers between devices, local(): lax.ppermute(far, 'gy', [(i, (i - 1) % count) for i in range(count)])  0.87 us
  transfers between devices with their start and end apart: 4, of which 4 were waited for; matrix products, arithmetic and copies ran while one was open for 0% of the time, Pallas kernels for 12%

profile of v7, /device:TPU:1, one launch (start us, length us, event | category | flops | bytes accessed | tf_op | source)
XLA Modules:
  0.0 41.1 jit_solution(1387021089046772660)
XLA Ops:
  0.6 1.0 %pack.1 = (f32[8,64,128]{2,1,0:T(8,128)S(1)}, f32[8,48,128]{2,1,0:T(8,128)S(1)}, f32[8,48,128]{2,1,0:T(8,128)S(1)}) custom-call(f32[8,8,128]{2,1,0:T(8,128)} %mass_ref.1, f32[3,8,8,128]{3,2,1,0:T(8,128)} %velocity_ref.1, f32[8,8,128]{2,1,0:T(8,128)} %stress_ref.1, f32[3,8,8,128]{3,2,1,0:T(8,128)} %magnetic_ref.1), custom_call_target="tpu_custom_call" | custom-call | tf_op jit(solution)/shard_map/pack/pallas_call | solution.py:427
  1.7 5.5 %collective-permute-start.1 = (f32[8,48,128]{2,1,0:T(8,128)S(1)}, f32[8,48,128]{2,1,0:T(8,128)S(1)}, u32[]{:S(2)}, u32[]{:S(2)}) collective-permute-start(f32[8,48,128]{2,1,0:T(8,128)S(1)} %get-tuple-element.29), channel_id=1, source_target_pairs={{0,1},{1,2},{2,3},{3,4},{4,5},{5,6},{6,7},{7,8},{8,9},{9,10},{10,1... | collective-permute-start | bytes 589832 | tf_op jit(solution)/shard_map/ppermute | solution.py:471
  7.2 10.4 %collective-permute-start.2 = (f32[8,48,128]{2,1,0:T(8,128)S(1)}, f32[8,48,128]{2,1,0:T(8,128)S(1)}, u32[]{:S(2)}, u32[]{:S(2)}) collective-permute-start(f32[8,48,128]{2,1,0:T(8,128)S(1)} %get-tuple-element.30), channel_id=1, source_target_pairs={{0,15},{1,0},{2,1},{3,2},{4,3},{5,4},{6,5},{7,6},{8,7},{9,8},{10,9... | collective-permute-start | bytes 589832 | tf_op jit(solution)/shard_map/ppermute | solution.py:470
  17.6 2.7 %collective-permute-done.1.near_ref = f32[8,48,128]{2,1,0:T(8,128)S(1)} collective-permute-done((f32[8,48,128]{2,1,0:T(8,128)S(1)}, f32[8,48,128]{2,1,0:T(8,128)S(1)}, u32[]{:S(2)}, u32[]{:S(2)}) %collective-permute-start.1) | collective-permute-done | bytes 196640 | tf_op jit(solution)/shard_map/ppermute | solution.py:471
  20.3 0.9 %collective-permute-done.2.far_ref = f32[8,48,128]{2,1,0:T(8,128)S(1)} collective-permute-done((f32[8,48,128]{2,1,0:T(8,128)S(1)}, f32[8,48,128]{2,1,0:T(8,128)S(1)}, u32[]{:S(2)}, u32[]{:S(2)}) %collective-permute-start.2) | collective-permute-done | bytes 196640 | tf_op jit(solution)/shard_map/ppermute | solution.py:470
  21.2 0.1 widen.1
  21.3 3.7 %collective-permute-start.3 = (f32[8,120,128]{2,1,0:T(8,128)S(1)}, f32[8,120,128]{2,1,0:T(8,128)S(1)}, u32[]{:S(2)}, u32[]{:S(2)}) collective-permute-start(f32[8,120,128]{2,1,0:T(8,128)S(1)} %get-tuple-element.31), channel_id=1, source_target_pairs={{0,496},{16,32},{32,16},{48,64},{64,48},{80,96},{96,80},{112,128},... | collective-permute-start | bytes 1474568 | tf_op jit(solution)/shard_map/ppermute | solution.py:446
  25.0 5.3 %conditional.1 = (f32[8,120,128]{2,1,0:T(8,128)S(1)}) conditional(s32[]{:T(128)} %convert_element_type.3, f32[8,120,128]{2,1,0:T(8,128)S(1)} %get-tuple-element.33, f32[8,120,128]{2,1,0:T(8,128)S(1)} %get-tuple-element.33), branch_computations={%region_0.0_spmd, %region_1.0_spmd} | conditional | bytes 2949168 | solution.py:477
  25.0 3.8 %collective-permute-start = (f32[8,120,128]{2,1,0:T(8,128)S(1)}, f32[8,120,128]{2,1,0:T(8,128)S(1)}, u32[]{:S(2)}, u32[]{:S(2)}) collective-permute-start(f32[8,120,128]{2,1,0:T(8,128)S(1)} %param.1), channel_id=1, source_target_pairs={{0,16},{16,0},{32,48},{48,32},{64,80},{80,64},{96,112},{112,96},{1... | collective-permute-start | bytes 1474568 | tf_op jit(solution)/shard_map/cond/branch_1_fun/ppermute | solution.py:446
  28.7 1.5 %collective-permute-done = f32[8,120,128]{2,1,0:T(8,128)S(1)} collective-permute-done((f32[8,120,128]{2,1,0:T(8,128)S(1)}, f32[8,120,128]{2,1,0:T(8,128)S(1)}, u32[]{:S(2)}, u32[]{:S(2)}) %collective-permute-start) | collective-permute-done | bytes 491552 | tf_op jit(solution)/shard_map/cond/branch_1_fun/ppermute | solution.py:446
  30.2 5.0 %early.1 = (f32[11,528,128]{2,1,0:T(8,128)S(1)}, f32[7,528,128]{2,1,0:T(8,128)S(1)}, f32[7,528,128]{2,1,0:T(8,128)S(1)}, f32[7,528,128]{2,1,0:T(8,128)S(1)}, f32...) custom-call(f32[8,160,128]{2,1,0:T(8,128)S(1)} %get-tuple-element.32, ...), custom_call_target="tpu_custom_call" | custom-call | bytes 1024 | tf_op jit(solution)/shard_map/early/pallas_call | solution.py:427
  35.3 1.5 %collective-permute-done.3.far_ref = f32[8,120,128]{2,1,0:T(8,128)S(1)} collective-permute-done((f32[8,120,128]{2,1,0:T(8,128)S(1)}, f32[8,120,128]{2,1,0:T(8,128)S(1)}, u32[]{:S(2)}, u32[]{:S(2)}) %collective-permute-start.3) | collective-permute-done | bytes 491552 | tf_op jit(solution)/shard_map/ppermute | solution.py:446
  36.7 4.4 %main.1 = (f32[8,8,128]{2,1,0:T(8,128)}, f32[3,8,8,128]{3,2,1,0:T(8,128)}, f32[8,8,128]{2,1,0:T(8,128)}, f32[3,8,8,128]{3,2,1,0:T(8,128)}, f32[11,528,128]{2,1,0...) custom-call(f32[8,120,128]{2,1,0:T(8,128)S(1)} %collective-permute-d, ...), custom_call_target="tpu_custom_call", output_to_operand_aliasing={{4}: (1, {}), {5}: (2, {}), {6}: (3, {}), {7}: (4, {}), {8}... | custom-call | tf_op jit(solution)/shard_map/main/pallas_call | solution.py:453
  (1 shorter events, 0.0 us)
Async XLA Ops:
  1.7 18.6 %collective-permute-start.1 = (f32[8,48,128]{2,1,0:T(8,128)S(1)}, f32[8,48,128]{2,1,0:T(8,128)S(1)}, u32[]{:S(2)}, u32[]{:S(2)}) collective-permute-start(f32[8,48,128]{2,1,0:T(8,128)S(1)} %get-tuple-element.29), channel_id=1, source_target_pairs={{0,1},{1,2},{2,3},{3,4},{4,5},{5,6},{6,7},{7,8},{8,9},{9,10},{10,1... | collective-permute-start | bytes 589832 | tf_op jit(solution)/shard_map/ppermute | solution.py:471
  7.2 14.0 %collective-permute-start.2 = (f32[8,48,128]{2,1,0:T(8,128)S(1)}, f32[8,48,128]{2,1,0:T(8,128)S(1)}, u32[]{:S(2)}, u32[]{:S(2)}) collective-permute-start(f32[8,48,128]{2,1,0:T(8,128)S(1)} %get-tuple-element.30), channel_id=1, source_target_pairs={{0,15},{1,0},{2,1},{3,2},{4,3},{5,4},{6,5},{7,6},{8,7},{9,8},{10,9... | collective-permute-start | bytes 589832 | tf_op jit(solution)/shard_map/ppermute | solution.py:470
  21.3 15.4 %collective-permute-start.3 = (f32[8,120,128]{2,1,0:T(8,128)S(1)}, f32[8,120,128]{2,1,0:T(8,128)S(1)}, u32[]{:S(2)}, u32[]{:S(2)}) collective-permute-start(f32[8,120,128]{2,1,0:T(8,128)S(1)} %get-tuple-element.31), channel_id=1, source_target_pairs={{0,496},{16,32},{32,16},{48,64},{64,48},{80,96},{96,80},{112,128},... | collective-permute-start | bytes 1474568 | tf_op jit(solution)/shard_map/ppermute | solution.py:446
  25.0 5.3 %collective-permute-start = (f32[8,120,128]{2,1,0:T(8,128)S(1)}, f32[8,120,128]{2,1,0:T(8,128)S(1)}, u32[]{:S(2)}, u32[]{:S(2)}) collective-permute-start(f32[8,120,128]{2,1,0:T(8,128)S(1)} %param.1), channel_id=1, source_target_pairs={{0,16},{16,0},{32,48},{48,32},{64,80},{80,64},{96,112},{112,96},{1... | collective-permute-start | bytes 1474568 | tf_op jit(solution)/shard_map/cond/branch_1_fun/ppermute | solution.py:446

commit v8 on v7

--- a/solution.py
+++ b/solution.py
@@ -307,7 +307,7 @@
         q[n, pl.ds(target, SENT), :] = landed[n]
     upright(jnp.where(even, 256, 0))
     base = jnp.where(even, SENT, 0)
-    blocks(base + 16, 16, 16, lambda r: side_fluxes(q, hi, 0, W, gx, r))
+    blocks(base + 16, 32, 8, lambda r: side_fluxes(q, hi, 0, W, gx, r))
     blocks(base + 40, 224, 1, lambda r: edges(gx, gy, gz, edge, r))
     blocks(base + 40, 224, 1, lambda r: new_faces(q, edge, face, r))
     blocks(base + 40, 200, 1, lambda r: new_cells(q, gx, gy, gz, face, cell, heat, r))

time: 41.4 us -> 41.4 us (level)
  no operation moved by 1% of the time
where the time goes in v8:
time: 41.4 us; the launch traced here: 41.1 us
  starting transfers between devices  23.3 us (56%)
  Pallas kernels  10.6 us (26%)
  waiting for transfers between devices  6.49 us (16%)
  between operations  0.68 us (2%)
    ppermute x1, starting transfers between devices, local(): lax.ppermute(far, 'gy', [(i, (i - 1) % count) for i in range(count)])  10.4 us
    ppermute x2, starting transfers between devices, swapped(): return kept(lax.ppermute(a, axis, pairs))  7.43 us
    pallas_call x3, Pallas kernels, on_chip(): pl.pallas_call(kernel, in_specs=[spec] * (len(arguments) - anywhere) + [p...  6.19 us
    ppermute x1, starting transfers between devices, local(): lax.ppermute(near, 'gy', [(i, (i + 1) % count) for i in range(count)])  5.48 us
    pallas_call x1, Pallas kernels, main_call(): pl.pallas_call(main_kernel, in_specs=[spec] * (1 + len(buffers)), out_spe...  4.4 us
    ppermute x2, waiting for transfers between devices, swapped(): return kept(lax.ppermute(a, axis, pairs))  2.9 us
    ppermute x1, waiting for transfers between devices, local(): lax.ppermute(near, 'gy', [(i, (i + 1) % count) for i in range(count)])  2.72 us
    ppermute x1, waiting for transfers between devices, local(): lax.ppermute(far, 'gy', [(i, (i - 1) % count) for i in range(count)])  0.87 us
  transfers between devices with their start and end apart: 4, of which 4 were waited for; matrix products, arithmetic and copies ran while one was open for 0% of the time, Pallas kernels for 12%

profile of v8, /device:TPU:1, one launch (start us, length us, event | category | flops | bytes accessed | tf_op | source)
XLA Modules:
  0.0 41.1 jit_solution(7225357432094987955)
XLA Ops:
  0.6 1.0 %pack.1 = (f32[8,64,128]{2,1,0:T(8,128)S(1)}, f32[8,48,128]{2,1,0:T(8,128)S(1)}, f32[8,48,128]{2,1,0:T(8,128)S(1)}) custom-call(f32[8,8,128]{2,1,0:T(8,128)} %mass_ref.1, f32[3,8,8,128]{3,2,1,0:T(8,128)} %velocity_ref.1, f32[8,8,128]{2,1,0:T(8,128)} %stress_ref.1, f32[3,8,8,128]{3,2,1,0:T(8,128)} %magnetic_ref.1), custom_call_target="tpu_custom_call" | custom-call | tf_op jit(solution)/shard_map/pack/pallas_call | solution.py:427
  1.7 5.5 %collective-permute-start.1 = (f32[8,48,128]{2,1,0:T(8,128)S(1)}, f32[8,48,128]{2,1,0:T(8,128)S(1)}, u32[]{:S(2)}, u32[]{:S(2)}) collective-permute-start(f32[8,48,128]{2,1,0:T(8,128)S(1)} %get-tuple-element.29), channel_id=1, source_target_pairs={{0,1},{1,2},{2,3},{3,4},{4,5},{5,6},{6,7},{7,8},{8,9},{9,10},{10,1... | collective-permute-start | bytes 589832 | tf_op jit(solution)/shard_map/ppermute | solution.py:471
  7.2 10.4 %collective-permute-start.2 = (f32[8,48,128]{2,1,0:T(8,128)S(1)}, f32[8,48,128]{2,1,0:T(8,128)S(1)}, u32[]{:S(2)}, u32[]{:S(2)}) collective-permute-start(f32[8,48,128]{2,1,0:T(8,128)S(1)} %get-tuple-element.30), channel_id=1, source_target_pairs={{0,15},{1,0},{2,1},{3,2},{4,3},{5,4},{6,5},{7,6},{8,7},{9,8},{10,9... | collective-permute-start | bytes 589832 | tf_op jit(solution)/shard_map/ppermute | solution.py:470
  17.6 2.7 %collective-permute-done.1.near_ref = f32[8,48,128]{2,1,0:T(8,128)S(1)} collective-permute-done((f32[8,48,128]{2,1,0:T(8,128)S(1)}, f32[8,48,128]{2,1,0:T(8,128)S(1)}, u32[]{:S(2)}, u32[]{:S(2)}) %collective-permute-start.1) | collective-permute-done | bytes 196640 | tf_op jit(solution)/shard_map/ppermute | solution.py:471
  20.3 0.9 %collective-permute-done.2.far_ref = f32[8,48,128]{2,1,0:T(8,128)S(1)} collective-permute-done((f32[8,48,128]{2,1,0:T(8,128)S(1)}, f32[8,48,128]{2,1,0:T(8,128)S(1)}, u32[]{:S(2)}, u32[]{:S(2)}) %collective-permute-start.2) | collective-permute-done | bytes 196640 | tf_op jit(solution)/shard_map/ppermute | solution.py:470
  21.2 0.1 widen.1
  21.3 3.7 %collective-permute-start.3 = (f32[8,120,128]{2,1,0:T(8,128)S(1)}, f32[8,120,128]{2,1,0:T(8,128)S(1)}, u32[]{:S(2)}, u32[]{:S(2)}) collective-permute-start(f32[8,120,128]{2,1,0:T(8,128)S(1)} %get-tuple-element.31), channel_id=1, source_target_pairs={{0,496},{16,32},{32,16},{48,64},{64,48},{80,96},{96,80},{112,128},... | collective-permute-start | bytes 1474568 | tf_op jit(solution)/shard_map/ppermute | solution.py:446
  25.0 5.3 %conditional.1 = (f32[8,120,128]{2,1,0:T(8,128)S(1)}) conditional(s32[]{:T(128)} %convert_element_type.3, f32[8,120,128]{2,1,0:T(8,128)S(1)} %get-tuple-element.33, f32[8,120,128]{2,1,0:T(8,128)S(1)} %get-tuple-element.33), branch_computations={%region_0.0_spmd, %region_1.0_spmd} | conditional | bytes 2949168 | solution.py:477
  25.0 3.8 %collective-permute-start = (f32[8,120,128]{2,1,0:T(8,128)S(1)}, f32[8,120,128]{2,1,0:T(8,128)S(1)}, u32[]{:S(2)}, u32[]{:S(2)}) collective-permute-start(f32[8,120,128]{2,1,0:T(8,128)S(1)} %param.1), channel_id=1, source_target_pairs={{0,16},{16,0},{32,48},{48,32},{64,80},{80,64},{96,112},{112,96},{1... | collective-permute-start | bytes 1474568 | tf_op jit(solution)/shard_map/cond/branch_1_fun/ppermute | solution.py:446
  28.7 1.5 %collective-permute-done = f32[8,120,128]{2,1,0:T(8,128)S(1)} collective-permute-done((f32[8,120,128]{2,1,0:T(8,128)S(1)}, f32[8,120,128]{2,1,0:T(8,128)S(1)}, u32[]{:S(2)}, u32[]{:S(2)}) %collective-permute-start) | collective-permute-done | bytes 491552 | tf_op jit(solution)/shard_map/cond/branch_1_fun/ppermute | solution.py:446
  30.2 5.0 %early.1 = (f32[11,528,128]{2,1,0:T(8,128)S(1)}, f32[7,528,128]{2,1,0:T(8,128)S(1)}, f32[7,528,128]{2,1,0:T(8,128)S(1)}, f32[7,528,128]{2,1,0:T(8,128)S(1)}, f32...) custom-call(f32[8,160,128]{2,1,0:T(8,128)S(1)} %get-tuple-element.32, ...), custom_call_target="tpu_custom_call" | custom-call | bytes 1024 | tf_op jit(solution)/shard_map/early/pallas_call | solution.py:427
  35.3 1.4 %collective-permute-done.3.far_ref = f32[8,120,128]{2,1,0:T(8,128)S(1)} collective-permute-done((f32[8,120,128]{2,1,0:T(8,128)S(1)}, f32[8,120,128]{2,1,0:T(8,128)S(1)}, u32[]{:S(2)}, u32[]{:S(2)}) %collective-permute-start.3) | collective-permute-done | bytes 491552 | tf_op jit(solution)/shard_map/ppermute | solution.py:446
  36.7 4.4 %main.1 = (f32[8,8,128]{2,1,0:T(8,128)}, f32[3,8,8,128]{3,2,1,0:T(8,128)}, f32[8,8,128]{2,1,0:T(8,128)}, f32[3,8,8,128]{3,2,1,0:T(8,128)}, f32[11,528,128]{2,1,0...) custom-call(f32[8,120,128]{2,1,0:T(8,128)S(1)} %collective-permute-d, ...), custom_call_target="tpu_custom_call", output_to_operand_aliasing={{4}: (1, {}), {5}: (2, {}), {6}: (3, {}), {7}: (4, {}), {8}... | custom-call | tf_op jit(solution)/shard_map/main/pallas_call | solution.py:453
  (1 shorter events, 0.0 us)
Async XLA Ops:
  1.7 18.6 %collective-permute-start.1 = (f32[8,48,128]{2,1,0:T(8,128)S(1)}, f32[8,48,128]{2,1,0:T(8,128)S(1)}, u32[]{:S(2)}, u32[]{:S(2)}) collective-permute-start(f32[8,48,128]{2,1,0:T(8,128)S(1)} %get-tuple-element.29), channel_id=1, source_target_pairs={{0,1},{1,2},{2,3},{3,4},{4,5},{5,6},{6,7},{7,8},{8,9},{9,10},{10,1... | collective-permute-start | bytes 589832 | tf_op jit(solution)/shard_map/ppermute | solution.py:471
  7.2 14.0 %collective-permute-start.2 = (f32[8,48,128]{2,1,0:T(8,128)S(1)}, f32[8,48,128]{2,1,0:T(8,128)S(1)}, u32[]{:S(2)}, u32[]{:S(2)}) collective-permute-start(f32[8,48,128]{2,1,0:T(8,128)S(1)} %get-tuple-element.30), channel_id=1, source_target_pairs={{0,15},{1,0},{2,1},{3,2},{4,3},{5,4},{6,5},{7,6},{8,7},{9,8},{10,9... | collective-permute-start | bytes 589832 | tf_op jit(solution)/shard_map/ppermute | solution.py:470
  21.3 15.4 %collective-permute-start.3 = (f32[8,120,128]{2,1,0:T(8,128)S(1)}, f32[8,120,128]{2,1,0:T(8,128)S(1)}, u32[]{:S(2)}, u32[]{:S(2)}) collective-permute-start(f32[8,120,128]{2,1,0:T(8,128)S(1)} %get-tuple-element.31), channel_id=1, source_target_pairs={{0,496},{16,32},{32,16},{48,64},{64,48},{80,96},{96,80},{112,128},... | collective-permute-start | bytes 1474568 | tf_op jit(solution)/shard_map/ppermute | solution.py:446
  25.0 5.3 %collective-permute-start = (f32[8,120,128]{2,1,0:T(8,128)S(1)}, f32[8,120,128]{2,1,0:T(8,128)S(1)}, u32[]{:S(2)}, u32[]{:S(2)}) collective-permute-start(f32[8,120,128]{2,1,0:T(8,128)S(1)} %param.1), channel_id=1, source_target_pairs={{0,16},{16,0},{32,48},{48,32},{64,80},{80,64},{96,112},{112,96},{1... | collective-permute-start | bytes 1474568 | tf_op jit(solution)/shard_map/cond/branch_1_fun/ppermute | solution.py:446
